TPU v7x, 32 devices: a whole 2x2x4 slice. The times are simulated.
32 devices in a mesh: shard: 4 (over z), ctx: 2 (over y), tp: 4 (over x, core).
Axes of the slice: x: 2, y: 2, z: 4, core: 2. Of those that a mesh axis runs over, the one named last changes fastest.
Arguments:
- inputs: float32 [8, 256, 1024], P('shard', 'ctx'), may hold values from -12 to 12
- segment_ids: int32 [8, 256], P('shard', 'ctx'), may hold values from 0 to 3, never falling along the last dimension, each value on 1 to 128 neighbouring positions
- gains: bfloat16 [2, 1024], P(None, ('shard', 'ctx')), may hold values from 0.5 to 1.5
- shifts: bfloat16 [2, 1024], P(None, ('shard', 'ctx')), may hold values from -3 to 3
- attend_weight: bfloat16 [1024, 3, 1024], P(('shard', 'ctx'), None, 'tp'), may hold values from -1 to 1
- merge_weight: bfloat16 [1024, 1024], P(('shard', 'ctx'), 'tp'), may hold values from -0.75 to 0.75
- expand_weight: bfloat16 [1024, 4096], P(('shard', 'ctx'), 'tp'), may hold values from -0.1875 to 0.1875
- expand_bias: bfloat16 [4, 1024], P('tp', ('shard', 'ctx')), may hold values from -3 to 3
- reduce_weight: bfloat16 [1024, 4096], P(('shard', 'ctx'), 'tp'), may hold values from -0.09375 to 0.09375
- cotangent: float32 [8, 256, 1024], P('shard', 'ctx'), may hold values from -6 to 6
Outputs:
- block_out: float32 [8, 256, 1024], P('shard', 'ctx')
- input_grad: float32 [8, 256, 1024], P('shard', 'ctx')
- gains_grad: float32 [2, 1024], P(None, ('shard', 'ctx'))
- shifts_grad: float32 [2, 1024], P(None, ('shard', 'ctx'))
- attend_grad: float32 [1024, 3, 1024], P(('shard', 'ctx'), None, 'tp')
- merge_grad: float32 [1024, 1024], P(('shard', 'ctx'), 'tp')
- expand_grad: float32 [1024, 4096], P(('shard', 'ctx'), 'tp')
- bias_grad: float32 [4, 1024], P('tp', ('shard', 'ctx'))
- reduce_grad: float32 [1024, 4096], P(('shard', 'ctx'), 'tp')
Inputs may be any that keep to these rules, and one draw needn't show every extreme that they name: `segment_ids`: within each sequence segment ids never fall; every document holds 1 to 128 tokens, and one of them exactly 128.
All inputs are finite; a program needn't handle non-finite values.
Results may differ from a plain program's by a relative error of at most 0.0093.
Values may be sent and summed in bfloat16 or wider, within the bound.
No kernel may reach another device: no remote copies, remote signals or barrier semaphores. Data moves between devices by JAX's collectives and lax.ppermute only.
A program may use at most 128 MiB of HBM per device.

v0:
```python
import math

import jax
import jax.numpy as jnp
from jax import lax
from jax.experimental import pallas as pl
from jax.experimental.pallas import tpu as pltpu
from jax.sharding import PartitionSpec as P

HD = 64


epsilon = 1e-05
masked_score = -1e30
gelu_scale = 0.7978845608028654
gelu_cubic = 0.044715


def norm_forward(values, gain, shift):
    average = jnp.mean(values, axis=-1, keepdims=True)
    centered = values - average
    variance = jnp.mean(centered * centered, axis=-1, keepdims=True)
    inverse = lax.rsqrt(variance + epsilon)
    normed = centered * inverse
    return (normed, inverse, normed * gain.astype(jnp.float32) + shift.astype(jnp.float32))


def norm_backward(upstream, normed, inverse, gain):
    scaled = upstream * gain.astype(jnp.float32)
    first_mean = jnp.mean(scaled, axis=-1, keepdims=True)
    second_mean = jnp.mean(scaled * normed, axis=-1, keepdims=True)
    return inverse * (scaled - first_mean - normed * second_mean)


def gelu_pair(pre_act):
    inner_arg = gelu_scale * (pre_act + gelu_cubic * pre_act * pre_act * pre_act)
    tangent = jnp.tanh(inner_arg)
    gelu_value = 0.5 * pre_act * (1.0 + tangent)
    gelu_slope = 0.5 * (1.0 + tangent) + 0.5 * pre_act * (1.0 - tangent * tangent) * gelu_scale * (
        1.0 + 3.0 * gelu_cubic * pre_act * pre_act
    )
    return (gelu_value, gelu_slope)


def shards(
    inputs,
    segment_ids,
    gains,
    shifts,
    attend_weight,
    merge_weight,
    expand_weight,
    expand_bias,
    reduce_weight,
    cotangent,
):
    seq_count, group_len, model_width = inputs.shape
    row_count = seq_count * group_len
    full_len = group_len * lax.axis_size("ctx")
    head_scale = HD ** (-0.5)
    gathered = (
        lax.all_gather(attend_weight, ("shard", "ctx"), axis=0, tiled=True),
        lax.all_gather(merge_weight, ("shard", "ctx"), axis=0, tiled=True),
        lax.all_gather(expand_weight, ("shard", "ctx"), axis=0, tiled=True),
        lax.all_gather(reduce_weight, ("shard", "ctx"), axis=0, tiled=True),
        lax.all_gather(expand_bias, ("shard", "ctx"), axis=1, tiled=True),
        lax.all_gather(gains, ("shard", "ctx"), axis=1, tiled=True),
        lax.all_gather(shifts, ("shard", "ctx"), axis=1, tiled=True),
    )
    attend_full, merge_full, expand_full, reduce_full, bias_full, gains_full, shifts_full = gathered
    local_cols = attend_full.shape[2]
    head_local = local_cols // HD
    flat_in = inputs.reshape(row_count, model_width)
    normed_early, inverse_early, affine_early = norm_forward(flat_in, gains_full[0], shifts_full[0])
    hidden_early = affine_early.astype(jnp.bfloat16)
    projected = jnp.einsum(
        "rd,dtc->rtc", hidden_early, attend_full, preferred_element_type=jnp.float32
    )
    query_heads = (
        (projected[:, 0] * head_scale)
        .astype(jnp.bfloat16)
        .reshape(seq_count, group_len, head_local, HD)
    )
    key_rows = projected[:, 1].astype(jnp.bfloat16).reshape(seq_count, group_len, local_cols)
    value_rows = projected[:, 2].astype(jnp.bfloat16).reshape(seq_count, group_len, local_cols)
    all_keys, all_values, all_segments = (
        lax.all_gather(key_rows, "ctx", axis=1, tiled=True),
        lax.all_gather(value_rows, "ctx", axis=1, tiled=True),
        lax.all_gather(segment_ids, "ctx", axis=1, tiled=True),
    )
    key_heads = all_keys.reshape(seq_count, full_len, head_local, HD)
    value_heads = all_values.reshape(seq_count, full_len, head_local, HD)
    query_pos = lax.axis_index("ctx") * group_len + jnp.arange(group_len, dtype=jnp.int32)
    key_pos = jnp.arange(full_len, dtype=jnp.int32)
    allowed = (segment_ids[:, :, None] == all_segments[:, None, :]) & (
        key_pos[None, None, :] <= query_pos[None, :, None]
    )
    allowed = allowed[:, None]

    def score_block():
        raw_scores = jnp.einsum(
            "sqhd,skhd->shqk", query_heads, key_heads, preferred_element_type=jnp.float32
        )
        return jnp.where(allowed, raw_scores, masked_score)

    scores = score_block()
    row_top = jnp.max(scores, axis=-1, keepdims=True)
    log_total = row_top + jnp.log(jnp.sum(jnp.exp(scores - row_top), axis=-1, keepdims=True))
    attn_probs = jnp.exp(scores - log_total)
    probs_half = attn_probs.astype(jnp.bfloat16)
    attended_heads = jnp.einsum(
        "shqk,skhd->sqhd", probs_half, value_heads, preferred_element_type=jnp.float32
    ).astype(jnp.bfloat16)
    attended = attended_heads.reshape(row_count, local_cols)
    merge_part = jnp.einsum("rc,oc->ro", attended, merge_full, preferred_element_type=jnp.float32)
    residual = flat_in + lax.psum(merge_part, "tp")
    normed_later, inverse_later, affine_later = norm_forward(
        residual, gains_full[1], shifts_full[1]
    )
    hidden_later = affine_later.astype(jnp.bfloat16)
    pre_act = jnp.dot(
        hidden_later, expand_full, preferred_element_type=jnp.float32
    ) + bias_full.astype(jnp.float32)
    gelu_value, gelu_slope = gelu_pair(pre_act)
    activated = gelu_value.astype(jnp.bfloat16)
    reduce_part = jnp.einsum(
        "rf,of->ro", activated, reduce_full, preferred_element_type=jnp.float32
    )
    block_out = residual + lax.psum(reduce_part.astype(jnp.bfloat16), "tp").astype(jnp.float32)
    back_set = (
        lax.all_gather(attend_weight, ("shard", "ctx"), axis=0, tiled=True),
        lax.all_gather(merge_weight, ("shard", "ctx"), axis=0, tiled=True),
        lax.all_gather(expand_weight, ("shard", "ctx"), axis=0, tiled=True),
        lax.all_gather(reduce_weight, ("shard", "ctx"), axis=0, tiled=True),
        lax.all_gather(gains, ("shard", "ctx"), axis=1, tiled=True),
    )
    attend_back, merge_back, expand_back, reduce_back, gains_back = back_set
    output_grad = cotangent.reshape(row_count, model_width)
    cot_half = output_grad.astype(jnp.bfloat16)
    reduce_grad = jnp.einsum("ro,rf->of", cot_half, activated, preferred_element_type=jnp.float32)
    pre_grad = jnp.dot(cot_half, reduce_back, preferred_element_type=jnp.float32) * gelu_slope
    pre_half = pre_grad.astype(jnp.bfloat16)
    bias_grad = jnp.sum(pre_grad, axis=0, keepdims=True)
    expand_grad = jnp.einsum(
        "rd,rf->df", hidden_later, pre_half, preferred_element_type=jnp.float32
    )
    later_part = jnp.einsum("rf,df->rd", pre_half, expand_back, preferred_element_type=jnp.float32)
    later_grad = lax.psum(later_part, "tp")
    residual_grad = output_grad + norm_backward(
        later_grad, normed_later, inverse_later, gains_back[1]
    )
    resid_half = residual_grad.astype(jnp.bfloat16)
    merge_grad = jnp.einsum("ro,rc->oc", resid_half, attended, preferred_element_type=jnp.float32)
    attended_grad = jnp.dot(resid_half, merge_back, preferred_element_type=jnp.float32).astype(
        jnp.bfloat16
    )
    grad_heads = attended_grad.reshape(seq_count, group_len, head_local, HD)
    scores_again = score_block()
    probs_again = jnp.exp(scores_again - log_total)
    probs_again_half = probs_again.astype(jnp.bfloat16)
    row_delta = jnp.einsum(
        "sqhd,sqhd->shq", grad_heads, attended_heads, preferred_element_type=jnp.float32
    )
    prob_grad = jnp.einsum(
        "sqhd,skhd->shqk", grad_heads, value_heads, preferred_element_type=jnp.float32
    )
    score_grad = probs_again * (prob_grad - row_delta[..., None])
    score_half = score_grad.astype(jnp.bfloat16)
    query_grad = (
        jnp.einsum("shqk,skhd->sqhd", score_half, key_heads, preferred_element_type=jnp.float32)
        * head_scale
    )
    keys_part = jnp.einsum(
        "shqk,sqhd->skhd", score_half, query_heads, preferred_element_type=jnp.float32
    ).reshape(seq_count, full_len, local_cols)
    values_part = jnp.einsum(
        "shqk,sqhd->skhd", probs_again_half, grad_heads, preferred_element_type=jnp.float32
    ).reshape(seq_count, full_len, local_cols)
    keys_grad, values_grad = (
        lax.psum_scatter(keys_part, "ctx", scatter_dimension=1, tiled=True),
        lax.psum_scatter(values_part, "ctx", scatter_dimension=1, tiled=True),
    )
    proj_grad = jnp.stack(
        [
            query_grad.reshape(row_count, local_cols),
            keys_grad.reshape(row_count, local_cols),
            values_grad.reshape(row_count, local_cols),
        ],
        axis=1,
    ).astype(jnp.bfloat16)
    attend_grad = jnp.einsum(
        "rd,rtc->dtc", hidden_early, proj_grad, preferred_element_type=jnp.float32
    )
    early_part = jnp.einsum(
        "rtc,dtc->rd", proj_grad, attend_back, preferred_element_type=jnp.float32
    )
    early_grad = lax.psum(early_part, "tp")
    input_grad = residual_grad + norm_backward(
        early_grad, normed_early, inverse_early, gains_back[0]
    )
    gains_grad = jnp.stack(
        [jnp.sum(early_grad * normed_early, axis=0), jnp.sum(later_grad * normed_later, axis=0)]
    )
    shifts_grad = jnp.stack([jnp.sum(early_grad, axis=0), jnp.sum(later_grad, axis=0)])
    shares = (
        lax.psum_scatter(attend_grad, ("shard", "ctx"), scatter_dimension=0, tiled=True),
        lax.psum_scatter(merge_grad, ("shard", "ctx"), scatter_dimension=0, tiled=True),
        lax.psum_scatter(expand_grad, ("shard", "ctx"), scatter_dimension=0, tiled=True),
        lax.psum_scatter(reduce_grad, ("shard", "ctx"), scatter_dimension=0, tiled=True),
        lax.psum_scatter(bias_grad, ("shard", "ctx"), scatter_dimension=1, tiled=True),
        lax.psum_scatter(gains_grad, ("shard", "ctx"), scatter_dimension=1, tiled=True),
        lax.psum_scatter(shifts_grad, ("shard", "ctx"), scatter_dimension=1, tiled=True),
    )
    return (
        block_out.reshape(inputs.shape),
        input_grad.reshape(inputs.shape),
        shares[5],
        shares[6],
        shares[0],
        shares[1],
        shares[2],
        shares[4],
        shares[3],
    )


VMEM = pl.BlockSpec(memory_space=pltpu.VMEM)
SMEM = pl.BlockSpec(memory_space=pltpu.SMEM)
f32 = jnp.float32
bf16 = jnp.bfloat16
RING = 8
ROOM = 6 << 20
NEAR = [(0, 1), (1, 0), (2, 3), (3, 2)]
FAR = [(0, 2), (2, 0), (1, 3), (3, 1)]
AXES = ("shard", "ctx")
TP = "tp"
CTX = "ctx"
IDS = [2 * p if p < 4 else 2 * (7 - p) + 1 for p in range(RING)]
AHEAD = [(IDS[p], IDS[(p + 1) % RING]) for p in range(RING)]
BEHIND = [(IDS[p], IDS[(p - 1) % RING]) for p in range(RING)]


def shape(dims, dtype):
    return jax.ShapeDtypeStruct(dims, dtype)


def call(kernel, outs, args, flops, scratch=(), transcendentals=0):
    nbytes = sum(a.size * a.dtype.itemsize for a in list(args) + list(outs))
    held = sum(math.prod(a.shape) * jnp.dtype(a.dtype).itemsize for a in scratch)
    return pl.pallas_call(
        kernel,
        out_shape=tuple(outs),
        in_specs=[SMEM] + [VMEM] * (len(args) - 1),
        out_specs=tuple(VMEM for _ in outs),
        scratch_shapes=list(scratch),
        compiler_params=pltpu.CompilerParams(vmem_limit_bytes=nbytes + held + ROOM),
        cost_estimate=pl.CostEstimate(
            flops=flops, bytes_accessed=nbytes, transcendentals=transcendentals
        ),
    )(*args)


def columns(meta, offset):
    return pl.ds(pl.multiple_of(meta[offset] * 128, 128), 128)


def rows_of(meta, mine):
    side = meta[8] if mine else 1 - meta[8]
    return pl.ds(pl.multiple_of(side * 128, 128), 128)


def dot(a, b):
    return jnp.dot(a, b, preferred_element_type=f32)


def dot_nt(a, b):
    return lax.dot_general(a, b, (((1,), (1,)), ((), ())), preferred_element_type=f32)


def dot_tn(a, b):
    return lax.dot_general(a, b, (((0,), (0,)), ((), ())), preferred_element_type=f32)


def norm_stats(values):
    average = jnp.mean(values, axis=-1, keepdims=True)
    centered = values - average
    variance = jnp.mean(centered * centered, axis=-1, keepdims=True)
    inverse = lax.rsqrt(variance + epsilon)
    return centered * inverse, inverse


def pack_kernel(meta, attend, merge, gains, shifts, bias, seg, out):
    for t in range(3):
        out[t * 128 : t * 128 + 128, :] = attend[t]
    out[384:512, :] = merge[...]
    zero = jnp.zeros((1, 128), f32)
    low, high, ids = gains[...].astype(f32), shifts[...].astype(f32), seg[...].astype(f32)
    tail = [
        jnp.concatenate([low[0:1], low[1:2]], axis=1),
        jnp.concatenate([high[0:1], high[1:2]], axis=1),
        jnp.concatenate([bias[...].astype(f32), zero], axis=1),
        jnp.concatenate([ids[0:1], ids[1:2]], axis=1),
        jnp.zeros((12, 256), f32),
    ]
    out[512:528, :] = jnp.concatenate(tail, axis=0).astype(bf16)


def norm_half_kernel(meta, x, out):
    normed, _ = norm_stats(x[rows_of(meta, True), :])
    out[...] = normed.astype(bf16)


def qkv_kernel(meta, x, far_a, far_b, *refs):
    blocks = refs[:9]
    (hidden, hidden_far, query, key_value, key_value_far, attend, merge, small, seg_far,
     seg_all) = refs[9:]

    def piece(offset, start, size):
        if offset < 4:
            return blocks[offset][start : start + size, :]
        if offset == 4:
            return jnp.concatenate(
                [blocks[4][start : start + size, :], blocks[5][start : start + size, :]], axis=1
            )
        return blocks[offset + 1][start : start + size, :]

    small[...] = jnp.zeros_like(small)
    for j in range(RING):
        at = columns(meta, j)
        for t in range(3):
            attend[t, at, :] = piece(j, t * 128, 128)
        merge[at, :] = piece(j, 384, 128)
        tail = piece(j, 512, 16).astype(f32)
        small[0:1, at] = tail[0:1, :128]
        small[1:2, at] = tail[0:1, 128:]
        small[2:3, at] = tail[1:2, :128]
        small[3:4, at] = tail[1:2, 128:]
        small[4:5, at] = tail[2:3, :128]
        seg_all[pl.ds(meta[j], 1), :] = tail[3:4, :]
    ids = seg_all[pl.ds(2 * meta[10], 1), :]
    seg_far[0:1, :] = ids[:, :128].astype(jnp.int32)
    seg_far[1:2, :] = ids[:, 128:].astype(jnp.int32)
    gain, shift = small[0:1, :], small[2:3, :]
    normed, _ = norm_stats(x[...])
    hidden[...] = (normed * gain + shift).astype(bf16)
    hidden_far[rows_of(meta, True), :] = (far_a[...].astype(f32) * gain + shift).astype(bf16)
    hidden_far[rows_of(meta, False), :] = (far_b[...].astype(f32) * gain + shift).astype(bf16)
    both, other = hidden[...], hidden_far[...]
    key_value[:, :256] = dot(both, attend[1]).astype(bf16)
    key_value[:, 256:] = dot(both, attend[2]).astype(bf16)
    key_value_far[:, :256] = dot(other, attend[1]).astype(bf16)
    key_value_far[:, 256:] = dot(other, attend[2]).astype(bf16)
    query[...] = (dot(both, attend[0]) * (HD**-0.5)).astype(bf16)


def masks(meta, seg, seg_col, seg_far, s):
    col = seg_col[:, s : s + 1]
    near = col == seg[s : s + 1, :]
    i = lax.broadcasted_iota(jnp.int32, (128, 128), 0)
    j = lax.broadcasted_iota(jnp.int32, (128, 128), 1)
    far = (col == seg_far[s : s + 1, :]) & (meta[9] == 1)
    return near & (j <= i), far


def head_probs(query, key, key_far, near, far):
    score = jnp.where(near, dot_nt(query, key), masked_score)
    score_far = jnp.where(far, dot_nt(query, key_far), masked_score)
    top = jnp.maximum(
        jnp.max(score, axis=-1, keepdims=True), jnp.max(score_far, axis=-1, keepdims=True)
    )
    total = jnp.sum(jnp.exp(score - top), axis=-1, keepdims=True) + jnp.sum(
        jnp.exp(score_far - top), axis=-1, keepdims=True
    )
    log_total = top + jnp.log(total)
    return jnp.exp(score - log_total), jnp.exp(score_far - log_total)


def attention_kernel(
    meta, query, kv, kv_far, seg, seg_col, seg_far, merge, attended, keep, give, part
):
    for s in range(2):
        near, far = masks(meta, seg, seg_col, seg_far, s)
        r = slice(s * 128, s * 128 + 128)
        for h in range(4):
            c = slice(h * 64, h * 64 + 64)
            v = slice(256 + h * 64, 256 + h * 64 + 64)
            probs, probs_far = head_probs(query[r, c], kv[r, c], kv_far[r, c], near, far)
            out = dot(probs.astype(bf16), kv[r, v]) + dot(probs_far.astype(bf16), kv_far[r, v])
            attended[r, c] = out.astype(bf16)
    part[...] = dot_nt(attended[...], merge[...])
    keep[...] = part[rows_of(meta, True), :]
    give[...] = part[rows_of(meta, False), :].astype(bf16)


def total_of(meta, sums, full):
    pair, far, pair_other, far_other = sums
    full[rows_of(meta, True), :] = pair[...].astype(f32) + far[...].astype(f32)
    full[rows_of(meta, False), :] = pair_other[...].astype(f32) + far_other[...].astype(f32)
    return full[...]


def assemble(meta, blocks, full):
    for j in range(RING):
        at = columns(meta, j)
        if j == 4:
            start = pl.multiple_of(meta[4] * 128, 128)
            full[pl.ds(start, 64), :] = blocks[4][...]
            full[pl.ds(pl.multiple_of(start + 64, 64), 64), :] = blocks[5][...]
        else:
            full[at, :] = (blocks[j] if j < 4 else blocks[j + 1])[...]


def store_parts(meta, left, right, outs):
    for j in range(RING):
        value = dot_tn(left[:, columns(meta, j)], right[...]).astype(bf16)
        if j == 4:
            outs[4][...] = value[:64]
            outs[5][...] = value[64:]
        else:
            (outs[j] if j < 4 else outs[j + 1])[...] = value


def ffn_first_kernel(meta, x, cot, small, s0, s1, s2, s3, *refs):
    blocks = refs[:9]
    residual, hidden, cot_half, act, slope, expand = refs[9:15]
    outs, part = refs[15:24], refs[24]
    assemble(meta, blocks, expand)
    residual[...] = x[...] + total_of(meta, (s0, s1, s2, s3), part)
    normed, _ = norm_stats(residual[...])
    hidden[...] = (normed * small[1:2, :] + small[3:4, :]).astype(bf16)
    cot_half[...] = cot[...].astype(bf16)

    def units(i, carry):
        at = pl.ds(pl.multiple_of(i * 256, 256), 256)
        pre_act = dot(hidden[...], expand[:, at]) + small[4:5, at]
        value, gradient = gelu_pair(pre_act)
        act[:, at] = value.astype(bf16)
        slope[:, at] = gradient
        return carry

    lax.fori_loop(0, 4, units, 0)
    store_parts(meta, cot_half, act, outs)


def ffn_second_kernel(meta, residual, cot_half, act, slope, expand, *refs):
    blocks = refs[:9]
    pre_half, later_keep, later_give, red_keep, red_give, grads, reduce, part = refs[9:]
    assemble(meta, blocks, reduce)
    grads[...] = jnp.zeros_like(grads)

    def units(i, carry):
        at = pl.ds(pl.multiple_of(i * 256, 256), 256)
        pre_grad = dot(cot_half[...], reduce[:, at]) * slope[:, at]
        pre_half[:, at] = pre_grad.astype(bf16)
        grads[2:3, at] = jnp.sum(pre_grad, axis=0, keepdims=True)
        return carry

    lax.fori_loop(0, 4, units, 0)

    def later(i, carry):
        at = pl.ds(pl.multiple_of(i * 256, 256), 256)
        part[:, at] = dot_nt(pre_half[...], expand[at, :])
        return carry

    lax.fori_loop(0, 4, later, 0)
    later_keep[...] = part[rows_of(meta, True), :]
    later_give[...] = part[rows_of(meta, False), :].astype(bf16)
    normed, _ = norm_stats(residual[...])
    grads[0:1, :] = jnp.sum(part[...] * normed, axis=0, keepdims=True)
    grads[1:2, :] = jnp.sum(part[...], axis=0, keepdims=True)

    def reduced(i, carry):
        at = pl.ds(pl.multiple_of(i * 256, 256), 256)
        part[:, at] = dot_nt(act[...], reduce[at, :])
        return carry

    lax.fori_loop(0, 4, reduced, 0)
    red_keep[...] = part[rows_of(meta, True), :]
    red_give[...] = part[rows_of(meta, False), :].astype(bf16)


def expand_grads_kernel(meta, hidden, pre_half, *outs):
    store_parts(meta, hidden, pre_half, outs)


def attention_back_kernel(
    meta, cot, residual, small, s0, s1, s2, s3, merge, query, kv, kv_far, attended,
    seg, seg_col, seg_far, residual_grad, resid_half, query_grad, kv_grad, kv_grad_far,
    part, att_grad
):
    later_grad = total_of(meta, (s0, s1, s2, s3), part)
    normed, inverse = norm_stats(residual[...])
    residual_grad[...] = cot[...] + norm_backward(later_grad, normed, inverse, small[1:2, :])
    resid_half[...] = residual_grad[...].astype(bf16)
    att_grad[...] = dot(resid_half[...], merge[...]).astype(bf16)
    for s in range(2):
        near, far = masks(meta, seg, seg_col, seg_far, s)
        r = slice(s * 128, s * 128 + 128)
        for h in range(4):
            c = slice(h * 64, h * 64 + 64)
            v = slice(256 + h * 64, 256 + h * 64 + 64)
            q, k, k_far = query[r, c], kv[r, c], kv_far[r, c]
            probs, probs_far = head_probs(q, k, k_far, near, far)
            up = att_grad[r, c]
            delta = jnp.sum(up.astype(f32) * attended[r, c].astype(f32), axis=-1, keepdims=True)
            score = (probs * (dot_nt(up, kv[r, v]) - delta)).astype(bf16)
            score_far = (probs_far * (dot_nt(up, kv_far[r, v]) - delta)).astype(bf16)
            query_grad[r, c] = (dot(score, k) + dot(score_far, k_far)) * (HD**-0.5)
            kv_grad[r, c] = dot_tn(score, q)
            kv_grad[r, v] = dot_tn(probs.astype(bf16), up)
            kv_grad_far[r, c] = dot_tn(score_far, q).astype(bf16)
            kv_grad_far[r, v] = dot_tn(probs_far.astype(bf16), up).astype(bf16)


def attention_grads_kernel(
    meta, x, far_a, far_b, hidden, hidden_far, query_grad, kv_grad, kv_grad_far, resid_half,
    attended, attend, grads, early, *refs
):
    outs, proj, sums, part = refs[:9], refs[9], refs[10], refs[11]
    proj[:, :256] = query_grad[...].astype(bf16)
    proj[:, 256:] = kv_grad[...].astype(bf16)
    early[...] = (
        dot_nt(proj[:, :256], attend[0])
        + dot_nt(proj[:, 256:512], attend[1])
        + dot_nt(proj[:, 512:], attend[2])
    )
    part[...] = dot_nt(kv_grad_far[:, :256], attend[1]) + dot_nt(kv_grad_far[:, 256:], attend[2])
    normed, _ = norm_stats(x[...])
    mine, other = part[rows_of(meta, True), :], part[rows_of(meta, False), :]
    sums[0:1, :] = (
        jnp.sum(early[...] * normed, axis=0, keepdims=True)
        + jnp.sum(mine * far_a[...].astype(f32), axis=0, keepdims=True)
        + jnp.sum(other * far_b[...].astype(f32), axis=0, keepdims=True)
    )
    sums[1:2, :] = jnp.sum(early[...] + part[...], axis=0, keepdims=True)
    for j in range(RING):
        at = columns(meta, j)
        lhs, lhs_far = hidden[:, at], hidden_far[:, at]
        pieces = [dot_tn(lhs, proj[:, :256]).astype(bf16)]
        for t in (1, 2):
            c, c_far = slice(t * 256, t * 256 + 256), slice(t * 256 - 256, t * 256)
            pieces.append((dot_tn(lhs, proj[:, c]) + dot_tn(lhs_far, kv_grad_far[:, c_far])).astype(bf16))
        pieces.append(dot_tn(resid_half[:, at], attended[...]).astype(bf16))
        zero = jnp.zeros((1, 128), f32)
        tail = jnp.concatenate(
            [
                jnp.concatenate([sums[0:1, at], grads[0:1, at]], axis=1),
                jnp.concatenate([sums[1:2, at], grads[1:2, at]], axis=1),
                jnp.concatenate([grads[2:3, at], zero], axis=1),
                jnp.zeros((13, 256), f32),
            ],
            axis=0,
        )
        pieces.append(tail.astype(bf16))
        start = 0
        for value in pieces:
            span = slice(start, start + value.shape[0])
            start += value.shape[0]
            if j == 4:
                outs[4][span, :] = value[:, :128]
                outs[5][span, :] = value[:, 128:]
            else:
                out = outs[j] if j < 4 else outs[j + 1]
                out[span, :] = value


def project_back_kernel(meta, early, kv_grad_in, attend, keep, give, part):
    part[...] = (
        early[...]
        + dot_nt(kv_grad_in[:, :256], attend[1])
        + dot_nt(kv_grad_in[:, 256:], attend[2])
    )
    keep[...] = part[rows_of(meta, True), :]
    give[...] = part[rows_of(meta, False), :].astype(bf16)


def first_rows_kernel(meta, up, down, ahead, behind, up_out, down_out):
    up_out[:64, :] = (up[:64, :].astype(f32) + ahead[...].astype(f32)).astype(bf16)
    up_out[64:, :] = up[64:, :]
    down_out[:64, :] = down[:64, :]
    down_out[64:, :] = (down[64:, :].astype(f32) + behind[...].astype(f32)).astype(bf16)


def first_columns_kernel(meta, up, down, ahead, behind, up_out, down_out):
    up_out[:, :128] = (up[:, :128].astype(f32) + ahead[...].astype(f32)).astype(bf16)
    up_out[:, 128:] = up[:, 128:]
    down_out[:, :128] = down[:, :128]
    down_out[:, 128:] = (down[:, 128:].astype(f32) + behind[...].astype(f32)).astype(bf16)


def step_kernel(meta, up, down, ahead, behind, up_out, down_out):
    up_out[...] = (up[...].astype(f32) + ahead[...].astype(f32)).astype(bf16)
    down_out[...] = (down[...].astype(f32) + behind[...].astype(f32)).astype(bf16)


def last_kernel(meta, own, ahead, behind, out):
    out[...] = own[...].astype(f32) + (ahead[...].astype(f32) + behind[...].astype(f32))


def last_pack_kernel(meta, own, ahead, behind, attend, merge, tail):
    def total(start, size):
        r = slice(start, start + size)
        return own[r, :].astype(f32) + (ahead[r, :].astype(f32) + behind[r, :].astype(f32))

    for t in range(3):
        attend[t] = total(t * 128, 128)
    merge[...] = total(384, 128)
    tail[...] = total(512, 16)


def block_out_kernel(meta, residual, s0, s1, s2, s3, out, part):
    out[...] = residual[...] + total_of(meta, (s0, s1, s2, s3), part)


def input_grad_kernel(meta, x, residual_grad, small, s0, s1, s2, s3, out, part):
    early_grad = total_of(meta, (s0, s1, s2, s3), part)
    normed, inverse = norm_stats(x[...])
    out[...] = residual_grad[...] + norm_backward(early_grad, normed, inverse, small[0:1, :])


def send_ahead(value):
    return lax.ppermute(value, AXES, AHEAD)


def send_behind(value):
    return lax.ppermute(value, AXES, BEHIND)


def gather_blocks(own, first, second):
    blocks = [own] + [None] * 8
    ahead, behind = own, own
    for step in range(1, 4):
        ahead = send_ahead(ahead)
        behind = send_behind(behind)
        blocks[9 - step], blocks[step] = ahead, behind
    blocks[4] = send_ahead(first(ahead))
    blocks[5] = send_behind(second(behind))
    return blocks


def sum_blocks(meta, parts, first, last, last_shapes):
    ahead = send_ahead(parts[4])
    behind = send_behind(parts[5])
    for step in range(3, 0, -1):
        up, down = call(
            first if step == 3 else step_kernel, [shape(parts[1].shape, bf16)] * 2,
            [meta, parts[step], parts[9 - step], ahead, behind], 1_000_000,
        )
        ahead = send_ahead(up)
        behind = send_behind(down)
    return call(last, last_shapes, [meta, parts[0], ahead, behind], 1_000_000)


def tp_send(pairs):
    return lambda value: lax.ppermute(value, TP, pairs)


def tp_exchange(keep, give):
    near = tp_send(NEAR)(give)
    pair = (keep + near.astype(f32)).astype(bf16)
    far = tp_send(FAR)(pair)
    pair_other = tp_send(NEAR)(pair)
    return pair, far, pair_other, tp_send(NEAR)(far)


def fast_shards(
    inputs, segment_ids, gains, shifts, attend_weight, merge_weight, expand_weight,
    expand_bias, reduce_weight, cotangent,
):
    shard, ctx = lax.axis_index(AXES[0]), lax.axis_index(CTX)
    place = jnp.where(ctx == 0, shard, RING - 1 - shard)
    spots = lax.rem(place + jnp.arange(RING, dtype=jnp.int32), RING)
    owners = jnp.where(spots < 4, 2 * spots, 2 * (7 - spots) + 1)
    side = lax.rem(lax.axis_index(TP), 2)
    meta = jnp.concatenate([owners, jnp.stack([side, ctx, shard])]).astype(jnp.int32)

    x = inputs.reshape(256, 1024)
    cot = cotangent.reshape(256, 1024)
    rows, half, square = (256, 1024), (128, 1024), (256, 256)
    part = pltpu.VMEM(rows, f32)
    (pack,) = call(
        pack_kernel, [shape((528, 256), bf16)],
        [meta, jnp.swapaxes(attend_weight, 0, 1), merge_weight, gains, shifts, expand_bias,
         segment_ids], 1_000_000,
    )
    blocks = gather_blocks(pack, lambda v: v[:, :128], lambda v: v[:, 128:])
    (normed_half,) = call(norm_half_kernel, [shape(half, bf16)], [meta, x], 1_000_000)
    far_a = lax.ppermute(normed_half, CTX, [(0, 1)])
    far_b = lax.ppermute(far_a, TP, NEAR)
    seg_col = segment_ids.T
    expand_weight, _ = lax.optimization_barrier((expand_weight, blocks[EXPAND_AFTER]))
    expand_blocks = gather_blocks(expand_weight, lambda v: v[:64], lambda v: v[64:])
    reduce_weight, _ = lax.optimization_barrier((reduce_weight, blocks[REDUCE_AFTER]))
    reduce_blocks = gather_blocks(reduce_weight, lambda v: v[:64], lambda v: v[64:])

    hidden_early, hidden_far, query, kv, kv_far, attend, merge, small, seg_far = call(
        qkv_kernel,
        [shape(rows, bf16), shape(rows, bf16), shape(square, bf16), shape((256, 512), bf16),
         shape((256, 512), bf16), shape((3, 1024, 256), bf16), shape((1024, 256), bf16),
         shape((8, 1024), f32), shape((2, 128), jnp.int32)],
        [meta, x, far_a, far_b] + blocks, 700_000_000, [pltpu.VMEM((8, 256), f32)],
    )
    attended, keep, give = call(
        attention_kernel,
        [shape(square, bf16), shape(half, f32), shape(half, bf16)],
        [meta, query, kv, kv_far, segment_ids, seg_col, seg_far, merge],
        300_000_000, [part], 800_000,
    )
    part_shapes = [shape(half, bf16)] * 9
    part_shapes[4] = part_shapes[5] = shape((64, 1024), bf16)
    residual, hidden_later, cot_half, act, slope, expand, *reduce_parts = call(
        ffn_first_kernel,
        [shape(rows, f32)] + [shape(rows, bf16)] * 3 + [shape(rows, f32)]
        + [shape((1024, 1024), bf16)] + part_shapes,
        [meta, x, cot, small, *tp_exchange(keep, give)] + expand_blocks,
        1_100_000_000, [part], 300_000,
    )
    pre_half, later_keep, later_give, red_keep, red_give, grads = call(
        ffn_second_kernel,
        [shape(rows, bf16)] + [shape(half, f32), shape(half, bf16)] * 2 + [shape((8, 1024), f32)],
        [meta, residual, cot_half, act, slope, expand] + reduce_blocks,
        1_600_000_000, [pltpu.VMEM((1024, 1024), bf16), part],
    )
    (reduce_grad,) = sum_blocks(
        meta, reduce_parts, first_rows_kernel, last_kernel, [shape(half, f32)]
    )
    later_sums = tp_exchange(later_keep, later_give)
    expand_parts = call(
        expand_grads_kernel, part_shapes,
        [meta, hidden_later, pre_half], 550_000_000,
    )
    (expand_grad,) = sum_blocks(
        meta, expand_parts, first_rows_kernel, last_kernel, [shape(half, f32)]
    )
    residual_grad, resid_half, query_grad, kv_grad, kv_grad_far = call(
        attention_back_kernel,
        [shape(rows, f32), shape(rows, bf16), shape(square, f32), shape((256, 512), f32),
         shape((256, 512), bf16)],
        [meta, cot, residual, small, *later_sums, merge, query, kv, kv_far, attended,
         segment_ids, seg_col, seg_far],
        500_000_000, [part, pltpu.VMEM(square, bf16)], 800_000,
    )
    kv_grad_in = lax.ppermute(kv_grad_far, CTX, [(1, 0)])
    pack_shapes = [shape((528, 256), bf16)] * 9
    pack_shapes[4] = pack_shapes[5] = shape((528, 128), bf16)
    early, *pack_parts = call(
        attention_grads_kernel, [shape(rows, f32)] + pack_shapes,
        [meta, x, far_a, far_b, hidden_early, hidden_far, query_grad, kv_grad, kv_grad_far,
         resid_half, attended, attend, grads], 1_100_000_000,
        [pltpu.VMEM((256, 768), bf16), pltpu.VMEM((8, 1024), f32), part],
    )
    attend_grad, merge_grad, tail = sum_blocks(
        meta, pack_parts, first_columns_kernel, last_pack_kernel,
        [shape((3, 128, 256), f32), shape((128, 256), f32), shape((16, 256), f32)],
    )
    early_keep, early_give = call(
        project_back_kernel, [shape(half, f32), shape(half, bf16)],
        [meta, early, kv_grad_in, attend], 300_000_000, [part],
    )
    early_sums = tp_exchange(early_keep, early_give)
    red_keep, red_give, _ = lax.optimization_barrier((red_keep, red_give, query_grad))
    (block_out,) = call(
        block_out_kernel, [shape(rows, f32)],
        [meta, residual, *tp_exchange(red_keep, red_give)], 1_000_000, [part],
    )
    (input_grad,) = call(
        input_grad_kernel, [shape(rows, f32)],
        [meta, x, residual_grad, small, *early_sums], 5_000_000, [part],
    )
    norms = tail[:2]
    norms = norms + lax.ppermute(norms, TP, NEAR)
    norms = norms + lax.ppermute(norms, TP, FAR)
    return (
        block_out.reshape(inputs.shape),
        input_grad.reshape(inputs.shape),
        norms[0].reshape(2, 128),
        norms[1].reshape(2, 128),
        jnp.swapaxes(attend_grad, 0, 1),
        merge_grad,
        expand_grad,
        tail[2:3, :128],
        reduce_grad,
    )


EXPAND_AFTER = 0
REDUCE_AFTER = 2


def fits(mesh_sizes, *args):
    shapes = tuple(a.shape for a in args)
    return mesh_sizes == (4, 2, 4) and shapes == (
        (2, 128, 1024), (2, 128), (2, 128), (2, 128), (128, 3, 256), (128, 256),
        (128, 1024), (1, 128), (128, 1024), (2, 128, 1024),
    )


def either(*args):
    sizes = tuple(lax.axis_size(name) for name in (*AXES, TP))
    if not fits(sizes, *args):
        return shards(*args)
    return fast_shards(*args)


def solution(mesh):
    in_specs = (
        P("shard", "ctx", None),
        P("shard", "ctx"),
        P(None, ("shard", "ctx")),
        P(None, ("shard", "ctx")),
        P(("shard", "ctx"), None, "tp"),
        P(("shard", "ctx"), "tp"),
        P(("shard", "ctx"), "tp"),
        P("tp", ("shard", "ctx")),
        P(("shard", "ctx"), "tp"),
        P("shard", "ctx", None),
    )
    out_specs = (
        P("shard", "ctx", None),
        P("shard", "ctx", None),
        P(None, ("shard", "ctx")),
        P(None, ("shard", "ctx")),
        P(("shard", "ctx"), None, "tp"),
        P(("shard", "ctx"), "tp"),
        P(("shard", "ctx"), "tp"),
        P("tp", ("shard", "ctx")),
        P(("shard", "ctx"), "tp"),
    )
    return jax.shard_map(either, mesh=mesh, in_specs=in_specs, out_specs=out_specs, check_vma=False)
```

profile of v0, /device:TPU:0, one launch (start us, length us, event | category | flops | bytes accessed | tf_op | source)
XLA Modules:
  0.0 190.7 jit_solution(5718865304780642535)
XLA Ops:
  5.7 3.0 %collective-permute-start.2 = (bf16[528,256]{1,0:T(8,128)(2,1)S(1)}, bf16[528,256]{1,0:T(8,128)(2,1)S(1)}, u32[]{:S(2)}, u32[]{:S(2)}) collective-permute-start(bf16[528,256]{1,0:T(8,128)(2,1)S(1)} %shard_map.170.refs_0_), channel_id=1, source_target_pairs={{0,4},{8,0},{16,8},{24,16},{28,24},{20,28},{12,20},{4,12},{1,5},{9... | collective-permute-start | bytes 811016 | tf_op jit(solution)/shard_map/ppermute | solution.py:626
  8.9 6.4 %collective-permute-done.2.refs_1_ = bf16[528,256]{1,0:T(8,128)(2,1)S(1)} collective-permute-done((bf16[528,256]{1,0:T(8,128)(2,1)S(1)}, bf16[528,256]{1,0:T(8,128)(2,1)S(1)}, u32[]{:S(2)}, u32[]{:S(2)}) %collective-permute-start.2) | collective-permute-done | bytes 270368 | tf_op jit(solution)/shard_map/ppermute | solution.py:626
  15.3 1.7 collective-permute-start.3
  19.4 3.6 %collective-permute-start = (bf16[128,1024]{1,0:T(8,128)(2,1)S(1)}, bf16[128,1024]{1,0:T(8,128)(2,1)S(1)}, u32[]{:S(2)}, u32[]{:S(2)}) collective-permute-start(bf16[128,1024]{1,0:T(8,128)(2,1)S(1)} %shard_map.169), channel_id=1, source_target_pairs={{0,4},{1,5},{2,6},{3,7},{8,12},{9,13},{10,14},{11,15},{16,20},{17,... | collective-permute-start | bytes 786440 | tf_op jit(solution)/shard_map/ppermute | solution.py:688
  23.0 1.8 collective-permute-start.4
  25.1 1.6 collective-permute-start.17
  26.7 3.0 %collective-permute-done.far_a = bf16[128,1024]{1,0:T(8,128)(2,1)S(1)} collective-permute-done((bf16[128,1024]{1,0:T(8,128)(2,1)S(1)}, bf16[128,1024]{1,0:T(8,128)(2,1)S(1)}, u32[]{:S(2)}, u32[]{:S(2)}) %collective-permute-start) | collective-permute-done | bytes 262176 | tf_op jit(solution)/shard_map/ppermute | solution.py:688
  29.7 3.7 %collective-permute-done.4.refs_3_ = bf16[528,256]{1,0:T(8,128)(2,1)S(1)} collective-permute-done((bf16[528,256]{1,0:T(8,128)(2,1)S(1)}, bf16[528,256]{1,0:T(8,128)(2,1)S(1)}, u32[]{:S(2)}, u32[]{:S(2)}) %collective-permute-start.4) | collective-permute-done | bytes 270368 | tf_op jit(solution)/shard_map/ppermute | solution.py:626
  34.0 2.5 %collective-permute-start.9 = (bf16[528,128]{1,0:T(8,128)(2,1)}, bf16[528,128]{1,0:T(8,128)(2,1)}, u32[]{:S(2)}, u32[]{:S(2)}) collective-permute-start(bf16[528,128]{1,0:T(8,128)(2,1)} %slice.41), channel_id=1, source_target_pairs={{0,4},{8,0},{16,8},{24,16},{28,24},{20,28},{12,20},{4,12},{1,5},{9... | collective-permute-start | bytes 405512 | tf_op jit(solution)/shard_map/ppermute | solution.py:626
  37.1 2.0 %collective-permute-start.14 = (bf16[128,1024]{1,0:T(8,128)(2,1)}, bf16[128,1024]{1,0:T(8,128)(2,1)}, u32[]{:S(2)}, u32[]{:S(2)}) collective-permute-start(bf16[128,1024]{1,0:T(8,128)(2,1)} %refs_0_), channel_id=1, source_target_pairs={{0,4},{8,0},{16,8},{24,16},{28,24},{20,28},{12,20},{4,12},{1,5},{9... | collective-permute-start | bytes 786440 | tf_op jit(solution)/shard_map/ppermute | solution.py:626
  39.4 1.7 collective-permute-start.25
  41.0 2.2 %collective-permute-start.22 = (bf16[128,1024]{1,0:T(8,128)(2,1)}, bf16[128,1024]{1,0:T(8,128)(2,1)S(1)}, u32[]{:S(2)}, u32[]{:S(2)}) collective-permute-start(bf16[128,1024]{1,0:T(8,128)(2,1)} %refs_0_.1), channel_id=1, source_target_pairs={{0,4},{8,0},{16,8},{24,16},{28,24},{20,28},{12,20},{4,12},{1,5},{9... | collective-permute-start | bytes 786440 | tf_op jit(solution)/shard_map/ppermute | solution.py:626
  43.9 2.5 %shard_map.171 = (bf16[256,1024]{1,0:T(8,128)(2,1)S(1)}, bf16[256,1024]{1,0:T(8,128)(2,1)S(1)}, bf16[256,256]{1,0:T(8,128)(2,1)S(1)}, bf16[256,512]{1,0:T(8,128)...) custom-call(s32[11]{0:T(128)S(1)} %pad_add_fusion.meta, ...), custom_call_target="tpu_custom_call" | custom-call | flops 700000000 | bytes 7570476 | tf_op jit(solution)/shard_map/pallas_call | solution.py:250
  46.4 4.1 %shard_map.172 = (bf16[256,256]{1,0:T(8,128)(2,1)S(1)}, f32[128,1024]{1,0:T(8,128)S(1)}, bf16[128,1024]{1,0:T(8,128)(2,1)S(1)}) custom-call(s32[11]{0:T(128)S(1)} %pad_add_fusion.meta, bf16[256,256]{1,0:T(8,128)(2,1)S(1)} %get-tuple-element.94.query, bf16[256,512]{1,0:T(8,128)(2,1)S(1)} %get-tuple-element.95.kv, ...), custom_call_target="tpu_custom_call" | custom-call | flops 300000000 | bytes 2100268 | tf_op jit(solution)/shard_map/pallas_call | solution.py:250
  50.7 2.0 %collective-permute-start.19 = (bf16[128,1024]{1,0:T(8,128)(2,1)S(1)}, bf16[128,1024]{1,0:T(8,128)(2,1)S(1)}, u32[]{:S(2)}, u32[]{:S(2)}) collective-permute-start(bf16[128,1024]{1,0:T(8,128)(2,1)S(1)} %collective-permute-done.18.refs_7_), channel_id=1, source_target_pairs={{0,8},{8,16},{16,24},{24,28},{28,20},{20,12},{12,4},{4,0},{1,9},{9... | collective-permute-start | bytes 786440 | tf_op jit(solution)/shard_map/ppermute | solution.py:622
  52.7 2.4 %collective-permute-start.26 = (bf16[128,1024]{1,0:T(8,128)(2,1)S(1)}, bf16[128,1024]{1,0:T(8,128)(2,1)S(1)}, u32[]{:S(2)}, u32[]{:S(2)}) collective-permute-start(bf16[128,1024]{1,0:T(8,128)(2,1)S(1)} %collective-permute-done.25.refs_8_), channel_id=1, source_target_pairs={{0,8},{8,16},{16,24},{24,28},{28,20},{20,12},{12,4},{4,0},{1,9},{9... | collective-permute-start | bytes 786440 | tf_op jit(solution)/shard_map/ppermute | solution.py:622
  55.2 1.6 collective-permute-start.11
  56.7 3.3 %collective-permute-done.15.refs_2_ = bf16[128,1024]{1,0:T(8,128)(2,1)S(1)} collective-permute-done((bf16[128,1024]{1,0:T(8,128)(2,1)}, bf16[128,1024]{1,0:T(8,128)(2,1)S(1)}, u32[]{:S(2)}, u32[]{:S(2)}) %collective-permute-start.15) | collective-permute-done | bytes 262176 | tf_op jit(solution)/shard_map/ppermute | solution.py:626
  60.0 4.9 %collective-permute-done.26.refs_7_ = bf16[128,1024]{1,0:T(8,128)(2,1)S(1)} collective-permute-done((bf16[128,1024]{1,0:T(8,128)(2,1)S(1)}, bf16[128,1024]{1,0:T(8,128)(2,1)S(1)}, u32[]{:S(2)}, u32[]{:S(2)}) %collective-permute-start.26) | collective-permute-done | bytes 262176 | tf_op jit(solution)/shard_map/ppermute | solution.py:622
  65.0 1.9 collective-permute-start.27
  67.9 3.4 %collective-permute-done.16.refs_3_ = bf16[128,1024]{1,0:T(8,128)(2,1)S(1)} collective-permute-done((bf16[128,1024]{1,0:T(8,128)(2,1)S(1)}, bf16[128,1024]{1,0:T(8,128)(2,1)S(1)}, u32[]{:S(2)}, u32[]{:S(2)}) %collective-permute-start.16) | collective-permute-done | bytes 262176 | tf_op jit(solution)/shard_map/ppermute | solution.py:626
  71.3 2.4 %collective-permute-start.20 = (bf16[64,1024]{1,0:T(8,128)(2,1)S(1)}, bf16[64,1024]{1,0:T(8,128)(2,1)S(1)}, u32[]{:S(2)}, u32[]{:S(2)}) collective-permute-start(bf16[64,1024]{1,0:T(8,128)(2,1)S(1)} %slice.42), channel_id=1, source_target_pairs={{0,8},{8,16},{16,24},{24,28},{28,20},{20,12},{12,4},{4,0},{1,9},{9... | collective-permute-start | bytes 393224 | tf_op jit(solution)/shard_map/ppermute | solution.py:622
  73.7 3.6 %collective-permute-start.21 = (bf16[64,1024]{1,0:T(8,128)(2,1)S(1)}, bf16[64,1024]{1,0:T(8,128)(2,1)S(1)}, u32[]{:S(2)}, u32[]{:S(2)}) collective-permute-start(bf16[64,1024]{1,0:T(8,128)(2,1)S(1)} %slice.43), channel_id=1, source_target_pairs={{0,4},{8,0},{16,8},{24,16},{28,24},{20,28},{12,20},{4,12},{1,5},{9... | collective-permute-start | bytes 393224 | tf_op jit(solution)/shard_map/ppermute | solution.py:626
  77.3 1.9 %collective-permute-start.28 = (bf16[64,1024]{1,0:T(8,128)(2,1)S(1)}, bf16[64,1024]{1,0:T(8,128)(2,1)S(1)}, u32[]{:S(2)}, u32[]{:S(2)}) collective-permute-start(bf16[64,1024]{1,0:T(8,128)(2,1)S(1)} %slice.44), channel_id=1, source_target_pairs={{0,8},{8,16},{16,24},{24,28},{28,20},{20,12},{12,4},{4,0},{1,9},{9... | collective-permute-start | bytes 393224 | tf_op jit(solution)/shard_map/ppermute | solution.py:622
  80.5 4.4 %shard_map.173 = (f32[256,1024]{1,0:T(8,128)S(1)}, bf16[256,1024]{1,0:T(8,128)(2,1)S(1)}, bf16[256,1024]{1,0:T(8,128)(2,1)S(1)}, bf16[256,1024]{1,0:T(8,128)(2,1...) custom-call(s32[11]{0:T(128)S(1)} %pad_add_fusion.meta, ...), custom_call_target="tpu_custom_call" | custom-call | flops 1100000000 | bytes 13140012 | tf_op jit(solution)/shard_map/pallas_call | solution.py:250
  85.0 5.2 %shard_map.174 = (bf16[256,1024]{1,0:T(8,128)(2,1)S(1)}, f32[128,1024]{1,0:T(8,128)S(1)}, bf16[128,1024]{1,0:T(8,128)(2,1)S(1)}, f32[128,1024]{1,0:T(8,128)S(1)}...) custom-call(s32[11]{0:T(128)S(1)} %pad_add_fusion.meta, f32[256,1024]{1,0:T(8,128)S(1)} %get-tuple-element.102.residual, ...), custom_call_target="tpu_custom_call" | custom-call | flops 1600000000 | bytes 9469996 | tf_op jit(solution)/shard_map/pallas_call | solution.py:250
  93.4 6.9 %collective-permute-done.31.s1 = bf16[128,1024]{1,0:T(8,128)(2,1)S(1)} collective-permute-done((bf16[128,1024]{1,0:T(8,128)(2,1)S(1)}, bf16[128,1024]{1,0:T(8,128)(2,1)S(1)}, u32[]{:S(2)}, u32[]{:S(2)}) %collective-permute-start.31) | collective-permute-done | bytes 262176 | tf_op jit(solution)/shard_map/ppermute | solution.py:655
  102.7 4.2 %collective-permute-done.61.ahead = bf16[64,1024]{1,0:T(8,128)(2,1)S(1)} collective-permute-done((bf16[64,1024]{1,0:T(8,128)(2,1)S(1)}, bf16[64,1024]{1,0:T(8,128)(2,1)S(1)}, u32[]{:S(2)}, u32[]{:S(2)}) %collective-permute-start.61) | collective-permute-done | bytes 131104 | tf_op jit(solution)/shard_map/ppermute | solution.py:622
  108.1 1.8 collective-permute-start.63
  111.2 1.8 collective-permute-start.53
  113.6 5.6 %shard_map.175 = (f32[256,1024]{1,0:T(8,128)S(1)}, bf16[256,1024]{1,0:T(8,128)(2,1)S(1)}, f32[256,256]{1,0:T(8,128)S(1)}, f32[256,512]{1,0:T(8,128)S(1)}, bf16[256,512]{1,0:T(8,128)(2,1)S(1)}) custom-call(s32[11]{0:T(128)S(1)} %pad_add_fusion.meta, f32[256,1024]{1,0:T(8,128)S(1)} %bitcast.18, f32[256,1024]{1,0:T(8,128)S(1)} %get-tuple-element.102.residual, ...), custom_call_target="tpu_custom_call" | custom-call | flops 500000000 | bytes 7113772 | tf_op jit(solution)/shard_map/pallas_call | solution.py:250
  119.2 2.8 %shard_map.177 = (f32[256,1024]{1,0:T(8,128)S(1)}, bf16[528,256]{1,0:T(8,128)(2,1)S(1)}, bf16[528,256]{1,0:T(8,128)(2,1)S(1)}, bf16[528,256]{1,0:T(8,128)(2,1)S(...) custom-call(s32[11]{0:T(128)S(1)} %pad_add_fusion.meta, ...), custom_call_target="tpu_custom_call" | custom-call | flops 1100000000 | bytes 9142316 | tf_op jit(solution)/shard_map/pallas_call | solution.py:250
  122.0 1.8 collective-permute-start.43
  124.7 1.8 collective-permute-start.55
  127.5 1.8 collective-permute-start.65
  130.9 1.7 collective-permute-start.45
  137.9 1.9 collective-permute-done.65.ahead
  139.8 1.8 collective-permute-start.57
  141.8 3.8 %collective-permute-done.45.ahead = bf16[528,256]{1,0:T(8,128)(2,1)S(1)} collective-permute-done((bf16[528,256]{1,0:T(8,128)(2,1)S(1)}, bf16[528,256]{1,0:T(8,128)(2,1)S(1)}, u32[]{:S(2)}, u32[]{:S(2)}) %collective-permute-start.45) | collective-permute-done | bytes 270368 | tf_op jit(solution)/shard_map/ppermute | solution.py:622
  148.0 1.7 collective-permute-start.47
  152.2 4.5 %collective-permute-done.57.ahead = bf16[128,1024]{1,0:T(8,128)(2,1)S(1)} collective-permute-done((bf16[128,1024]{1,0:T(8,128)(2,1)S(1)}, bf16[128,1024]{1,0:T(8,128)(2,1)S(1)}, u32[]{:S(2)}, u32[]{:S(2)}) %collective-permute-start.57) | collective-permute-done | bytes 262176 | tf_op jit(solution)/shard_map/ppermute | solution.py:622
  157.5 2.1 %collective-permute-start.68 = (bf16[128,1024]{1,0:T(8,128)(2,1)S(1)}, bf16[128,1024]{1,0:T(8,128)(2,1)S(1)}, u32[]{:S(2)}, u32[]{:S(2)}) collective-permute-start(bf16[128,1024]{1,0:T(8,128)(2,1)S(1)} %get-tuple-element.176), channel_id=1, source_target_pairs={{0,4},{8,0},{16,8},{24,16},{28,24},{20,28},{12,20},{4,12},{1,5},{9... | collective-permute-start | bytes 786440 | tf_op jit(solution)/shard_map/ppermute | solution.py:626
  159.6 3.0 %collective-permute-done.47.ahead = bf16[528,256]{1,0:T(8,128)(2,1)S(1)} collective-permute-done((bf16[528,256]{1,0:T(8,128)(2,1)S(1)}, bf16[528,256]{1,0:T(8,128)(2,1)S(1)}, u32[]{:S(2)}, u32[]{:S(2)}) %collective-permute-start.47) | collective-permute-done | bytes 270368 | tf_op jit(solution)/shard_map/ppermute | solution.py:622
  164.8 3.4 %collective-permute-done.67.ahead = bf16[128,1024]{1,0:T(8,128)(2,1)S(1)} collective-permute-done((bf16[128,1024]{1,0:T(8,128)(2,1)S(1)}, bf16[128,1024]{1,0:T(8,128)(2,1)S(1)}, u32[]{:S(2)}, u32[]{:S(2)}) %collective-permute-start.67) | collective-permute-done | bytes 262176 | tf_op jit(solution)/shard_map/ppermute | solution.py:622
  168.2 2.0 %collective-permute-start.50 = (bf16[528,256]{1,0:T(8,128)(2,1)S(1)}, bf16[528,256]{1,0:T(8,128)(2,1)S(1)}, u32[]{:S(2)}, u32[]{:S(2)}) collective-permute-start(bf16[528,256]{1,0:T(8,128)(2,1)S(1)} %get-tuple-element.141), channel_id=1, source_target_pairs={{0,4},{8,0},{16,8},{24,16},{28,24},{20,28},{12,20},{4,12},{1,5},{9... | collective-permute-start | bytes 811016 | tf_op jit(solution)/shard_map/ppermute | solution.py:626
  171.9 6.0 %collective-permute-done.49.ahead = bf16[528,256]{1,0:T(8,128)(2,1)S(1)} collective-permute-done((bf16[528,256]{1,0:T(8,128)(2,1)S(1)}, bf16[528,256]{1,0:T(8,128)(2,1)S(1)}, u32[]{:S(2)}, u32[]{:S(2)}) %collective-permute-start.49) | collective-permute-done | bytes 270368 | tf_op jit(solution)/shard_map/ppermute | solution.py:622
  185.5 1.8 shard_map.176
  188.3 2.3 %shard_map.179 = f32[256,1024]{1,0:T(8,128)} custom-call(s32[11]{0:T(128)S(1)} %pad_add_fusion.meta, f32[256,1024]{1,0:T(8,128)S(1)} %bitcast.16, f32[256,1024]{1,0:T(8,128)S(1)} %get-tuple-element.116.residual_grad, f32[8,1024]{1,0:T(8,128)S(1)} %get-tuple-element.93.small, bf16[128,1024]{1,0:T(8,128)(2,1)S(1)} %add_convert_fusion.s0, ...), custom_call_target="tpu_custom_call" | custom-call | flops 5000000 | bytes 4227116 | tf_op jit(solution)/shard_map/pallas_call | solution.py:250
  (154 shorter events, 48.3 us)
Async XLA Ops:
  5.7 9.6 %collective-permute-start.2 = (bf16[528,256]{1,0:T(8,128)(2,1)S(1)}, bf16[528,256]{1,0:T(8,128)(2,1)S(1)}, u32[]{:S(2)}, u32[]{:S(2)}) collective-permute-start(bf16[528,256]{1,0:T(8,128)(2,1)S(1)} %shard_map.170.refs_0_), channel_id=1, source_target_pairs={{0,4},{8,0},{16,8},{24,16},{28,24},{20,28},{12,20},{4,12},{1,5},{9... | collective-permute-start | bytes 811016 | tf_op jit(solution)/shard_map/ppermute | solution.py:626
  19.4 10.3 %collective-permute-start = (bf16[128,1024]{1,0:T(8,128)(2,1)S(1)}, bf16[128,1024]{1,0:T(8,128)(2,1)S(1)}, u32[]{:S(2)}, u32[]{:S(2)}) collective-permute-start(bf16[128,1024]{1,0:T(8,128)(2,1)S(1)} %shard_map.169), channel_id=1, source_target_pairs={{0,4},{1,5},{2,6},{3,7},{8,12},{9,13},{10,14},{11,15},{16,20},{17,... | collective-permute-start | bytes 786440 | tf_op jit(solution)/shard_map/ppermute | solution.py:688
  23.0 10.3 %collective-permute-start.4 = (bf16[528,256]{1,0:T(8,128)(2,1)S(1)}, bf16[528,256]{1,0:T(8,128)(2,1)S(1)}, u32[]{:S(2)}, u32[]{:S(2)}) collective-permute-start(bf16[528,256]{1,0:T(8,128)(2,1)S(1)} %collective-permute-done.3.refs_2_), channel_id=1, source_target_pairs={{0,4},{8,0},{16,8},{24,16},{28,24},{20,28},{12,20},{4,12},{1,5},{9... | collective-permute-start | bytes 811016 | tf_op jit(solution)/shard_map/ppermute | solution.py:626
  24.8 11.7 %collective-permute-start.7 = (bf16[528,256]{1,0:T(8,128)(2,1)S(1)}, bf16[528,256]{1,0:T(8,128)(2,1)S(1)}, u32[]{:S(2)}, u32[]{:S(2)}) collective-permute-start(bf16[528,256]{1,0:T(8,128)(2,1)S(1)} %collective-permute-done.6.refs_7_), channel_id=1, source_target_pairs={{0,8},{8,16},{16,24},{24,28},{28,20},{20,12},{12,4},{4,0},{1,9},{9... | collective-permute-start | bytes 811016 | tf_op jit(solution)/shard_map/ppermute | solution.py:622
  25.1 14.2 %collective-permute-start.17 = (bf16[128,1024]{1,0:T(8,128)(2,1)}, bf16[128,1024]{1,0:T(8,128)(2,1)}, u32[]{:S(2)}, u32[]{:S(2)}) collective-permute-start(bf16[128,1024]{1,0:T(8,128)(2,1)} %refs_0_), channel_id=1, source_target_pairs={{0,8},{8,16},{16,24},{24,28},{28,20},{20,12},{12,4},{4,0},{1,9},{9... | collective-permute-start | bytes 786440 | tf_op jit(solution)/shard_map/ppermute | solution.py:622
  29.7 9.7 %collective-permute-start.1 = (bf16[128,1024]{1,0:T(8,128)(2,1)S(1)}, bf16[128,1024]{1,0:T(8,128)(2,1)S(1)}, u32[]{:S(2)}, u32[]{:S(2)}) collective-permute-start(bf16[128,1024]{1,0:T(8,128)(2,1)S(1)} %collective-permute-done.far_a), channel_id=1, source_target_pairs={{0,1},{1,0},{2,3},{3,2},{4,5},{5,4},{6,7},{7,6},{8,9},{9,8},{10,11... | collective-permute-start | bytes 786440 | tf_op jit(solution)/shard_map/ppermute | solution.py:689
  37.1 13.5 %collective-permute-start.14 = (bf16[128,1024]{1,0:T(8,128)(2,1)}, bf16[128,1024]{1,0:T(8,128)(2,1)}, u32[]{:S(2)}, u32[]{:S(2)}) collective-permute-start(bf16[128,1024]{1,0:T(8,128)(2,1)} %refs_0_), channel_id=1, source_target_pairs={{0,4},{8,0},{16,8},{24,16},{28,24},{20,28},{12,20},{4,12},{1,5},{9... | collective-permute-start | bytes 786440 | tf_op jit(solution)/shard_map/ppermute | solution.py:626
  39.3 11.4 %collective-permute-start.18 = (bf16[128,1024]{1,0:T(8,128)(2,1)}, bf16[128,1024]{1,0:T(8,128)(2,1)S(1)}, u32[]{:S(2)}, u32[]{:S(2)}) collective-permute-start(bf16[128,1024]{1,0:T(8,128)(2,1)} %collective-permute-done.17.refs_8_), channel_id=1, source_target_pairs={{0,8},{8,16},{16,24},{24,28},{28,20},{20,12},{12,4},{4,0},{1,9},{9... | collective-permute-start | bytes 786440 | tf_op jit(solution)/shard_map/ppermute | solution.py:622
  39.4 13.3 %collective-permute-start.25 = (bf16[128,1024]{1,0:T(8,128)(2,1)}, bf16[128,1024]{1,0:T(8,128)(2,1)S(1)}, u32[]{:S(2)}, u32[]{:S(2)}) collective-permute-start(bf16[128,1024]{1,0:T(8,128)(2,1)} %refs_0_.1), channel_id=1, source_target_pairs={{0,8},{8,16},{16,24},{24,28},{28,20},{20,12},{12,4},{4,0},{1,9},{9... | collective-permute-start | bytes 786440 | tf_op jit(solution)/shard_map/ppermute | solution.py:622
  41.0 14.1 %collective-permute-start.22 = (bf16[128,1024]{1,0:T(8,128)(2,1)}, bf16[128,1024]{1,0:T(8,128)(2,1)S(1)}, u32[]{:S(2)}, u32[]{:S(2)}) collective-permute-start(bf16[128,1024]{1,0:T(8,128)(2,1)} %refs_0_.1), channel_id=1, source_target_pairs={{0,4},{8,0},{16,8},{24,16},{28,24},{20,28},{12,20},{4,12},{1,5},{9... | collective-permute-start | bytes 786440 | tf_op jit(solution)/shard_map/ppermute | solution.py:626
  50.6 9.4 %collective-permute-start.15 = (bf16[128,1024]{1,0:T(8,128)(2,1)}, bf16[128,1024]{1,0:T(8,128)(2,1)S(1)}, u32[]{:S(2)}, u32[]{:S(2)}) collective-permute-start(bf16[128,1024]{1,0:T(8,128)(2,1)} %collective-permute-done.14.refs_1_), channel_id=1, source_target_pairs={{0,4},{8,0},{16,8},{24,16},{28,24},{20,28},{12,20},{4,12},{1,5},{9... | collective-permute-start | bytes 786440 | tf_op jit(solution)/shard_map/ppermute | solution.py:626
  50.7 16.7 %collective-permute-start.19 = (bf16[128,1024]{1,0:T(8,128)(2,1)S(1)}, bf16[128,1024]{1,0:T(8,128)(2,1)S(1)}, u32[]{:S(2)}, u32[]{:S(2)}) collective-permute-start(bf16[128,1024]{1,0:T(8,128)(2,1)S(1)} %collective-permute-done.18.refs_7_), channel_id=1, source_target_pairs={{0,8},{8,16},{16,24},{24,28},{28,20},{20,12},{12,4},{4,0},{1,9},{9... | collective-permute-start | bytes 786440 | tf_op jit(solution)/shard_map/ppermute | solution.py:622
  52.7 12.3 %collective-permute-start.26 = (bf16[128,1024]{1,0:T(8,128)(2,1)S(1)}, bf16[128,1024]{1,0:T(8,128)(2,1)S(1)}, u32[]{:S(2)}, u32[]{:S(2)}) collective-permute-start(bf16[128,1024]{1,0:T(8,128)(2,1)S(1)} %collective-permute-done.25.refs_8_), channel_id=1, source_target_pairs={{0,8},{8,16},{16,24},{24,28},{28,20},{20,12},{12,4},{4,0},{1,9},{9... | collective-permute-start | bytes 786440 | tf_op jit(solution)/shard_map/ppermute | solution.py:622
  55.1 11.8 %collective-permute-start.23 = (bf16[128,1024]{1,0:T(8,128)(2,1)S(1)}, bf16[128,1024]{1,0:T(8,128)(2,1)S(1)}, u32[]{:S(2)}, u32[]{:S(2)}) collective-permute-start(bf16[128,1024]{1,0:T(8,128)(2,1)S(1)} %collective-permute-done.22.refs_1_), channel_id=1, source_target_pairs={{0,4},{8,0},{16,8},{24,16},{28,24},{20,28},{12,20},{4,12},{1,5},{9... | collective-permute-start | bytes 786440 | tf_op jit(solution)/shard_map/ppermute | solution.py:626
  55.2 12.2 %collective-permute-start.11 = (bf16[128,1024]{1,0:T(8,128)(2,1)S(1)}, bf16[128,1024]{1,0:T(8,128)(2,1)S(1)}, u32[]{:S(2)}, u32[]{:S(2)}) collective-permute-start(bf16[128,1024]{1,0:T(8,128)(2,1)S(1)} %add_convert_fusion.3.s0), channel_id=1, source_target_pairs={{0,2},{2,0},{1,3},{3,1},{4,6},{6,4},{5,7},{7,5},{8,10},{10,8},{9,1... | collective-permute-start | bytes 786440 | tf_op jit(solution)/shard_map/ppermute | solution.py:655
  60.0 11.2 %collective-permute-start.16 = (bf16[128,1024]{1,0:T(8,128)(2,1)S(1)}, bf16[128,1024]{1,0:T(8,128)(2,1)S(1)}, u32[]{:S(2)}, u32[]{:S(2)}) collective-permute-start(bf16[128,1024]{1,0:T(8,128)(2,1)S(1)} %collective-permute-done.15.refs_2_), channel_id=1, source_target_pairs={{0,4},{8,0},{16,8},{24,16},{28,24},{20,28},{12,20},{4,12},{1,5},{9... | collective-permute-start | bytes 786440 | tf_op jit(solution)/shard_map/ppermute | solution.py:626
  65.0 8.7 %collective-permute-start.27 = (bf16[128,1024]{1,0:T(8,128)(2,1)S(1)}, bf16[128,1024]{1,0:T(8,128)(2,1)S(1)}, u32[]{:S(2)}, u32[]{:S(2)}) collective-permute-start(bf16[128,1024]{1,0:T(8,128)(2,1)S(1)} %collective-permute-done.26.refs_7_), channel_id=1, source_target_pairs={{0,8},{8,16},{16,24},{24,28},{28,20},{20,12},{12,4},{4,0},{1,9},{9... | collective-permute-start | bytes 786440 | tf_op jit(solution)/shard_map/ppermute | solution.py:622
  66.9 10.4 %collective-permute-start.24 = (bf16[128,1024]{1,0:T(8,128)(2,1)S(1)}, bf16[128,1024]{1,0:T(8,128)(2,1)S(1)}, u32[]{:S(2)}, u32[]{:S(2)}) collective-permute-start(bf16[128,1024]{1,0:T(8,128)(2,1)S(1)} %collective-permute-done.23.refs_2_), channel_id=1, source_target_pairs={{0,4},{8,0},{16,8},{24,16},{28,24},{20,28},{12,20},{4,12},{1,5},{9... | collective-permute-start | bytes 786440 | tf_op jit(solution)/shard_map/ppermute | solution.py:626
  67.3 13.2 %collective-permute-start.12 = (bf16[128,1024]{1,0:T(8,128)(2,1)S(1)}, bf16[128,1024]{1,0:T(8,128)(2,1)S(1)}, u32[]{:S(2)}, u32[]{:S(2)}) collective-permute-start(bf16[128,1024]{1,0:T(8,128)(2,1)S(1)} %add_convert_fusion.3.s0), channel_id=1, source_target_pairs={{0,1},{1,0},{2,3},{3,2},{4,5},{5,4},{6,7},{7,6},{8,9},{9,8},{10,11... | collective-permute-start | bytes 786440 | tf_op jit(solution)/shard_map/ppermute | solution.py:655
  67.4 13.2 %collective-permute-start.13 = (bf16[128,1024]{1,0:T(8,128)(2,1)S(1)}, bf16[128,1024]{1,0:T(8,128)(2,1)S(1)}, u32[]{:S(2)}, u32[]{:S(2)}) collective-permute-start(bf16[128,1024]{1,0:T(8,128)(2,1)S(1)} %collective-permute-done.11.s1), channel_id=1, source_target_pairs={{0,1},{1,0},{2,3},{3,2},{4,5},{5,4},{6,7},{7,6},{8,9},{9,8},{10,11... | collective-permute-start | bytes 786440 | tf_op jit(solution)/shard_map/ppermute | solution.py:655
  93.4 19.9 %collective-permute-start.32 = (bf16[128,1024]{1,0:T(8,128)(2,1)S(1)}, bf16[128,1024]{1,0:T(8,128)(2,1)S(1)}, u32[]{:S(2)}, u32[]{:S(2)}) collective-permute-start(bf16[128,1024]{1,0:T(8,128)(2,1)S(1)} %add_convert_fusion.2.s0), channel_id=1, source_target_pairs={{0,1},{1,0},{2,3},{3,2},{4,5},{5,4},{6,7},{7,6},{8,9},{9,8},{10,11... | collective-permute-start | bytes 786440 | tf_op jit(solution)/shard_map/ppermute | solution.py:655
  100.3 13.3 %collective-permute-start.33 = (bf16[128,1024]{1,0:T(8,128)(2,1)S(1)}, bf16[128,1024]{1,0:T(8,128)(2,1)S(1)}, u32[]{:S(2)}, u32[]{:S(2)}) collective-permute-start(bf16[128,1024]{1,0:T(8,128)(2,1)S(1)} %collective-permute-done.31.s1), channel_id=1, source_target_pairs={{0,1},{1,0},{2,3},{3,2},{4,5},{5,4},{6,7},{7,6},{8,9},{9,8},{10,11... | collective-permute-start | bytes 786440 | tf_op jit(solution)/shard_map/ppermute | solution.py:655
  108.1 18.4 %collective-permute-start.63 = (bf16[128,1024]{1,0:T(8,128)(2,1)S(1)}, bf16[128,1024]{1,0:T(8,128)(2,1)S(1)}, u32[]{:S(2)}, u32[]{:S(2)}) collective-permute-start(bf16[128,1024]{1,0:T(8,128)(2,1)S(1)} %get-tuple-element.171), channel_id=1, source_target_pairs={{0,8},{8,16},{16,24},{24,28},{28,20},{20,12},{12,4},{4,0},{1,9},{9... | collective-permute-start | bytes 786440 | tf_op jit(solution)/shard_map/ppermute | solution.py:622
  111.2 12.6 %collective-permute-start.53 = (bf16[64,1024]{1,0:T(8,128)(2,1)S(1)}, bf16[64,1024]{1,0:T(8,128)(2,1)S(1)}, u32[]{:S(2)}, u32[]{:S(2)}) collective-permute-start(bf16[64,1024]{1,0:T(8,128)(2,1)S(1)} %get-tuple-element.154), channel_id=1, source_target_pairs={{0,8},{8,16},{16,24},{24,28},{28,20},{20,12},{12,4},{4,0},{1,9},{9... | collective-permute-start | bytes 393224 | tf_op jit(solution)/shard_map/ppermute | solution.py:622
  113.0 11.1 %collective-permute-start.54 = (bf16[64,1024]{1,0:T(8,128)(2,1)S(1)}, bf16[64,1024]{1,0:T(8,128)(2,1)S(1)}, u32[]{:S(2)}, u32[]{:S(2)}) collective-permute-start(bf16[64,1024]{1,0:T(8,128)(2,1)S(1)} %get-tuple-element.155), channel_id=1, source_target_pairs={{0,4},{8,0},{16,8},{24,16},{28,24},{20,28},{12,20},{4,12},{1,5},{9... | collective-permute-start | bytes 393224 | tf_op jit(solution)/shard_map/ppermute | solution.py:626
  113.3 13.5 %collective-permute-start.64 = (bf16[128,1024]{1,0:T(8,128)(2,1)S(1)}, bf16[128,1024]{1,0:T(8,128)(2,1)S(1)}, u32[]{:S(2)}, u32[]{:S(2)}) collective-permute-start(bf16[128,1024]{1,0:T(8,128)(2,1)S(1)} %get-tuple-element.172), channel_id=1, source_target_pairs={{0,4},{8,0},{16,8},{24,16},{28,24},{20,28},{12,20},{4,12},{1,5},{9... | collective-permute-start | bytes 786440 | tf_op jit(solution)/shard_map/ppermute | solution.py:626
  124.7 9.4 %collective-permute-start.55 = (bf16[128,1024]{1,0:T(8,128)(2,1)S(1)}, bf16[128,1024]{1,0:T(8,128)(2,1)S(1)}, u32[]{:S(2)}, u32[]{:S(2)}) collective-permute-start(bf16[128,1024]{1,0:T(8,128)(2,1)S(1)} %get-tuple-element.156), channel_id=1, source_target_pairs={{0,8},{8,16},{16,24},{24,28},{28,20},{20,12},{12,4},{4,0},{1,9},{9... | collective-permute-start | bytes 786440 | tf_op jit(solution)/shard_map/ppermute | solution.py:622
  126.5 9.4 %collective-permute-start.56 = (bf16[128,1024]{1,0:T(8,128)(2,1)S(1)}, bf16[128,1024]{1,0:T(8,128)(2,1)S(1)}, u32[]{:S(2)}, u32[]{:S(2)}) collective-permute-start(bf16[128,1024]{1,0:T(8,128)(2,1)S(1)} %get-tuple-element.157), channel_id=1, source_target_pairs={{0,4},{8,0},{16,8},{24,16},{28,24},{20,28},{12,20},{4,12},{1,5},{9... | collective-permute-start | bytes 786440 | tf_op jit(solution)/shard_map/ppermute | solution.py:626
  127.5 12.3 %collective-permute-start.65 = (bf16[128,1024]{1,0:T(8,128)(2,1)S(1)}, bf16[128,1024]{1,0:T(8,128)(2,1)S(1)}, u32[]{:S(2)}, u32[]{:S(2)}) collective-permute-start(bf16[128,1024]{1,0:T(8,128)(2,1)S(1)} %get-tuple-element.173), channel_id=1, source_target_pairs={{0,8},{8,16},{16,24},{24,28},{28,20},{20,12},{12,4},{4,0},{1,9},{9... | collective-permute-start | bytes 786440 | tf_op jit(solution)/shard_map/ppermute | solution.py:622
  129.3 12.2 %collective-permute-start.66 = (bf16[128,1024]{1,0:T(8,128)(2,1)S(1)}, bf16[128,1024]{1,0:T(8,128)(2,1)S(1)}, u32[]{:S(2)}, u32[]{:S(2)}) collective-permute-start(bf16[128,1024]{1,0:T(8,128)(2,1)S(1)} %get-tuple-element.174), channel_id=1, source_target_pairs={{0,4},{8,0},{16,8},{24,16},{28,24},{20,28},{12,20},{4,12},{1,5},{9... | collective-permute-start | bytes 786440 | tf_op jit(solution)/shard_map/ppermute | solution.py:626
  130.9 14.6 %collective-permute-start.45 = (bf16[528,256]{1,0:T(8,128)(2,1)S(1)}, bf16[528,256]{1,0:T(8,128)(2,1)S(1)}, u32[]{:S(2)}, u32[]{:S(2)}) collective-permute-start(bf16[528,256]{1,0:T(8,128)(2,1)S(1)} %get-tuple-element.136), channel_id=1, source_target_pairs={{0,8},{8,16},{16,24},{24,28},{28,20},{20,12},{12,4},{4,0},{1,9},{9... | collective-permute-start | bytes 811016 | tf_op jit(solution)/shard_map/ppermute | solution.py:622
  134.1 13.2 %collective-permute-start.46 = (bf16[528,256]{1,0:T(8,128)(2,1)S(1)}, bf16[528,256]{1,0:T(8,128)(2,1)S(1)}, u32[]{:S(2)}, u32[]{:S(2)}) collective-permute-start(bf16[528,256]{1,0:T(8,128)(2,1)S(1)} %get-tuple-element.137), channel_id=1, source_target_pairs={{0,4},{8,0},{16,8},{24,16},{28,24},{20,28},{12,20},{4,12},{1,5},{9... | collective-permute-start | bytes 811016 | tf_op jit(solution)/shard_map/ppermute | solution.py:626
  135.9 15.3 %collective-permute-start.38 = (bf16[256,512]{1,0:T(8,128)(2,1)S(1)}, bf16[256,512]{1,0:T(8,128)(2,1)S(1)}, u32[]{:S(2)}, u32[]{:S(2)}) collective-permute-start(bf16[256,512]{1,0:T(8,128)(2,1)S(1)} %get-tuple-element.120.kv_grad_far), channel_id=1, source_target_pairs={{4,0},{5,1},{6,2},{7,3},{12,8},{13,9},{14,10},{15,11},{20,16},{21,... | collective-permute-start | bytes 786440 | tf_op jit(solution)/shard_map/ppermute | solution.py:743
  139.8 17.0 %collective-permute-start.57 = (bf16[128,1024]{1,0:T(8,128)(2,1)S(1)}, bf16[128,1024]{1,0:T(8,128)(2,1)S(1)}, u32[]{:S(2)}, u32[]{:S(2)}) collective-permute-start(bf16[128,1024]{1,0:T(8,128)(2,1)S(1)} %get-tuple-element.158), channel_id=1, source_target_pairs={{0,8},{8,16},{16,24},{24,28},{28,20},{20,12},{12,4},{4,0},{1,9},{9... | collective-permute-start | bytes 786440 | tf_op jit(solution)/shard_map/ppermute | solution.py:622
  141.5 15.3 %collective-permute-start.58 = (bf16[128,1024]{1,0:T(8,128)(2,1)S(1)}, bf16[128,1024]{1,0:T(8,128)(2,1)S(1)}, u32[]{:S(2)}, u32[]{:S(2)}) collective-permute-start(bf16[128,1024]{1,0:T(8,128)(2,1)S(1)} %get-tuple-element.159), channel_id=1, source_target_pairs={{0,4},{8,0},{16,8},{24,16},{28,24},{20,28},{12,20},{4,12},{1,5},{9... | collective-permute-start | bytes 786440 | tf_op jit(solution)/shard_map/ppermute | solution.py:626
  145.6 11.9 %collective-permute-start.34 = (bf16[128,1024]{1,0:T(8,128)(2,1)S(1)}, bf16[128,1024]{1,0:T(8,128)(2,1)S(1)}, u32[]{:S(2)}, u32[]{:S(2)}) collective-permute-start(bf16[128,1024]{1,0:T(8,128)(2,1)S(1)} %get-tuple-element.115), channel_id=1, source_target_pairs={{0,1},{1,0},{2,3},{3,2},{4,5},{5,4},{6,7},{7,6},{8,9},{9,8},{10,11... | collective-permute-start | bytes 786440 | tf_op jit(solution)/shard_map/ppermute | solution.py:655
  148.0 14.6 %collective-permute-start.47 = (bf16[528,256]{1,0:T(8,128)(2,1)S(1)}, bf16[528,256]{1,0:T(8,128)(2,1)S(1)}, u32[]{:S(2)}, u32[]{:S(2)}) collective-permute-start(bf16[528,256]{1,0:T(8,128)(2,1)S(1)} %get-tuple-element.138), channel_id=1, source_target_pairs={{0,8},{8,16},{16,24},{24,28},{28,20},{20,12},{12,4},{4,0},{1,9},{9... | collective-permute-start | bytes 811016 | tf_op jit(solution)/shard_map/ppermute | solution.py:622
  151.2 11.4 %collective-permute-start.48 = (bf16[528,256]{1,0:T(8,128)(2,1)S(1)}, bf16[528,256]{1,0:T(8,128)(2,1)S(1)}, u32[]{:S(2)}, u32[]{:S(2)}) collective-permute-start(bf16[528,256]{1,0:T(8,128)(2,1)S(1)} %get-tuple-element.139), channel_id=1, source_target_pairs={{0,4},{8,0},{16,8},{24,16},{28,24},{20,28},{12,20},{4,12},{1,5},{9... | collective-permute-start | bytes 811016 | tf_op jit(solution)/shard_map/ppermute | solution.py:626
  156.8 11.4 %collective-permute-start.67 = (bf16[128,1024]{1,0:T(8,128)(2,1)S(1)}, bf16[128,1024]{1,0:T(8,128)(2,1)S(1)}, u32[]{:S(2)}, u32[]{:S(2)}) collective-permute-start(bf16[128,1024]{1,0:T(8,128)(2,1)S(1)} %get-tuple-element.175), channel_id=1, source_target_pairs={{0,8},{8,16},{16,24},{24,28},{28,20},{20,12},{12,4},{4,0},{1,9},{9... | collective-permute-start | bytes 786440 | tf_op jit(solution)/shard_map/ppermute | solution.py:622
  156.8 11.4 %collective-permute-start.39 = (bf16[128,1024]{1,0:T(8,128)(2,1)S(1)}, bf16[128,1024]{1,0:T(8,128)(2,1)S(1)}, u32[]{:S(2)}, u32[]{:S(2)}) collective-permute-start(bf16[128,1024]{1,0:T(8,128)(2,1)S(1)} %get-tuple-element.126), channel_id=1, source_target_pairs={{0,1},{1,0},{2,3},{3,2},{4,5},{5,4},{6,7},{7,6},{8,9},{9,8},{10,11... | collective-permute-start | bytes 786440 | tf_op jit(solution)/shard_map/ppermute | solution.py:655
  157.5 12.8 %collective-permute-start.68 = (bf16[128,1024]{1,0:T(8,128)(2,1)S(1)}, bf16[128,1024]{1,0:T(8,128)(2,1)S(1)}, u32[]{:S(2)}, u32[]{:S(2)}) collective-permute-start(bf16[128,1024]{1,0:T(8,128)(2,1)S(1)} %get-tuple-element.176), channel_id=1, source_target_pairs={{0,4},{8,0},{16,8},{24,16},{28,24},{20,28},{12,20},{4,12},{1,5},{9... | collective-permute-start | bytes 786440 | tf_op jit(solution)/shard_map/ppermute | solution.py:626
  162.6 17.2 %collective-permute-start.59 = (bf16[128,1024]{1,0:T(8,128)(2,1)S(1)}, bf16[128,1024]{1,0:T(8,128)(2,1)S(1)}, u32[]{:S(2)}, u32[]{:S(2)}) collective-permute-start(bf16[128,1024]{1,0:T(8,128)(2,1)S(1)} %get-tuple-element.160), channel_id=1, source_target_pairs={{0,8},{8,16},{16,24},{24,28},{28,20},{20,12},{12,4},{4,0},{1,9},{9... | collective-permute-start | bytes 786440 | tf_op jit(solution)/shard_map/ppermute | solution.py:622
  162.6 9.3 %collective-permute-start.35 = (bf16[128,1024]{1,0:T(8,128)(2,1)S(1)}, bf16[128,1024]{1,0:T(8,128)(2,1)S(1)}, u32[]{:S(2)}, u32[]{:S(2)}) collective-permute-start(bf16[128,1024]{1,0:T(8,128)(2,1)S(1)} %add_convert_fusion.1.s0), channel_id=1, source_target_pairs={{0,2},{2,0},{1,3},{3,1},{4,6},{6,4},{5,7},{7,5},{8,10},{10,8},{9,1... | collective-permute-start | bytes 786440 | tf_op jit(solution)/shard_map/ppermute | solution.py:655
  168.2 9.6 %collective-permute-start.49 = (bf16[528,256]{1,0:T(8,128)(2,1)S(1)}, bf16[528,256]{1,0:T(8,128)(2,1)S(1)}, u32[]{:S(2)}, u32[]{:S(2)}) collective-permute-start(bf16[528,256]{1,0:T(8,128)(2,1)S(1)} %get-tuple-element.140), channel_id=1, source_target_pairs={{0,8},{8,16},{16,24},{24,28},{28,20},{20,12},{12,4},{4,0},{1,9},{9... | collective-permute-start | bytes 811016 | tf_op jit(solution)/shard_map/ppermute | solution.py:622
  168.2 9.6 %collective-permute-start.50 = (bf16[528,256]{1,0:T(8,128)(2,1)S(1)}, bf16[528,256]{1,0:T(8,128)(2,1)S(1)}, u32[]{:S(2)}, u32[]{:S(2)}) collective-permute-start(bf16[528,256]{1,0:T(8,128)(2,1)S(1)} %get-tuple-element.141), channel_id=1, source_target_pairs={{0,4},{8,0},{16,8},{24,16},{28,24},{20,28},{12,20},{4,12},{1,5},{9... | collective-permute-start | bytes 811016 | tf_op jit(solution)/shard_map/ppermute | solution.py:626
  170.3 9.5 %collective-permute-start.40 = (bf16[128,1024]{1,0:T(8,128)(2,1)S(1)}, bf16[128,1024]{1,0:T(8,128)(2,1)S(1)}, u32[]{:S(2)}, u32[]{:S(2)}) collective-permute-start(bf16[128,1024]{1,0:T(8,128)(2,1)S(1)} %add_convert_fusion.s0), channel_id=1, source_target_pairs={{0,2},{2,0},{1,3},{3,1},{4,6},{6,4},{5,7},{7,5},{8,10},{10,8},{9,1... | collective-permute-start | bytes 786440 | tf_op jit(solution)/shard_map/ppermute | solution.py:655
  171.9 9.3 %collective-permute-start.60 = (bf16[128,1024]{1,0:T(8,128)(2,1)S(1)}, bf16[128,1024]{1,0:T(8,128)(2,1)S(1)}, u32[]{:S(2)}, u32[]{:S(2)}) collective-permute-start(bf16[128,1024]{1,0:T(8,128)(2,1)S(1)} %get-tuple-element.161), channel_id=1, source_target_pairs={{0,4},{8,0},{16,8},{24,16},{28,24},{20,28},{12,20},{4,12},{1,5},{9... | collective-permute-start | bytes 786440 | tf_op jit(solution)/shard_map/ppermute | solution.py:626
  179.8 8.5 %collective-permute-start.41 = (bf16[128,1024]{1,0:T(8,128)(2,1)S(1)}, bf16[128,1024]{1,0:T(8,128)(2,1)S(1)}, u32[]{:S(2)}, u32[]{:S(2)}) collective-permute-start(bf16[128,1024]{1,0:T(8,128)(2,1)S(1)} %add_convert_fusion.s0), channel_id=1, source_target_pairs={{0,1},{1,0},{2,3},{3,2},{4,5},{5,4},{6,7},{7,6},{8,9},{9,8},{10,11... | collective-permute-start | bytes 786440 | tf_op jit(solution)/shard_map/ppermute | solution.py:655
  (32 other events, 244.9 us)
where the time goes:
time: 191 us
  starting transfers between devices  70.7 us (37%)
  waiting for transfers between devices  67.8 us (35%)
  Pallas kernels  42.5 us (22%)
  local copies, waits for them, and re-layouts  8.23 us (4%)
    pallas_call x24, Pallas kernels, call(): pl.pallas_call(kernel, out_shape=tuple(outs), in_specs=[SMEM] + [VMEM] *...  42.5 us
    ppermute x24, waiting for transfers between devices, send_ahead(): return lax.ppermute(value, AXES, AHEAD)  33.9 us
    ppermute x24, starting transfers between devices, send_ahead(): return lax.ppermute(value, AXES, AHEAD)  30.3 us
    ppermute x24, starting transfers between devices, send_behind(): return lax.ppermute(value, AXES, BEHIND)  26 us
    ppermute x24, waiting for transfers between devices, send_behind(): return lax.ppermute(value, AXES, BEHIND)  20.5 us
    ppermute x16, waiting for transfers between devices, tp_send(): return lambda value: lax.ppermute(value, TP, pairs)  8.41 us
    ppermute x16, starting transfers between devices, tp_send(): return lambda value: lax.ppermute(value, TP, pairs)  7.99 us
    unnamed x23, local copies, waits for them, and re-layouts  5.77 us
  transfers between devices with their start and end apart: 69, of which 24 were waited for; matrix products, arithmetic and copies ran while one was open for 1% of the time, Pallas kernels for 18%

commit v1 on v0

--- a/solution.py
+++ b/solution.py
@@ -289,7 +289,11 @@
     return centered * inverse, inverse
 
 
-def pack_kernel(meta, attend, merge, gains, shifts, bias, seg, out):
+def whole_block(dims):
+    return pl.BlockSpec(dims, lambda i: (0,) * len(dims))
+
+
+def pack_kernel(attend, merge, gains, shifts, bias, seg, out):
     for t in range(3):
         out[t * 128 : t * 128 + 128, :] = attend[t]
     out[384:512, :] = merge[...]
@@ -442,9 +446,9 @@
     store_parts(meta, cot_half, act, outs)
 
 
-def ffn_second_kernel(meta, residual, cot_half, act, slope, expand, *refs):
+def ffn_second_kernel(meta, residual, cot_half, slope, expand, *refs):
     blocks = refs[:9]
-    pre_half, later_keep, later_give, red_keep, red_give, grads, reduce, part = refs[9:]
+    pre_half, later_keep, later_give, grads, reduce, part = refs[9:]
     assemble(meta, blocks, reduce)
     grads[...] = jnp.zeros_like(grads)
 
@@ -469,6 +473,8 @@
     grads[0:1, :] = jnp.sum(part[...] * normed, axis=0, keepdims=True)
     grads[1:2, :] = jnp.sum(part[...], axis=0, keepdims=True)
 
+
+def reduced_kernel(meta, act, reduce, red_keep, red_give, part):
     def reduced(i, carry):
         at = pl.ds(pl.multiple_of(i * 256, 256), 256)
         part[:, at] = dot_nt(act[...], reduce[at, :])
@@ -678,11 +684,18 @@
     cot = cotangent.reshape(256, 1024)
     rows, half, square = (256, 1024), (128, 1024), (256, 256)
     part = pltpu.VMEM(rows, f32)
-    (pack,) = call(
-        pack_kernel, [shape((528, 256), bf16)],
-        [meta, jnp.swapaxes(attend_weight, 0, 1), merge_weight, gains, shifts, expand_bias,
-         segment_ids], 1_000_000,
-    )
+    pack_args = [
+        jnp.swapaxes(attend_weight, 0, 1), merge_weight, gains, shifts, expand_bias, segment_ids
+    ]
+    pack_args = [pltpu.with_memory_space_constraint(a, pltpu.HBM) for a in pack_args]
+    pack = pl.pallas_call(
+        pack_kernel,
+        grid=(1,),
+        out_shape=shape((528, 256), bf16),
+        in_specs=[whole_block(a.shape) for a in pack_args],
+        out_specs=whole_block((528, 256)),
+        compiler_params=pltpu.CompilerParams(vmem_limit_bytes=ROOM),
+    )(*pack_args)
     blocks = gather_blocks(pack, lambda v: v[:, :128], lambda v: v[:, 128:])
     (normed_half,) = call(norm_half_kernel, [shape(half, bf16)], [meta, x], 1_000_000)
     far_a = lax.ppermute(normed_half, CTX, [(0, 1)])
@@ -715,11 +728,15 @@
         [meta, x, cot, small, *tp_exchange(keep, give)] + expand_blocks,
         1_100_000_000, [part], 300_000,
     )
-    pre_half, later_keep, later_give, red_keep, red_give, grads = call(
+    pre_half, later_keep, later_give, grads, reduce = call(
         ffn_second_kernel,
-        [shape(rows, bf16)] + [shape(half, f32), shape(half, bf16)] * 2 + [shape((8, 1024), f32)],
-        [meta, residual, cot_half, act, slope, expand] + reduce_blocks,
-        1_600_000_000, [pltpu.VMEM((1024, 1024), bf16), part],
+        [shape(rows, bf16), shape(half, f32), shape(half, bf16), shape((8, 1024), f32),
+         shape((1024, 1024), bf16)],
+        [meta, residual, cot_half, slope, expand] + reduce_blocks, 1_100_000_000, [part],
+    )
+    red_keep, red_give = call(
+        reduced_kernel, [shape(half, f32), shape(half, bf16)], [meta, act, reduce],
+        550_000_000, [part],
     )
     (reduce_grad,) = sum_blocks(
         meta, reduce_parts, first_rows_kernel, last_kernel, [shape(half, f32)]

time: 191 us -> 186 us (0.974)
  local copies, waits for them, and re-layouts: 8.23 us -> 3.82 us
  waiting for transfers between devices: 67.8 us -> 64.4 us
    ppermute x24, waiting for transfers between devices: 33.9 us -> 19.8 us  [send_ahead(): return lax.ppermute(value, AXES, AHEAD)]
    ppermute x24, waiting for transfers between devices: 20.5 us -> 27.8 us  [send_behind(): return lax.ppermute(value, AXES, BEHIND)]
    unnamed x23 -> x13, local copies, waits for them, and re-layouts: 5.77 us -> 1.36 us
    ppermute x1, waiting for transfers between devices: 1.44 us -> 4.77 us  [fast_shards(): kv_grad_in = lax.ppermute(kv_grad_far, CTX, [(1, 0)])]
    ppermute x24, starting transfers between devices: 30.3 us -> 33 us  [send_ahead(): return lax.ppermute(value, AXES, AHEAD)]
  transfers between devices with their start and end apart: 69 -> 69, of which waited for: 24 -> 27; matrix products, arithmetic and copies ran while one was open for 1% -> 2% of each run, Pallas kernels for 18% -> 20%
where the time goes in v1:
time: 186 us
  starting transfers between devices  72.6 us (39%)
  waiting for transfers between devices  64.4 us (35%)
  Pallas kernels  43.5 us (23%)
  local copies, waits for them, and re-layouts  3.82 us (2%)
    pallas_call x24, Pallas kernels, call(): pl.pallas_call(kernel, out_shape=tuple(outs), in_specs=[SMEM] + [VMEM] *...  42.5 us
    ppermute x24, starting transfers between devices, send_ahead(): return lax.ppermute(value, AXES, AHEAD)  33 us
    ppermute x24, waiting for transfers between devices, send_behind(): return lax.ppermute(value, AXES, BEHIND)  27.8 us
    ppermute x24, starting transfers between devices, send_behind(): return lax.ppermute(value, AXES, BEHIND)  25.1 us
    ppermute x24, waiting for transfers between devices, send_ahead(): return lax.ppermute(value, AXES, AHEAD)  19.8 us
    ppermute x16, waiting for transfers between devices, tp_send(): return lambda value: lax.ppermute(value, TP, pairs)  8.4 us
    ppermute x16, starting transfers between devices, tp_send(): return lambda value: lax.ppermute(value, TP, pairs)  7.83 us
    ppermute x1, waiting for transfers between devices, fast_shards(): kv_grad_in = lax.ppermute(kv_grad_far, CTX, [(1, 0)])  4.77 us
  transfers between devices with their start and end apart: 69, of which 27 were waited for; matrix products, arithmetic and copies ran while one was open for 2% of the time, Pallas kernels for 20%

profile of v1, /device:TPU:0, one launch (start us, length us, event | category | flops | bytes accessed | tf_op | source)
XLA Modules:
  0.0 185.8 jit_solution(18183958945379954753)
XLA Ops:
  1.7 3.0 %collective-permute-start.2 = (bf16[528,256]{1,0:T(8,128)(2,1)S(1)}, bf16[528,256]{1,0:T(8,128)(2,1)S(1)}, u32[]{:S(2)}, u32[]{:S(2)}) collective-permute-start(bf16[528,256]{1,0:T(8,128)(2,1)S(1)} %shard_map.170.refs_0_), channel_id=1, source_target_pairs={{0,4},{8,0},{16,8},{24,16},{28,24},{20,28},{12,20},{4,12},{1,5},{9... | collective-permute-start | bytes 811016 | tf_op jit(solution)/shard_map/ppermute | solution.py:632
  4.8 6.4 %collective-permute-done.2.refs_1_ = bf16[528,256]{1,0:T(8,128)(2,1)S(1)} collective-permute-done((bf16[528,256]{1,0:T(8,128)(2,1)S(1)}, bf16[528,256]{1,0:T(8,128)(2,1)S(1)}, u32[]{:S(2)}, u32[]{:S(2)}) %collective-permute-start.2) | collective-permute-done | bytes 270368 | tf_op jit(solution)/shard_map/ppermute | solution.py:632
  11.3 1.7 collective-permute-start.3
  15.4 3.6 %collective-permute-start = (bf16[128,1024]{1,0:T(8,128)(2,1)S(1)}, bf16[128,1024]{1,0:T(8,128)(2,1)S(1)}, u32[]{:S(2)}, u32[]{:S(2)}) collective-permute-start(bf16[128,1024]{1,0:T(8,128)(2,1)S(1)} %shard_map.169), channel_id=1, source_target_pairs={{0,4},{1,5},{2,6},{3,7},{8,12},{9,13},{10,14},{11,15},{16,20},{17,... | collective-permute-start | bytes 786440 | tf_op jit(solution)/shard_map/ppermute | solution.py:701
  19.0 1.6 collective-permute-start.4
  21.1 1.6 collective-permute-start.17
  22.7 3.0 %collective-permute-done.far_a = bf16[128,1024]{1,0:T(8,128)(2,1)S(1)} collective-permute-done((bf16[128,1024]{1,0:T(8,128)(2,1)S(1)}, bf16[128,1024]{1,0:T(8,128)(2,1)S(1)}, u32[]{:S(2)}, u32[]{:S(2)}) %collective-permute-start) | collective-permute-done | bytes 262176 | tf_op jit(solution)/shard_map/ppermute | solution.py:701
  25.7 3.6 %collective-permute-done.4.refs_3_ = bf16[528,256]{1,0:T(8,128)(2,1)S(1)} collective-permute-done((bf16[528,256]{1,0:T(8,128)(2,1)S(1)}, bf16[528,256]{1,0:T(8,128)(2,1)S(1)}, u32[]{:S(2)}, u32[]{:S(2)}) %collective-permute-start.4) | collective-permute-done | bytes 270368 | tf_op jit(solution)/shard_map/ppermute | solution.py:632
  29.9 2.5 %collective-permute-start.9 = (bf16[528,128]{1,0:T(8,128)(2,1)}, bf16[528,128]{1,0:T(8,128)(2,1)}, u32[]{:S(2)}, u32[]{:S(2)}) collective-permute-start(bf16[528,128]{1,0:T(8,128)(2,1)} %slice.41), channel_id=1, source_target_pairs={{0,4},{8,0},{16,8},{24,16},{28,24},{20,28},{12,20},{4,12},{1,5},{9... | collective-permute-start | bytes 405512 | tf_op jit(solution)/shard_map/ppermute | solution.py:632
  33.1 2.0 %collective-permute-start.14 = (bf16[128,1024]{1,0:T(8,128)(2,1)}, bf16[128,1024]{1,0:T(8,128)(2,1)}, u32[]{:S(2)}, u32[]{:S(2)}) collective-permute-start(bf16[128,1024]{1,0:T(8,128)(2,1)} %refs_0_), channel_id=1, source_target_pairs={{0,4},{8,0},{16,8},{24,16},{28,24},{20,28},{12,20},{4,12},{1,5},{9... | collective-permute-start | bytes 786440 | tf_op jit(solution)/shard_map/ppermute | solution.py:632
  35.3 1.8 collective-permute-start.25
  37.0 2.1 %collective-permute-start.22 = (bf16[128,1024]{1,0:T(8,128)(2,1)}, bf16[128,1024]{1,0:T(8,128)(2,1)S(1)}, u32[]{:S(2)}, u32[]{:S(2)}) collective-permute-start(bf16[128,1024]{1,0:T(8,128)(2,1)} %refs_0_.1), channel_id=1, source_target_pairs={{0,4},{8,0},{16,8},{24,16},{28,24},{20,28},{12,20},{4,12},{1,5},{9... | collective-permute-start | bytes 786440 | tf_op jit(solution)/shard_map/ppermute | solution.py:632
  39.8 2.5 %shard_map.171 = (bf16[256,1024]{1,0:T(8,128)(2,1)S(1)}, bf16[256,1024]{1,0:T(8,128)(2,1)S(1)}, bf16[256,256]{1,0:T(8,128)(2,1)S(1)}, bf16[256,512]{1,0:T(8,128)...) custom-call(s32[11]{0:T(128)S(1)} %pad_add_fusion.meta, ...), custom_call_target="tpu_custom_call" | custom-call | flops 700000000 | bytes 7570476 | tf_op jit(solution)/shard_map/pallas_call | solution.py:250
  42.3 4.1 %shard_map.172 = (bf16[256,256]{1,0:T(8,128)(2,1)S(1)}, f32[128,1024]{1,0:T(8,128)S(1)}, bf16[128,1024]{1,0:T(8,128)(2,1)S(1)}) custom-call(s32[11]{0:T(128)S(1)} %pad_add_fusion.meta, bf16[256,256]{1,0:T(8,128)(2,1)S(1)} %get-tuple-element.95.query, bf16[256,512]{1,0:T(8,128)(2,1)S(1)} %get-tuple-element.96.kv, ...), custom_call_target="tpu_custom_call" | custom-call | flops 300000000 | bytes 2100268 | tf_op jit(solution)/shard_map/pallas_call | solution.py:250
  46.6 2.1 %collective-permute-start.19 = (bf16[128,1024]{1,0:T(8,128)(2,1)S(1)}, bf16[128,1024]{1,0:T(8,128)(2,1)S(1)}, u32[]{:S(2)}, u32[]{:S(2)}) collective-permute-start(bf16[128,1024]{1,0:T(8,128)(2,1)S(1)} %collective-permute-done.18.refs_7_), channel_id=1, source_target_pairs={{0,8},{8,16},{16,24},{24,28},{28,20},{20,12},{12,4},{4,0},{1,9},{9... | collective-permute-start | bytes 786440 | tf_op jit(solution)/shard_map/ppermute | solution.py:628
  48.7 2.5 %collective-permute-start.26 = (bf16[128,1024]{1,0:T(8,128)(2,1)S(1)}, bf16[128,1024]{1,0:T(8,128)(2,1)S(1)}, u32[]{:S(2)}, u32[]{:S(2)}) collective-permute-start(bf16[128,1024]{1,0:T(8,128)(2,1)S(1)} %collective-permute-done.25.refs_8_), channel_id=1, source_target_pairs={{0,8},{8,16},{16,24},{24,28},{28,20},{20,12},{12,4},{4,0},{1,9},{9... | collective-permute-start | bytes 786440 | tf_op jit(solution)/shard_map/ppermute | solution.py:628
  52.8 3.2 %collective-permute-done.15.refs_2_ = bf16[128,1024]{1,0:T(8,128)(2,1)S(1)} collective-permute-done((bf16[128,1024]{1,0:T(8,128)(2,1)}, bf16[128,1024]{1,0:T(8,128)(2,1)S(1)}, u32[]{:S(2)}, u32[]{:S(2)}) %collective-permute-start.15) | collective-permute-done | bytes 262176 | tf_op jit(solution)/shard_map/ppermute | solution.py:632
  56.0 4.9 %collective-permute-done.26.refs_7_ = bf16[128,1024]{1,0:T(8,128)(2,1)S(1)} collective-permute-done((bf16[128,1024]{1,0:T(8,128)(2,1)S(1)}, bf16[128,1024]{1,0:T(8,128)(2,1)S(1)}, u32[]{:S(2)}, u32[]{:S(2)}) %collective-permute-start.26) | collective-permute-done | bytes 262176 | tf_op jit(solution)/shard_map/ppermute | solution.py:628
  60.9 2.0 %collective-permute-start.27 = (bf16[128,1024]{1,0:T(8,128)(2,1)S(1)}, bf16[128,1024]{1,0:T(8,128)(2,1)S(1)}, u32[]{:S(2)}, u32[]{:S(2)}) collective-permute-start(bf16[128,1024]{1,0:T(8,128)(2,1)S(1)} %collective-permute-done.26.refs_7_), channel_id=1, source_target_pairs={{0,8},{8,16},{16,24},{24,28},{28,20},{20,12},{12,4},{4,0},{1,9},{9... | collective-permute-start | bytes 786440 | tf_op jit(solution)/shard_map/ppermute | solution.py:628
  63.9 3.3 %collective-permute-done.16.refs_3_ = bf16[128,1024]{1,0:T(8,128)(2,1)S(1)} collective-permute-done((bf16[128,1024]{1,0:T(8,128)(2,1)S(1)}, bf16[128,1024]{1,0:T(8,128)(2,1)S(1)}, u32[]{:S(2)}, u32[]{:S(2)}) %collective-permute-start.16) | collective-permute-done | bytes 262176 | tf_op jit(solution)/shard_map/ppermute | solution.py:632
  67.2 2.5 %collective-permute-start.20 = (bf16[64,1024]{1,0:T(8,128)(2,1)S(1)}, bf16[64,1024]{1,0:T(8,128)(2,1)S(1)}, u32[]{:S(2)}, u32[]{:S(2)}) collective-permute-start(bf16[64,1024]{1,0:T(8,128)(2,1)S(1)} %slice.42), channel_id=1, source_target_pairs={{0,8},{8,16},{16,24},{24,28},{28,20},{20,12},{12,4},{4,0},{1,9},{9... | collective-permute-start | bytes 393224 | tf_op jit(solution)/shard_map/ppermute | solution.py:628
  69.7 3.6 %collective-permute-start.21 = (bf16[64,1024]{1,0:T(8,128)(2,1)S(1)}, bf16[64,1024]{1,0:T(8,128)(2,1)S(1)}, u32[]{:S(2)}, u32[]{:S(2)}) collective-permute-start(bf16[64,1024]{1,0:T(8,128)(2,1)S(1)} %slice.43), channel_id=1, source_target_pairs={{0,4},{8,0},{16,8},{24,16},{28,24},{20,28},{12,20},{4,12},{1,5},{9... | collective-permute-start | bytes 393224 | tf_op jit(solution)/shard_map/ppermute | solution.py:632
  73.4 1.9 %collective-permute-start.28 = (bf16[64,1024]{1,0:T(8,128)(2,1)S(1)}, bf16[64,1024]{1,0:T(8,128)(2,1)S(1)}, u32[]{:S(2)}, u32[]{:S(2)}) collective-permute-start(bf16[64,1024]{1,0:T(8,128)(2,1)S(1)} %slice.44), channel_id=1, source_target_pairs={{0,8},{8,16},{16,24},{24,28},{28,20},{20,12},{12,4},{4,0},{1,9},{9... | collective-permute-start | bytes 393224 | tf_op jit(solution)/shard_map/ppermute | solution.py:628
  76.6 4.3 %shard_map.173 = (f32[256,1024]{1,0:T(8,128)S(1)}, bf16[256,1024]{1,0:T(8,128)(2,1)S(1)}, bf16[256,1024]{1,0:T(8,128)(2,1)S(1)}, bf16[256,1024]{1,0:T(8,128)(2,1...) custom-call(s32[11]{0:T(128)S(1)} %pad_add_fusion.meta, ...), custom_call_target="tpu_custom_call" | custom-call | flops 1100000000 | bytes 13140012 | tf_op jit(solution)/shard_map/pallas_call | solution.py:250
  80.9 3.8 %shard_map.174 = (bf16[256,1024]{1,0:T(8,128)(2,1)S(1)}, f32[128,1024]{1,0:T(8,128)S(1)}, bf16[128,1024]{1,0:T(8,128)(2,1)S(1)}, f32[8,1024]{1,0:T(8,128)S(1)}, bf16[1024,1024]{1,0:T(8,128)(2,1)S(1)}) custom-call(s32[11]{0:T(128)S(1)} %pad_add_fusion.meta, f32[256,1024]{1,0:T(8,128)S(1)} %get-tuple-element.103.residual, ...), custom_call_target="tpu_custom_call" | custom-call | flops 1100000000 | bytes 10256428 | tf_op jit(solution)/shard_map/pallas_call | solution.py:250
  88.0 6.8 %collective-permute-done.31.s1 = bf16[128,1024]{1,0:T(8,128)(2,1)S(1)} collective-permute-done((bf16[128,1024]{1,0:T(8,128)(2,1)S(1)}, bf16[128,1024]{1,0:T(8,128)(2,1)S(1)}, u32[]{:S(2)}, u32[]{:S(2)}) %collective-permute-start.31) | collective-permute-done | bytes 262176 | tf_op jit(solution)/shard_map/ppermute | solution.py:661
  99.6 1.8 collective-permute-done.61.ahead
  102.8 1.8 collective-permute-start.63
  104.8 5.6 %shard_map.176 = (f32[256,1024]{1,0:T(8,128)S(1)}, bf16[256,1024]{1,0:T(8,128)(2,1)S(1)}, f32[256,256]{1,0:T(8,128)S(1)}, f32[256,512]{1,0:T(8,128)S(1)}, bf16[256,512]{1,0:T(8,128)(2,1)S(1)}) custom-call(s32[11]{0:T(128)S(1)} %pad_add_fusion.meta, f32[256,1024]{1,0:T(8,128)S(1)} %bitcast.18, f32[256,1024]{1,0:T(8,128)S(1)} %get-tuple-element.103.residual, ...), custom_call_target="tpu_custom_call" | custom-call | flops 500000000 | bytes 7113772 | tf_op jit(solution)/shard_map/pallas_call | solution.py:250
  110.4 2.9 %shard_map.178 = (f32[256,1024]{1,0:T(8,128)S(1)}, bf16[528,256]{1,0:T(8,128)(2,1)S(1)}, bf16[528,256]{1,0:T(8,128)(2,1)S(1)}, bf16[528,256]{1,0:T(8,128)(2,1)S(...) custom-call(s32[11]{0:T(128)S(1)} %pad_add_fusion.meta, ...), custom_call_target="tpu_custom_call" | custom-call | flops 1100000000 | bytes 9142316 | tf_op jit(solution)/shard_map/pallas_call | solution.py:250
  113.3 1.8 collective-permute-start.43
  116.7 3.8 %collective-permute-done.54.behind = bf16[64,1024]{1,0:T(8,128)(2,1)S(1)} collective-permute-done((bf16[64,1024]{1,0:T(8,128)(2,1)S(1)}, bf16[64,1024]{1,0:T(8,128)(2,1)S(1)}, u32[]{:S(2)}, u32[]{:S(2)}) %collective-permute-start.54) | collective-permute-done | bytes 131104 | tf_op jit(solution)/shard_map/ppermute | solution.py:632
  121.1 1.7 collective-permute-start.55
  123.8 1.7 collective-permute-start.65
  126.6 1.7 collective-permute-start.45
  128.2 2.0 %collective-permute-done.55.ahead = bf16[128,1024]{1,0:T(8,128)(2,1)S(1)} collective-permute-done((bf16[128,1024]{1,0:T(8,128)(2,1)S(1)}, bf16[128,1024]{1,0:T(8,128)(2,1)S(1)}, u32[]{:S(2)}, u32[]{:S(2)}) %collective-permute-start.55) | collective-permute-done | bytes 262176 | tf_op jit(solution)/shard_map/ppermute | solution.py:628
  137.3 2.6 %collective-permute-start.46 = (bf16[528,256]{1,0:T(8,128)(2,1)S(1)}, bf16[528,256]{1,0:T(8,128)(2,1)S(1)}, u32[]{:S(2)}, u32[]{:S(2)}) collective-permute-start(bf16[528,256]{1,0:T(8,128)(2,1)S(1)} %get-tuple-element.139), channel_id=1, source_target_pairs={{0,4},{8,0},{16,8},{24,16},{28,24},{20,28},{12,20},{4,12},{1,5},{9... | collective-permute-start | bytes 811016 | tf_op jit(solution)/shard_map/ppermute | solution.py:632
  139.9 2.0 %shard_map.175 = (f32[128,1024]{1,0:T(8,128)S(1)}, bf16[128,1024]{1,0:T(8,128)(2,1)S(1)}) custom-call(s32[11]{0:T(128)S(1)} %pad_add_fusion.meta, bf16[256,1024]{1,0:T(8,128)(2,1)S(1)} %get-tuple-element.104.act, bf16[1024,1024]{1,0:T(8,128)(2,1)S(1)} %get-tuple-element.109.reduce), custom_call_target="tpu_custom_call" | custom-call | flops 550000000 | bytes 3407916 | tf_op jit(solution)/shard_map/pallas_call | solution.py:250
  142.6 2.3 %collective-permute-done.46.behind = bf16[528,256]{1,0:T(8,128)(2,1)S(1)} collective-permute-done((bf16[528,256]{1,0:T(8,128)(2,1)S(1)}, bf16[528,256]{1,0:T(8,128)(2,1)S(1)}, u32[]{:S(2)}, u32[]{:S(2)}) %collective-permute-start.46) | collective-permute-done | bytes 270368 | tf_op jit(solution)/shard_map/ppermute | solution.py:632
  145.7 1.6 collective-permute-start.47
  147.2 4.8 %collective-permute-done.38.kv_grad_in = bf16[256,512]{1,0:T(8,128)(2,1)S(1)} collective-permute-done((bf16[256,512]{1,0:T(8,128)(2,1)S(1)}, bf16[256,512]{1,0:T(8,128)(2,1)S(1)}, u32[]{:S(2)}, u32[]{:S(2)}) %collective-permute-start.38) | collective-permute-done | bytes 262176 | tf_op jit(solution)/shard_map/ppermute | solution.py:760
  153.1 2.1 %collective-permute-start.67 = (bf16[128,1024]{1,0:T(8,128)(2,1)S(1)}, bf16[128,1024]{1,0:T(8,128)(2,1)S(1)}, u32[]{:S(2)}, u32[]{:S(2)}) collective-permute-start(bf16[128,1024]{1,0:T(8,128)(2,1)S(1)} %get-tuple-element.177), channel_id=1, source_target_pairs={{0,8},{8,16},{16,24},{24,28},{28,20},{20,12},{12,4},{4,0},{1,9},{9... | collective-permute-start | bytes 786440 | tf_op jit(solution)/shard_map/ppermute | solution.py:628
  156.0 1.8 collective-permute-done.47.ahead
  165.0 1.6 collective-permute-start.40
  166.6 5.5 %collective-permute-done.49.ahead = bf16[528,256]{1,0:T(8,128)(2,1)S(1)} collective-permute-done((bf16[528,256]{1,0:T(8,128)(2,1)S(1)}, bf16[528,256]{1,0:T(8,128)(2,1)S(1)}, u32[]{:S(2)}, u32[]{:S(2)}) %collective-permute-start.49) | collective-permute-done | bytes 270368 | tf_op jit(solution)/shard_map/ppermute | solution.py:628
  176.0 1.7 collective-permute-start.52
  180.6 1.8 shard_map.177
  183.5 2.3 %shard_map.180 = f32[256,1024]{1,0:T(8,128)} custom-call(s32[11]{0:T(128)S(1)} %pad_add_fusion.meta, f32[256,1024]{1,0:T(8,128)S(1)} %bitcast.16, f32[256,1024]{1,0:T(8,128)S(1)} %get-tuple-element.118.residual_grad, f32[8,1024]{1,0:T(8,128)S(1)} %get-tuple-element.94.small, bf16[128,1024]{1,0:T(8,128)(2,1)S(1)} %add_convert_fusion.s0, ...), custom_call_target="tpu_custom_call" | custom-call | flops 5000000 | bytes 4227116 | tf_op jit(solution)/shard_map/pallas_call | solution.py:250
  (145 shorter events, 49.5 us)
Async XLA Ops:
  1.7 9.6 %collective-permute-start.2 = (bf16[528,256]{1,0:T(8,128)(2,1)S(1)}, bf16[528,256]{1,0:T(8,128)(2,1)S(1)}, u32[]{:S(2)}, u32[]{:S(2)}) collective-permute-start(bf16[528,256]{1,0:T(8,128)(2,1)S(1)} %shard_map.170.refs_0_), channel_id=1, source_target_pairs={{0,4},{8,0},{16,8},{24,16},{28,24},{20,28},{12,20},{4,12},{1,5},{9... | collective-permute-start | bytes 811016 | tf_op jit(solution)/shard_map/ppermute | solution.py:632
  15.4 10.3 %collective-permute-start = (bf16[128,1024]{1,0:T(8,128)(2,1)S(1)}, bf16[128,1024]{1,0:T(8,128)(2,1)S(1)}, u32[]{:S(2)}, u32[]{:S(2)}) collective-permute-start(bf16[128,1024]{1,0:T(8,128)(2,1)S(1)} %shard_map.169), channel_id=1, source_target_pairs={{0,4},{1,5},{2,6},{3,7},{8,12},{9,13},{10,14},{11,15},{16,20},{17,... | collective-permute-start | bytes 786440 | tf_op jit(solution)/shard_map/ppermute | solution.py:701
  19.0 10.2 %collective-permute-start.4 = (bf16[528,256]{1,0:T(8,128)(2,1)S(1)}, bf16[528,256]{1,0:T(8,128)(2,1)S(1)}, u32[]{:S(2)}, u32[]{:S(2)}) collective-permute-start(bf16[528,256]{1,0:T(8,128)(2,1)S(1)} %collective-permute-done.3.refs_2_), channel_id=1, source_target_pairs={{0,4},{8,0},{16,8},{24,16},{28,24},{20,28},{12,20},{4,12},{1,5},{9... | collective-permute-start | bytes 811016 | tf_op jit(solution)/shard_map/ppermute | solution.py:632
  20.6 11.8 %collective-permute-start.7 = (bf16[528,256]{1,0:T(8,128)(2,1)S(1)}, bf16[528,256]{1,0:T(8,128)(2,1)S(1)}, u32[]{:S(2)}, u32[]{:S(2)}) collective-permute-start(bf16[528,256]{1,0:T(8,128)(2,1)S(1)} %collective-permute-done.6.refs_7_), channel_id=1, source_target_pairs={{0,8},{8,16},{16,24},{24,28},{28,20},{20,12},{12,4},{4,0},{1,9},{9... | collective-permute-start | bytes 811016 | tf_op jit(solution)/shard_map/ppermute | solution.py:628
  21.1 14.1 %collective-permute-start.17 = (bf16[128,1024]{1,0:T(8,128)(2,1)}, bf16[128,1024]{1,0:T(8,128)(2,1)}, u32[]{:S(2)}, u32[]{:S(2)}) collective-permute-start(bf16[128,1024]{1,0:T(8,128)(2,1)} %refs_0_), channel_id=1, source_target_pairs={{0,8},{8,16},{16,24},{24,28},{28,20},{20,12},{12,4},{4,0},{1,9},{9... | collective-permute-start | bytes 786440 | tf_op jit(solution)/shard_map/ppermute | solution.py:628
  25.7 9.6 %collective-permute-start.1 = (bf16[128,1024]{1,0:T(8,128)(2,1)S(1)}, bf16[128,1024]{1,0:T(8,128)(2,1)S(1)}, u32[]{:S(2)}, u32[]{:S(2)}) collective-permute-start(bf16[128,1024]{1,0:T(8,128)(2,1)S(1)} %collective-permute-done.far_a), channel_id=1, source_target_pairs={{0,1},{1,0},{2,3},{3,2},{4,5},{5,4},{6,7},{7,6},{8,9},{9,8},{10,11... | collective-permute-start | bytes 786440 | tf_op jit(solution)/shard_map/ppermute | solution.py:702
  33.1 13.5 %collective-permute-start.14 = (bf16[128,1024]{1,0:T(8,128)(2,1)}, bf16[128,1024]{1,0:T(8,128)(2,1)}, u32[]{:S(2)}, u32[]{:S(2)}) collective-permute-start(bf16[128,1024]{1,0:T(8,128)(2,1)} %refs_0_), channel_id=1, source_target_pairs={{0,4},{8,0},{16,8},{24,16},{28,24},{20,28},{12,20},{4,12},{1,5},{9... | collective-permute-start | bytes 786440 | tf_op jit(solution)/shard_map/ppermute | solution.py:632
  35.2 11.4 %collective-permute-start.18 = (bf16[128,1024]{1,0:T(8,128)(2,1)}, bf16[128,1024]{1,0:T(8,128)(2,1)S(1)}, u32[]{:S(2)}, u32[]{:S(2)}) collective-permute-start(bf16[128,1024]{1,0:T(8,128)(2,1)} %collective-permute-done.17.refs_8_), channel_id=1, source_target_pairs={{0,8},{8,16},{16,24},{24,28},{28,20},{20,12},{12,4},{4,0},{1,9},{9... | collective-permute-start | bytes 786440 | tf_op jit(solution)/shard_map/ppermute | solution.py:628
  35.3 13.4 %collective-permute-start.25 = (bf16[128,1024]{1,0:T(8,128)(2,1)}, bf16[128,1024]{1,0:T(8,128)(2,1)S(1)}, u32[]{:S(2)}, u32[]{:S(2)}) collective-permute-start(bf16[128,1024]{1,0:T(8,128)(2,1)} %refs_0_.1), channel_id=1, source_target_pairs={{0,8},{8,16},{16,24},{24,28},{28,20},{20,12},{12,4},{4,0},{1,9},{9... | collective-permute-start | bytes 786440 | tf_op jit(solution)/shard_map/ppermute | solution.py:628
  37.0 14.1 %collective-permute-start.22 = (bf16[128,1024]{1,0:T(8,128)(2,1)}, bf16[128,1024]{1,0:T(8,128)(2,1)S(1)}, u32[]{:S(2)}, u32[]{:S(2)}) collective-permute-start(bf16[128,1024]{1,0:T(8,128)(2,1)} %refs_0_.1), channel_id=1, source_target_pairs={{0,4},{8,0},{16,8},{24,16},{28,24},{20,28},{12,20},{4,12},{1,5},{9... | collective-permute-start | bytes 786440 | tf_op jit(solution)/shard_map/ppermute | solution.py:632
  46.5 9.4 %collective-permute-start.15 = (bf16[128,1024]{1,0:T(8,128)(2,1)}, bf16[128,1024]{1,0:T(8,128)(2,1)S(1)}, u32[]{:S(2)}, u32[]{:S(2)}) collective-permute-start(bf16[128,1024]{1,0:T(8,128)(2,1)} %collective-permute-done.14.refs_1_), channel_id=1, source_target_pairs={{0,4},{8,0},{16,8},{24,16},{28,24},{20,28},{12,20},{4,12},{1,5},{9... | collective-permute-start | bytes 786440 | tf_op jit(solution)/shard_map/ppermute | solution.py:632
  46.6 16.8 %collective-permute-start.19 = (bf16[128,1024]{1,0:T(8,128)(2,1)S(1)}, bf16[128,1024]{1,0:T(8,128)(2,1)S(1)}, u32[]{:S(2)}, u32[]{:S(2)}) collective-permute-start(bf16[128,1024]{1,0:T(8,128)(2,1)S(1)} %collective-permute-done.18.refs_7_), channel_id=1, source_target_pairs={{0,8},{8,16},{16,24},{24,28},{28,20},{20,12},{12,4},{4,0},{1,9},{9... | collective-permute-start | bytes 786440 | tf_op jit(solution)/shard_map/ppermute | solution.py:628
  48.7 12.2 %collective-permute-start.26 = (bf16[128,1024]{1,0:T(8,128)(2,1)S(1)}, bf16[128,1024]{1,0:T(8,128)(2,1)S(1)}, u32[]{:S(2)}, u32[]{:S(2)}) collective-permute-start(bf16[128,1024]{1,0:T(8,128)(2,1)S(1)} %collective-permute-done.25.refs_8_), channel_id=1, source_target_pairs={{0,8},{8,16},{16,24},{24,28},{28,20},{20,12},{12,4},{4,0},{1,9},{9... | collective-permute-start | bytes 786440 | tf_op jit(solution)/shard_map/ppermute | solution.py:628
  51.2 11.8 %collective-permute-start.23 = (bf16[128,1024]{1,0:T(8,128)(2,1)S(1)}, bf16[128,1024]{1,0:T(8,128)(2,1)S(1)}, u32[]{:S(2)}, u32[]{:S(2)}) collective-permute-start(bf16[128,1024]{1,0:T(8,128)(2,1)S(1)} %collective-permute-done.22.refs_1_), channel_id=1, source_target_pairs={{0,4},{8,0},{16,8},{24,16},{28,24},{20,28},{12,20},{4,12},{1,5},{9... | collective-permute-start | bytes 786440 | tf_op jit(solution)/shard_map/ppermute | solution.py:632
  51.2 12.2 %collective-permute-start.11 = (bf16[128,1024]{1,0:T(8,128)(2,1)S(1)}, bf16[128,1024]{1,0:T(8,128)(2,1)S(1)}, u32[]{:S(2)}, u32[]{:S(2)}) collective-permute-start(bf16[128,1024]{1,0:T(8,128)(2,1)S(1)} %add_convert_fusion.3.s0), channel_id=1, source_target_pairs={{0,2},{2,0},{1,3},{3,1},{4,6},{6,4},{5,7},{7,5},{8,10},{10,8},{9,1... | collective-permute-start | bytes 786440 | tf_op jit(solution)/shard_map/ppermute | solution.py:661
  56.0 11.2 %collective-permute-start.16 = (bf16[128,1024]{1,0:T(8,128)(2,1)S(1)}, bf16[128,1024]{1,0:T(8,128)(2,1)S(1)}, u32[]{:S(2)}, u32[]{:S(2)}) collective-permute-start(bf16[128,1024]{1,0:T(8,128)(2,1)S(1)} %collective-permute-done.15.refs_2_), channel_id=1, source_target_pairs={{0,4},{8,0},{16,8},{24,16},{28,24},{20,28},{12,20},{4,12},{1,5},{9... | collective-permute-start | bytes 786440 | tf_op jit(solution)/shard_map/ppermute | solution.py:632
  60.9 8.8 %collective-permute-start.27 = (bf16[128,1024]{1,0:T(8,128)(2,1)S(1)}, bf16[128,1024]{1,0:T(8,128)(2,1)S(1)}, u32[]{:S(2)}, u32[]{:S(2)}) collective-permute-start(bf16[128,1024]{1,0:T(8,128)(2,1)S(1)} %collective-permute-done.26.refs_7_), channel_id=1, source_target_pairs={{0,8},{8,16},{16,24},{24,28},{28,20},{20,12},{12,4},{4,0},{1,9},{9... | collective-permute-start | bytes 786440 | tf_op jit(solution)/shard_map/ppermute | solution.py:628
  62.9 10.4 %collective-permute-start.24 = (bf16[128,1024]{1,0:T(8,128)(2,1)S(1)}, bf16[128,1024]{1,0:T(8,128)(2,1)S(1)}, u32[]{:S(2)}, u32[]{:S(2)}) collective-permute-start(bf16[128,1024]{1,0:T(8,128)(2,1)S(1)} %collective-permute-done.23.refs_2_), channel_id=1, source_target_pairs={{0,4},{8,0},{16,8},{24,16},{28,24},{20,28},{12,20},{4,12},{1,5},{9... | collective-permute-start | bytes 786440 | tf_op jit(solution)/shard_map/ppermute | solution.py:632
  63.4 13.2 %collective-permute-start.12 = (bf16[128,1024]{1,0:T(8,128)(2,1)S(1)}, bf16[128,1024]{1,0:T(8,128)(2,1)S(1)}, u32[]{:S(2)}, u32[]{:S(2)}) collective-permute-start(bf16[128,1024]{1,0:T(8,128)(2,1)S(1)} %add_convert_fusion.3.s0), channel_id=1, source_target_pairs={{0,1},{1,0},{2,3},{3,2},{4,5},{5,4},{6,7},{7,6},{8,9},{9,8},{10,11... | collective-permute-start | bytes 786440 | tf_op jit(solution)/shard_map/ppermute | solution.py:661
  63.4 13.2 %collective-permute-start.13 = (bf16[128,1024]{1,0:T(8,128)(2,1)S(1)}, bf16[128,1024]{1,0:T(8,128)(2,1)S(1)}, u32[]{:S(2)}, u32[]{:S(2)}) collective-permute-start(bf16[128,1024]{1,0:T(8,128)(2,1)S(1)} %collective-permute-done.11.s1), channel_id=1, source_target_pairs={{0,1},{1,0},{2,3},{3,2},{4,5},{5,4},{6,7},{7,6},{8,9},{9,8},{10,11... | collective-permute-start | bytes 786440 | tf_op jit(solution)/shard_map/ppermute | solution.py:661
  86.4 8.4 %collective-permute-start.31 = (bf16[128,1024]{1,0:T(8,128)(2,1)S(1)}, bf16[128,1024]{1,0:T(8,128)(2,1)S(1)}, u32[]{:S(2)}, u32[]{:S(2)}) collective-permute-start(bf16[128,1024]{1,0:T(8,128)(2,1)S(1)} %add_convert_fusion.2.s0), channel_id=1, source_target_pairs={{0,2},{2,0},{1,3},{3,1},{4,6},{6,4},{5,7},{7,5},{8,10},{10,8},{9,1... | collective-permute-start | bytes 786440 | tf_op jit(solution)/shard_map/ppermute | solution.py:661
  88.0 16.8 %collective-permute-start.32 = (bf16[128,1024]{1,0:T(8,128)(2,1)S(1)}, bf16[128,1024]{1,0:T(8,128)(2,1)S(1)}, u32[]{:S(2)}, u32[]{:S(2)}) collective-permute-start(bf16[128,1024]{1,0:T(8,128)(2,1)S(1)} %add_convert_fusion.2.s0), channel_id=1, source_target_pairs={{0,1},{1,0},{2,3},{3,2},{4,5},{5,4},{6,7},{7,6},{8,9},{9,8},{10,11... | collective-permute-start | bytes 786440 | tf_op jit(solution)/shard_map/ppermute | solution.py:661
  94.8 10.0 %collective-permute-start.33 = (bf16[128,1024]{1,0:T(8,128)(2,1)S(1)}, bf16[128,1024]{1,0:T(8,128)(2,1)S(1)}, u32[]{:S(2)}, u32[]{:S(2)}) collective-permute-start(bf16[128,1024]{1,0:T(8,128)(2,1)S(1)} %collective-permute-done.31.s1), channel_id=1, source_target_pairs={{0,1},{1,0},{2,3},{3,2},{4,5},{5,4},{6,7},{7,6},{8,9},{9,8},{10,11... | collective-permute-start | bytes 786440 | tf_op jit(solution)/shard_map/ppermute | solution.py:661
  98.6 16.7 %collective-permute-start.53 = (bf16[64,1024]{1,0:T(8,128)(2,1)S(1)}, bf16[64,1024]{1,0:T(8,128)(2,1)S(1)}, u32[]{:S(2)}, u32[]{:S(2)}) collective-permute-start(bf16[64,1024]{1,0:T(8,128)(2,1)S(1)} %get-tuple-element.156), channel_id=1, source_target_pairs={{0,8},{8,16},{16,24},{24,28},{28,20},{20,12},{12,4},{4,0},{1,9},{9... | collective-permute-start | bytes 393224 | tf_op jit(solution)/shard_map/ppermute | solution.py:628
  102.8 20.0 %collective-permute-start.63 = (bf16[128,1024]{1,0:T(8,128)(2,1)S(1)}, bf16[128,1024]{1,0:T(8,128)(2,1)S(1)}, u32[]{:S(2)}, u32[]{:S(2)}) collective-permute-start(bf16[128,1024]{1,0:T(8,128)(2,1)S(1)} %get-tuple-element.173), channel_id=1, source_target_pairs={{0,8},{8,16},{16,24},{24,28},{28,20},{20,12},{12,4},{4,0},{1,9},{9... | collective-permute-start | bytes 786440 | tf_op jit(solution)/shard_map/ppermute | solution.py:628
  104.5 18.6 %collective-permute-start.64 = (bf16[128,1024]{1,0:T(8,128)(2,1)S(1)}, bf16[128,1024]{1,0:T(8,128)(2,1)S(1)}, u32[]{:S(2)}, u32[]{:S(2)}) collective-permute-start(bf16[128,1024]{1,0:T(8,128)(2,1)S(1)} %get-tuple-element.174), channel_id=1, source_target_pairs={{0,4},{8,0},{16,8},{24,16},{28,24},{20,28},{12,20},{4,12},{1,5},{9... | collective-permute-start | bytes 786440 | tf_op jit(solution)/shard_map/ppermute | solution.py:632
  113.3 12.2 %collective-permute-start.43 = (bf16[528,128]{1,0:T(8,128)(2,1)S(1)}, bf16[528,128]{1,0:T(8,128)(2,1)S(1)}, u32[]{:S(2)}, u32[]{:S(2)}) collective-permute-start(bf16[528,128]{1,0:T(8,128)(2,1)S(1)} %get-tuple-element.136), channel_id=1, source_target_pairs={{0,8},{8,16},{16,24},{24,28},{28,20},{20,12},{12,4},{4,0},{1,9},{9... | collective-permute-start | bytes 405512 | tf_op jit(solution)/shard_map/ppermute | solution.py:628
  115.4 10.5 %collective-permute-start.44 = (bf16[528,128]{1,0:T(8,128)(2,1)S(1)}, bf16[528,128]{1,0:T(8,128)(2,1)S(1)}, u32[]{:S(2)}, u32[]{:S(2)}) collective-permute-start(bf16[528,128]{1,0:T(8,128)(2,1)S(1)} %get-tuple-element.137), channel_id=1, source_target_pairs={{0,4},{8,0},{16,8},{24,16},{28,24},{20,28},{12,20},{4,12},{1,5},{9... | collective-permute-start | bytes 405512 | tf_op jit(solution)/shard_map/ppermute | solution.py:632
  121.1 9.2 %collective-permute-start.55 = (bf16[128,1024]{1,0:T(8,128)(2,1)S(1)}, bf16[128,1024]{1,0:T(8,128)(2,1)S(1)}, u32[]{:S(2)}, u32[]{:S(2)}) collective-permute-start(bf16[128,1024]{1,0:T(8,128)(2,1)S(1)} %get-tuple-element.158), channel_id=1, source_target_pairs={{0,8},{8,16},{16,24},{24,28},{28,20},{20,12},{12,4},{4,0},{1,9},{9... | collective-permute-start | bytes 786440 | tf_op jit(solution)/shard_map/ppermute | solution.py:628
  122.8 8.9 %collective-permute-start.56 = (bf16[128,1024]{1,0:T(8,128)(2,1)S(1)}, bf16[128,1024]{1,0:T(8,128)(2,1)S(1)}, u32[]{:S(2)}, u32[]{:S(2)}) collective-permute-start(bf16[128,1024]{1,0:T(8,128)(2,1)S(1)} %get-tuple-element.159), channel_id=1, source_target_pairs={{0,4},{8,0},{16,8},{24,16},{28,24},{20,28},{12,20},{4,12},{1,5},{9... | collective-permute-start | bytes 786440 | tf_op jit(solution)/shard_map/ppermute | solution.py:632
  123.8 12.1 %collective-permute-start.65 = (bf16[128,1024]{1,0:T(8,128)(2,1)S(1)}, bf16[128,1024]{1,0:T(8,128)(2,1)S(1)}, u32[]{:S(2)}, u32[]{:S(2)}) collective-permute-start(bf16[128,1024]{1,0:T(8,128)(2,1)S(1)} %get-tuple-element.175), channel_id=1, source_target_pairs={{0,8},{8,16},{16,24},{24,28},{28,20},{20,12},{12,4},{4,0},{1,9},{9... | collective-permute-start | bytes 786440 | tf_op jit(solution)/shard_map/ppermute | solution.py:628
  125.5 11.8 %collective-permute-start.66 = (bf16[128,1024]{1,0:T(8,128)(2,1)S(1)}, bf16[128,1024]{1,0:T(8,128)(2,1)S(1)}, u32[]{:S(2)}, u32[]{:S(2)}) collective-permute-start(bf16[128,1024]{1,0:T(8,128)(2,1)S(1)} %get-tuple-element.176), channel_id=1, source_target_pairs={{0,4},{8,0},{16,8},{24,16},{28,24},{20,28},{12,20},{4,12},{1,5},{9... | collective-permute-start | bytes 786440 | tf_op jit(solution)/shard_map/ppermute | solution.py:632
  126.6 15.3 %collective-permute-start.45 = (bf16[528,256]{1,0:T(8,128)(2,1)S(1)}, bf16[528,256]{1,0:T(8,128)(2,1)S(1)}, u32[]{:S(2)}, u32[]{:S(2)}) collective-permute-start(bf16[528,256]{1,0:T(8,128)(2,1)S(1)} %get-tuple-element.138), channel_id=1, source_target_pairs={{0,8},{8,16},{16,24},{24,28},{28,20},{20,12},{12,4},{4,0},{1,9},{9... | collective-permute-start | bytes 811016 | tf_op jit(solution)/shard_map/ppermute | solution.py:628
  132.4 20.7 %collective-permute-start.57 = (bf16[128,1024]{1,0:T(8,128)(2,1)S(1)}, bf16[128,1024]{1,0:T(8,128)(2,1)S(1)}, u32[]{:S(2)}, u32[]{:S(2)}) collective-permute-start(bf16[128,1024]{1,0:T(8,128)(2,1)S(1)} %get-tuple-element.160), channel_id=1, source_target_pairs={{0,8},{8,16},{16,24},{24,28},{28,20},{20,12},{12,4},{4,0},{1,9},{9... | collective-permute-start | bytes 786440 | tf_op jit(solution)/shard_map/ppermute | solution.py:628
  133.8 21.4 %collective-permute-start.58 = (bf16[128,1024]{1,0:T(8,128)(2,1)S(1)}, bf16[128,1024]{1,0:T(8,128)(2,1)S(1)}, u32[]{:S(2)}, u32[]{:S(2)}) collective-permute-start(bf16[128,1024]{1,0:T(8,128)(2,1)S(1)} %get-tuple-element.161), channel_id=1, source_target_pairs={{0,4},{8,0},{16,8},{24,16},{28,24},{20,28},{12,20},{4,12},{1,5},{9... | collective-permute-start | bytes 786440 | tf_op jit(solution)/shard_map/ppermute | solution.py:632
  135.9 16.1 %collective-permute-start.38 = (bf16[256,512]{1,0:T(8,128)(2,1)S(1)}, bf16[256,512]{1,0:T(8,128)(2,1)S(1)}, u32[]{:S(2)}, u32[]{:S(2)}) collective-permute-start(bf16[256,512]{1,0:T(8,128)(2,1)S(1)} %get-tuple-element.122.kv_grad_far), channel_id=1, source_target_pairs={{4,0},{5,1},{6,2},{7,3},{12,8},{13,9},{14,10},{15,11},{20,16},{21,... | collective-permute-start | bytes 786440 | tf_op jit(solution)/shard_map/ppermute | solution.py:760
  141.9 14.0 %collective-permute-start.34 = (bf16[128,1024]{1,0:T(8,128)(2,1)S(1)}, bf16[128,1024]{1,0:T(8,128)(2,1)S(1)}, u32[]{:S(2)}, u32[]{:S(2)}) collective-permute-start(bf16[128,1024]{1,0:T(8,128)(2,1)S(1)} %get-tuple-element.117), channel_id=1, source_target_pairs={{0,1},{1,0},{2,3},{3,2},{4,5},{5,4},{6,7},{7,6},{8,9},{9,8},{10,11... | collective-permute-start | bytes 786440 | tf_op jit(solution)/shard_map/ppermute | solution.py:661
  145.7 12.1 %collective-permute-start.47 = (bf16[528,256]{1,0:T(8,128)(2,1)S(1)}, bf16[528,256]{1,0:T(8,128)(2,1)S(1)}, u32[]{:S(2)}, u32[]{:S(2)}) collective-permute-start(bf16[528,256]{1,0:T(8,128)(2,1)S(1)} %get-tuple-element.140), channel_id=1, source_target_pairs={{0,8},{8,16},{16,24},{24,28},{28,20},{20,12},{12,4},{4,0},{1,9},{9... | collective-permute-start | bytes 811016 | tf_op jit(solution)/shard_map/ppermute | solution.py:628
  153.1 9.1 %collective-permute-start.67 = (bf16[128,1024]{1,0:T(8,128)(2,1)S(1)}, bf16[128,1024]{1,0:T(8,128)(2,1)S(1)}, u32[]{:S(2)}, u32[]{:S(2)}) collective-permute-start(bf16[128,1024]{1,0:T(8,128)(2,1)S(1)} %get-tuple-element.177), channel_id=1, source_target_pairs={{0,8},{8,16},{16,24},{24,28},{28,20},{20,12},{12,4},{4,0},{1,9},{9... | collective-permute-start | bytes 786440 | tf_op jit(solution)/shard_map/ppermute | solution.py:628
  155.9 9.1 %collective-permute-start.68 = (bf16[128,1024]{1,0:T(8,128)(2,1)S(1)}, bf16[128,1024]{1,0:T(8,128)(2,1)S(1)}, u32[]{:S(2)}, u32[]{:S(2)}) collective-permute-start(bf16[128,1024]{1,0:T(8,128)(2,1)S(1)} %get-tuple-element.178), channel_id=1, source_target_pairs={{0,4},{8,0},{16,8},{24,16},{28,24},{20,28},{12,20},{4,12},{1,5},{9... | collective-permute-start | bytes 786440 | tf_op jit(solution)/shard_map/ppermute | solution.py:632
  157.8 16.2 %collective-permute-start.59 = (bf16[128,1024]{1,0:T(8,128)(2,1)S(1)}, bf16[128,1024]{1,0:T(8,128)(2,1)S(1)}, u32[]{:S(2)}, u32[]{:S(2)}) collective-permute-start(bf16[128,1024]{1,0:T(8,128)(2,1)S(1)} %get-tuple-element.162), channel_id=1, source_target_pairs={{0,8},{8,16},{16,24},{24,28},{28,20},{20,12},{12,4},{4,0},{1,9},{9... | collective-permute-start | bytes 786440 | tf_op jit(solution)/shard_map/ppermute | solution.py:628
  162.1 9.9 %collective-permute-start.49 = (bf16[528,256]{1,0:T(8,128)(2,1)S(1)}, bf16[528,256]{1,0:T(8,128)(2,1)S(1)}, u32[]{:S(2)}, u32[]{:S(2)}) collective-permute-start(bf16[528,256]{1,0:T(8,128)(2,1)S(1)} %get-tuple-element.142), channel_id=1, source_target_pairs={{0,8},{8,16},{16,24},{24,28},{28,20},{20,12},{12,4},{4,0},{1,9},{9... | collective-permute-start | bytes 811016 | tf_op jit(solution)/shard_map/ppermute | solution.py:628
  163.4 8.8 %collective-permute-start.50 = (bf16[528,256]{1,0:T(8,128)(2,1)S(1)}, bf16[528,256]{1,0:T(8,128)(2,1)S(1)}, u32[]{:S(2)}, u32[]{:S(2)}) collective-permute-start(bf16[528,256]{1,0:T(8,128)(2,1)S(1)} %get-tuple-element.143), channel_id=1, source_target_pairs={{0,4},{8,0},{16,8},{24,16},{28,24},{20,28},{12,20},{4,12},{1,5},{9... | collective-permute-start | bytes 811016 | tf_op jit(solution)/shard_map/ppermute | solution.py:632
  165.0 9.2 %collective-permute-start.40 = (bf16[128,1024]{1,0:T(8,128)(2,1)S(1)}, bf16[128,1024]{1,0:T(8,128)(2,1)S(1)}, u32[]{:S(2)}, u32[]{:S(2)}) collective-permute-start(bf16[128,1024]{1,0:T(8,128)(2,1)S(1)} %add_convert_fusion.s0), channel_id=1, source_target_pairs={{0,2},{2,0},{1,3},{3,1},{4,6},{6,4},{5,7},{7,5},{8,10},{10,8},{9,1... | collective-permute-start | bytes 786440 | tf_op jit(solution)/shard_map/ppermute | solution.py:661
  166.6 9.5 %collective-permute-start.60 = (bf16[128,1024]{1,0:T(8,128)(2,1)S(1)}, bf16[128,1024]{1,0:T(8,128)(2,1)S(1)}, u32[]{:S(2)}, u32[]{:S(2)}) collective-permute-start(bf16[128,1024]{1,0:T(8,128)(2,1)S(1)} %get-tuple-element.163), channel_id=1, source_target_pairs={{0,4},{8,0},{16,8},{24,16},{28,24},{20,28},{12,20},{4,12},{1,5},{9... | collective-permute-start | bytes 786440 | tf_op jit(solution)/shard_map/ppermute | solution.py:632
  172.1 8.5 %collective-permute-start.36 = (bf16[128,1024]{1,0:T(8,128)(2,1)S(1)}, bf16[128,1024]{1,0:T(8,128)(2,1)S(1)}, u32[]{:S(2)}, u32[]{:S(2)}) collective-permute-start(bf16[128,1024]{1,0:T(8,128)(2,1)S(1)} %add_convert_fusion.1.s0), channel_id=1, source_target_pairs={{0,1},{1,0},{2,3},{3,2},{4,5},{5,4},{6,7},{7,6},{8,9},{9,8},{10,11... | collective-permute-start | bytes 786440 | tf_op jit(solution)/shard_map/ppermute | solution.py:661
  172.2 8.4 %collective-permute-start.37 = (bf16[128,1024]{1,0:T(8,128)(2,1)S(1)}, bf16[128,1024]{1,0:T(8,128)(2,1)S(1)}, u32[]{:S(2)}, u32[]{:S(2)}) collective-permute-start(bf16[128,1024]{1,0:T(8,128)(2,1)S(1)} %collective-permute-done.35.s1), channel_id=1, source_target_pairs={{0,1},{1,0},{2,3},{3,2},{4,5},{5,4},{6,7},{7,6},{8,9},{9,8},{10,11... | collective-permute-start | bytes 786440 | tf_op jit(solution)/shard_map/ppermute | solution.py:661
  174.1 9.3 %collective-permute-start.41 = (bf16[128,1024]{1,0:T(8,128)(2,1)S(1)}, bf16[128,1024]{1,0:T(8,128)(2,1)S(1)}, u32[]{:S(2)}, u32[]{:S(2)}) collective-permute-start(bf16[128,1024]{1,0:T(8,128)(2,1)S(1)} %add_convert_fusion.s0), channel_id=1, source_target_pairs={{0,1},{1,0},{2,3},{3,2},{4,5},{5,4},{6,7},{7,6},{8,9},{9,8},{10,11... | collective-permute-start | bytes 786440 | tf_op jit(solution)/shard_map/ppermute | solution.py:661
  (27 other events, 270.5 us)

commit v2 on v1

--- a/solution.py
+++ b/solution.py
@@ -603,7 +603,7 @@
     out[...] = own[...].astype(f32) + (ahead[...].astype(f32) + behind[...].astype(f32))
 
 
-def last_pack_kernel(meta, own, ahead, behind, attend, merge, tail):
+def last_pack_kernel(meta, own, ahead, behind, attend, merge, norms, bias):
     def total(start, size):
         r = slice(start, start + size)
         return own[r, :].astype(f32) + (ahead[r, :].astype(f32) + behind[r, :].astype(f32))
@@ -611,7 +611,9 @@
     for t in range(3):
         attend[t] = total(t * 128, 128)
     merge[...] = total(384, 128)
-    tail[...] = total(512, 16)
+    tail = total(512, 16)
+    norms[...] = tail[0:2, :]
+    bias[...] = tail[2:3, :128]
 
 
 def block_out_kernel(meta, residual, s0, s1, s2, s3, out, part):
@@ -766,9 +768,10 @@
          resid_half, attended, attend, grads], 1_100_000_000,
         [pltpu.VMEM((256, 768), bf16), pltpu.VMEM((8, 1024), f32), part],
     )
-    attend_grad, merge_grad, tail = sum_blocks(
+    attend_grad, merge_grad, norms, bias_grad = sum_blocks(
         meta, pack_parts, first_columns_kernel, last_pack_kernel,
-        [shape((3, 128, 256), f32), shape((128, 256), f32), shape((16, 256), f32)],
+        [shape((3, 128, 256), f32), shape((128, 256), f32), shape((2, 256), f32),
+         shape((1, 128), f32)],
     )
     early_keep, early_give = call(
         project_back_kernel, [shape(half, f32), shape(half, bf16)],
@@ -784,7 +787,6 @@
         input_grad_kernel, [shape(rows, f32)],
         [meta, x, residual_grad, small, *early_sums], 5_000_000, [part],
     )
-    norms = tail[:2]
     norms = norms + lax.ppermute(norms, TP, NEAR)
     norms = norms + lax.ppermute(norms, TP, FAR)
     return (
@@ -795,13 +797,13 @@
         jnp.swapaxes(attend_grad, 0, 1),
         merge_grad,
         expand_grad,
-        tail[2:3, :128],
+        bias_grad,
         reduce_grad,
     )
 
 
 EXPAND_AFTER = 0
-REDUCE_AFTER = 2
+REDUCE_AFTER = 1
 
 
 def fits(mesh_sizes, *args):

time: 186 us -> 186 us (level)
  transfers between devices with their start and end apart: 69 -> 69, of which waited for: 27 -> 27; matrix products, arithmetic and copies ran while one was open for 2% -> 1% of each run, Pallas kernels for 20% -> 20%
where the time goes in v2:
time: 186 us; the launch traced here: 185 us
  starting transfers between devices  72.6 us (39%)
  waiting for transfers between devices  64.5 us (35%)
  Pallas kernels  43.4 us (23%)
  local copies, waits for them, and re-layouts  3.31 us (2%)
    pallas_call x24, Pallas kernels, call(): pl.pallas_call(kernel, out_shape=tuple(outs), in_specs=[SMEM] + [VMEM] *...  42.4 us
    ppermute x24, starting transfers between devices, send_ahead(): return lax.ppermute(value, AXES, AHEAD)  33 us
    ppermute x24, waiting for transfers between devices, send_behind(): return lax.ppermute(value, AXES, BEHIND)  27.9 us
    ppermute x24, starting transfers between devices, send_behind(): return lax.ppermute(value, AXES, BEHIND)  25.1 us
    ppermute x24, waiting for transfers between devices, send_ahead(): return lax.ppermute(value, AXES, AHEAD)  19.8 us
    ppermute x16, waiting for transfers between devices, tp_send(): return lambda value: lax.ppermute(value, TP, pairs)  8.4 us
    ppermute x16, starting transfers between devices, tp_send(): return lambda value: lax.ppermute(value, TP, pairs)  7.83 us
    ppermute x1, waiting for transfers between devices, fast_shards(): kv_grad_in = lax.ppermute(kv_grad_far, CTX, [(1, 0)])  4.77 us
  transfers between devices with their start and end apart: 69, of which 27 were waited for; matrix products, arithmetic and copies ran while one was open for 1% of the time, Pallas kernels for 20%

profile of v2, /device:TPU:0, one launch (start us, length us, event | category | flops | bytes accessed | tf_op | source)
XLA Modules:
  0.0 185.3 jit_solution(18033413139984884202)
XLA Ops:
  1.7 3.0 %collective-permute-start.2 = (bf16[528,256]{1,0:T(8,128)(2,1)S(1)}, bf16[528,256]{1,0:T(8,128)(2,1)S(1)}, u32[]{:S(2)}, u32[]{:S(2)}) collective-permute-start(bf16[528,256]{1,0:T(8,128)(2,1)S(1)} %shard_map.170.refs_0_), channel_id=1, source_target_pairs={{0,4},{8,0},{16,8},{24,16},{28,24},{20,28},{12,20},{4,12},{1,5},{9... | collective-permute-start | bytes 811016 | tf_op jit(solution)/shard_map/ppermute | solution.py:634
  4.8 6.4 %collective-permute-done.2.refs_1_ = bf16[528,256]{1,0:T(8,128)(2,1)S(1)} collective-permute-done((bf16[528,256]{1,0:T(8,128)(2,1)S(1)}, bf16[528,256]{1,0:T(8,128)(2,1)S(1)}, u32[]{:S(2)}, u32[]{:S(2)}) %collective-permute-start.2) | collective-permute-done | bytes 270368 | tf_op jit(solution)/shard_map/ppermute | solution.py:634
  11.3 1.7 collective-permute-start.3
  15.4 3.6 %collective-permute-start = (bf16[128,1024]{1,0:T(8,128)(2,1)S(1)}, bf16[128,1024]{1,0:T(8,128)(2,1)S(1)}, u32[]{:S(2)}, u32[]{:S(2)}) collective-permute-start(bf16[128,1024]{1,0:T(8,128)(2,1)S(1)} %shard_map.169), channel_id=1, source_target_pairs={{0,4},{1,5},{2,6},{3,7},{8,12},{9,13},{10,14},{11,15},{16,20},{17,... | collective-permute-start | bytes 786440 | tf_op jit(solution)/shard_map/ppermute | solution.py:703
  19.0 1.6 collective-permute-start.4
  21.1 1.6 collective-permute-start.17
  22.7 3.0 %collective-permute-done.far_a = bf16[128,1024]{1,0:T(8,128)(2,1)S(1)} collective-permute-done((bf16[128,1024]{1,0:T(8,128)(2,1)S(1)}, bf16[128,1024]{1,0:T(8,128)(2,1)S(1)}, u32[]{:S(2)}, u32[]{:S(2)}) %collective-permute-start) | collective-permute-done | bytes 262176 | tf_op jit(solution)/shard_map/ppermute | solution.py:703
  25.7 3.6 %collective-permute-done.4.refs_3_ = bf16[528,256]{1,0:T(8,128)(2,1)S(1)} collective-permute-done((bf16[528,256]{1,0:T(8,128)(2,1)S(1)}, bf16[528,256]{1,0:T(8,128)(2,1)S(1)}, u32[]{:S(2)}, u32[]{:S(2)}) %collective-permute-start.4) | collective-permute-done | bytes 270368 | tf_op jit(solution)/shard_map/ppermute | solution.py:634
  29.9 2.5 %collective-permute-start.9 = (bf16[528,128]{1,0:T(8,128)(2,1)}, bf16[528,128]{1,0:T(8,128)(2,1)}, u32[]{:S(2)}, u32[]{:S(2)}) collective-permute-start(bf16[528,128]{1,0:T(8,128)(2,1)} %slice.33), channel_id=1, source_target_pairs={{0,4},{8,0},{16,8},{24,16},{28,24},{20,28},{12,20},{4,12},{1,5},{9... | collective-permute-start | bytes 405512 | tf_op jit(solution)/shard_map/ppermute | solution.py:634
  33.1 2.0 %collective-permute-start.14 = (bf16[128,1024]{1,0:T(8,128)(2,1)}, bf16[128,1024]{1,0:T(8,128)(2,1)}, u32[]{:S(2)}, u32[]{:S(2)}) collective-permute-start(bf16[128,1024]{1,0:T(8,128)(2,1)} %refs_0_), channel_id=1, source_target_pairs={{0,4},{8,0},{16,8},{24,16},{28,24},{20,28},{12,20},{4,12},{1,5},{9... | collective-permute-start | bytes 786440 | tf_op jit(solution)/shard_map/ppermute | solution.py:634
  35.3 1.8 collective-permute-start.25
  37.0 2.1 %collective-permute-start.22 = (bf16[128,1024]{1,0:T(8,128)(2,1)}, bf16[128,1024]{1,0:T(8,128)(2,1)S(1)}, u32[]{:S(2)}, u32[]{:S(2)}) collective-permute-start(bf16[128,1024]{1,0:T(8,128)(2,1)} %refs_0_.1), channel_id=1, source_target_pairs={{0,4},{8,0},{16,8},{24,16},{28,24},{20,28},{12,20},{4,12},{1,5},{9... | collective-permute-start | bytes 786440 | tf_op jit(solution)/shard_map/ppermute | solution.py:634
  39.8 2.5 %shard_map.171 = (bf16[256,1024]{1,0:T(8,128)(2,1)S(1)}, bf16[256,1024]{1,0:T(8,128)(2,1)S(1)}, bf16[256,256]{1,0:T(8,128)(2,1)S(1)}, bf16[256,512]{1,0:T(8,128)...) custom-call(s32[11]{0:T(128)S(1)} %pad_add_fusion.meta, ...), custom_call_target="tpu_custom_call" | custom-call | flops 700000000 | bytes 7570476 | tf_op jit(solution)/shard_map/pallas_call | solution.py:250
  42.3 4.1 %shard_map.172 = (bf16[256,256]{1,0:T(8,128)(2,1)S(1)}, f32[128,1024]{1,0:T(8,128)S(1)}, bf16[128,1024]{1,0:T(8,128)(2,1)S(1)}) custom-call(s32[11]{0:T(128)S(1)} %pad_add_fusion.meta, bf16[256,256]{1,0:T(8,128)(2,1)S(1)} %get-tuple-element.96.query, bf16[256,512]{1,0:T(8,128)(2,1)S(1)} %get-tuple-element.97.kv, ...), custom_call_target="tpu_custom_call" | custom-call | flops 300000000 | bytes 2100268 | tf_op jit(solution)/shard_map/pallas_call | solution.py:250
  46.6 2.1 %collective-permute-start.19 = (bf16[128,1024]{1,0:T(8,128)(2,1)S(1)}, bf16[128,1024]{1,0:T(8,128)(2,1)S(1)}, u32[]{:S(2)}, u32[]{:S(2)}) collective-permute-start(bf16[128,1024]{1,0:T(8,128)(2,1)S(1)} %collective-permute-done.18.refs_7_), channel_id=1, source_target_pairs={{0,8},{8,16},{16,24},{24,28},{28,20},{20,12},{12,4},{4,0},{1,9},{9... | collective-permute-start | bytes 786440 | tf_op jit(solution)/shard_map/ppermute | solution.py:630
  48.7 2.5 %collective-permute-start.26 = (bf16[128,1024]{1,0:T(8,128)(2,1)S(1)}, bf16[128,1024]{1,0:T(8,128)(2,1)S(1)}, u32[]{:S(2)}, u32[]{:S(2)}) collective-permute-start(bf16[128,1024]{1,0:T(8,128)(2,1)S(1)} %collective-permute-done.25.refs_8_), channel_id=1, source_target_pairs={{0,8},{8,16},{16,24},{24,28},{28,20},{20,12},{12,4},{4,0},{1,9},{9... | collective-permute-start | bytes 786440 | tf_op jit(solution)/shard_map/ppermute | solution.py:630
  52.8 3.2 %collective-permute-done.15.refs_2_ = bf16[128,1024]{1,0:T(8,128)(2,1)S(1)} collective-permute-done((bf16[128,1024]{1,0:T(8,128)(2,1)}, bf16[128,1024]{1,0:T(8,128)(2,1)S(1)}, u32[]{:S(2)}, u32[]{:S(2)}) %collective-permute-start.15) | collective-permute-done | bytes 262176 | tf_op jit(solution)/shard_map/ppermute | solution.py:634
  56.0 4.9 %collective-permute-done.26.refs_7_ = bf16[128,1024]{1,0:T(8,128)(2,1)S(1)} collective-permute-done((bf16[128,1024]{1,0:T(8,128)(2,1)S(1)}, bf16[128,1024]{1,0:T(8,128)(2,1)S(1)}, u32[]{:S(2)}, u32[]{:S(2)}) %collective-permute-start.26) | collective-permute-done | bytes 262176 | tf_op jit(solution)/shard_map/ppermute | solution.py:630
  60.9 2.0 %collective-permute-start.27 = (bf16[128,1024]{1,0:T(8,128)(2,1)S(1)}, bf16[128,1024]{1,0:T(8,128)(2,1)S(1)}, u32[]{:S(2)}, u32[]{:S(2)}) collective-permute-start(bf16[128,1024]{1,0:T(8,128)(2,1)S(1)} %collective-permute-done.26.refs_7_), channel_id=1, source_target_pairs={{0,8},{8,16},{16,24},{24,28},{28,20},{20,12},{12,4},{4,0},{1,9},{9... | collective-permute-start | bytes 786440 | tf_op jit(solution)/shard_map/ppermute | solution.py:630
  63.9 3.3 %collective-permute-done.16.refs_3_ = bf16[128,1024]{1,0:T(8,128)(2,1)S(1)} collective-permute-done((bf16[128,1024]{1,0:T(8,128)(2,1)S(1)}, bf16[128,1024]{1,0:T(8,128)(2,1)S(1)}, u32[]{:S(2)}, u32[]{:S(2)}) %collective-permute-start.16) | collective-permute-done | bytes 262176 | tf_op jit(solution)/shard_map/ppermute | solution.py:634
  67.2 2.5 %collective-permute-start.20 = (bf16[64,1024]{1,0:T(8,128)(2,1)S(1)}, bf16[64,1024]{1,0:T(8,128)(2,1)S(1)}, u32[]{:S(2)}, u32[]{:S(2)}) collective-permute-start(bf16[64,1024]{1,0:T(8,128)(2,1)S(1)} %slice.34), channel_id=1, source_target_pairs={{0,8},{8,16},{16,24},{24,28},{28,20},{20,12},{12,4},{4,0},{1,9},{9... | collective-permute-start | bytes 393224 | tf_op jit(solution)/shard_map/ppermute | solution.py:630
  69.7 3.6 %collective-permute-start.21 = (bf16[64,1024]{1,0:T(8,128)(2,1)S(1)}, bf16[64,1024]{1,0:T(8,128)(2,1)S(1)}, u32[]{:S(2)}, u32[]{:S(2)}) collective-permute-start(bf16[64,1024]{1,0:T(8,128)(2,1)S(1)} %slice.35), channel_id=1, source_target_pairs={{0,4},{8,0},{16,8},{24,16},{28,24},{20,28},{12,20},{4,12},{1,5},{9... | collective-permute-start | bytes 393224 | tf_op jit(solution)/shard_map/ppermute | solution.py:634
  73.4 1.9 %collective-permute-start.28 = (bf16[64,1024]{1,0:T(8,128)(2,1)S(1)}, bf16[64,1024]{1,0:T(8,128)(2,1)S(1)}, u32[]{:S(2)}, u32[]{:S(2)}) collective-permute-start(bf16[64,1024]{1,0:T(8,128)(2,1)S(1)} %slice.36), channel_id=1, source_target_pairs={{0,8},{8,16},{16,24},{24,28},{28,20},{20,12},{12,4},{4,0},{1,9},{9... | collective-permute-start | bytes 393224 | tf_op jit(solution)/shard_map/ppermute | solution.py:630
  76.6 4.3 %shard_map.173 = (f32[256,1024]{1,0:T(8,128)S(1)}, bf16[256,1024]{1,0:T(8,128)(2,1)S(1)}, bf16[256,1024]{1,0:T(8,128)(2,1)S(1)}, bf16[256,1024]{1,0:T(8,128)(2,1...) custom-call(s32[11]{0:T(128)S(1)} %pad_add_fusion.meta, ...), custom_call_target="tpu_custom_call" | custom-call | flops 1100000000 | bytes 13140012 | tf_op jit(solution)/shard_map/pallas_call | solution.py:250
  80.9 3.8 %shard_map.174 = (bf16[256,1024]{1,0:T(8,128)(2,1)S(1)}, f32[128,1024]{1,0:T(8,128)S(1)}, bf16[128,1024]{1,0:T(8,128)(2,1)S(1)}, f32[8,1024]{1,0:T(8,128)S(1)}, bf16[1024,1024]{1,0:T(8,128)(2,1)S(1)}) custom-call(s32[11]{0:T(128)S(1)} %pad_add_fusion.meta, f32[256,1024]{1,0:T(8,128)S(1)} %get-tuple-element.104.residual, ...), custom_call_target="tpu_custom_call" | custom-call | flops 1100000000 | bytes 10256428 | tf_op jit(solution)/shard_map/pallas_call | solution.py:250
  88.0 6.8 %collective-permute-done.31.s1 = bf16[128,1024]{1,0:T(8,128)(2,1)S(1)} collective-permute-done((bf16[128,1024]{1,0:T(8,128)(2,1)S(1)}, bf16[128,1024]{1,0:T(8,128)(2,1)S(1)}, u32[]{:S(2)}, u32[]{:S(2)}) %collective-permute-start.31) | collective-permute-done | bytes 262176 | tf_op jit(solution)/shard_map/ppermute | solution.py:663
  99.6 1.8 collective-permute-done.61.ahead
  102.8 1.8 collective-permute-start.63
  104.8 5.6 %shard_map.176 = (f32[256,1024]{1,0:T(8,128)S(1)}, bf16[256,1024]{1,0:T(8,128)(2,1)S(1)}, f32[256,256]{1,0:T(8,128)S(1)}, f32[256,512]{1,0:T(8,128)S(1)}, bf16[256,512]{1,0:T(8,128)(2,1)S(1)}) custom-call(s32[11]{0:T(128)S(1)} %pad_add_fusion.meta, f32[256,1024]{1,0:T(8,128)S(1)} %bitcast.18, f32[256,1024]{1,0:T(8,128)S(1)} %get-tuple-element.104.residual, ...), custom_call_target="tpu_custom_call" | custom-call | flops 500000000 | bytes 7113772 | tf_op jit(solution)/shard_map/pallas_call | solution.py:250
  110.4 2.9 %shard_map.178 = (f32[256,1024]{1,0:T(8,128)S(1)}, bf16[528,256]{1,0:T(8,128)(2,1)S(1)}, bf16[528,256]{1,0:T(8,128)(2,1)S(1)}, bf16[528,256]{1,0:T(8,128)(2,1)S(...) custom-call(s32[11]{0:T(128)S(1)} %pad_add_fusion.meta, ...), custom_call_target="tpu_custom_call" | custom-call | flops 1100000000 | bytes 9142316 | tf_op jit(solution)/shard_map/pallas_call | solution.py:250
  113.3 1.8 collective-permute-start.43
  116.7 3.8 %collective-permute-done.54.behind = bf16[64,1024]{1,0:T(8,128)(2,1)S(1)} collective-permute-done((bf16[64,1024]{1,0:T(8,128)(2,1)S(1)}, bf16[64,1024]{1,0:T(8,128)(2,1)S(1)}, u32[]{:S(2)}, u32[]{:S(2)}) %collective-permute-start.54) | collective-permute-done | bytes 131104 | tf_op jit(solution)/shard_map/ppermute | solution.py:634
  121.1 1.7 collective-permute-start.55
  123.8 1.7 collective-permute-start.65
  126.6 1.7 collective-permute-start.45
  128.2 2.0 %collective-permute-done.55.ahead = bf16[128,1024]{1,0:T(8,128)(2,1)S(1)} collective-permute-done((bf16[128,1024]{1,0:T(8,128)(2,1)S(1)}, bf16[128,1024]{1,0:T(8,128)(2,1)S(1)}, u32[]{:S(2)}, u32[]{:S(2)}) %collective-permute-start.55) | collective-permute-done | bytes 262176 | tf_op jit(solution)/shard_map/ppermute | solution.py:630
  137.3 2.6 %collective-permute-start.46 = (bf16[528,256]{1,0:T(8,128)(2,1)S(1)}, bf16[528,256]{1,0:T(8,128)(2,1)S(1)}, u32[]{:S(2)}, u32[]{:S(2)}) collective-permute-start(bf16[528,256]{1,0:T(8,128)(2,1)S(1)} %get-tuple-element.140), channel_id=1, source_target_pairs={{0,4},{8,0},{16,8},{24,16},{28,24},{20,28},{12,20},{4,12},{1,5},{9... | collective-permute-start | bytes 811016 | tf_op jit(solution)/shard_map/ppermute | solution.py:634
  139.9 2.0 %shard_map.175 = (f32[128,1024]{1,0:T(8,128)S(1)}, bf16[128,1024]{1,0:T(8,128)(2,1)S(1)}) custom-call(s32[11]{0:T(128)S(1)} %pad_add_fusion.meta, bf16[256,1024]{1,0:T(8,128)(2,1)S(1)} %get-tuple-element.105.act, bf16[1024,1024]{1,0:T(8,128)(2,1)S(1)} %get-tuple-element.110.reduce), custom_call_target="tpu_custom_call" | custom-call | flops 550000000 | bytes 3407916 | tf_op jit(solution)/shard_map/pallas_call | solution.py:250
  142.6 2.3 %collective-permute-done.46.behind = bf16[528,256]{1,0:T(8,128)(2,1)S(1)} collective-permute-done((bf16[528,256]{1,0:T(8,128)(2,1)S(1)}, bf16[528,256]{1,0:T(8,128)(2,1)S(1)}, u32[]{:S(2)}, u32[]{:S(2)}) %collective-permute-start.46) | collective-permute-done | bytes 270368 | tf_op jit(solution)/shard_map/ppermute | solution.py:634
  145.7 1.6 collective-permute-start.47
  147.2 4.8 %collective-permute-done.38.kv_grad_in = bf16[256,512]{1,0:T(8,128)(2,1)S(1)} collective-permute-done((bf16[256,512]{1,0:T(8,128)(2,1)S(1)}, bf16[256,512]{1,0:T(8,128)(2,1)S(1)}, u32[]{:S(2)}, u32[]{:S(2)}) %collective-permute-start.38) | collective-permute-done | bytes 262176 | tf_op jit(solution)/shard_map/ppermute | solution.py:762
  153.1 2.1 %collective-permute-start.67 = (bf16[128,1024]{1,0:T(8,128)(2,1)S(1)}, bf16[128,1024]{1,0:T(8,128)(2,1)S(1)}, u32[]{:S(2)}, u32[]{:S(2)}) collective-permute-start(bf16[128,1024]{1,0:T(8,128)(2,1)S(1)} %get-tuple-element.179), channel_id=1, source_target_pairs={{0,8},{8,16},{16,24},{24,28},{28,20},{20,12},{12,4},{4,0},{1,9},{9... | collective-permute-start | bytes 786440 | tf_op jit(solution)/shard_map/ppermute | solution.py:630
  156.0 1.8 collective-permute-done.47.ahead
  165.0 1.6 collective-permute-start.40
  166.6 5.5 %collective-permute-done.49.ahead = bf16[528,256]{1,0:T(8,128)(2,1)S(1)} collective-permute-done((bf16[528,256]{1,0:T(8,128)(2,1)S(1)}, bf16[528,256]{1,0:T(8,128)(2,1)S(1)}, u32[]{:S(2)}, u32[]{:S(2)}) %collective-permute-start.49) | collective-permute-done | bytes 270368 | tf_op jit(solution)/shard_map/ppermute | solution.py:630
  176.0 1.7 collective-permute-start.52
  180.6 1.8 shard_map.177
  182.9 2.3 %shard_map.180 = f32[256,1024]{1,0:T(8,128)} custom-call(s32[11]{0:T(128)S(1)} %pad_add_fusion.meta, f32[256,1024]{1,0:T(8,128)S(1)} %bitcast.16, f32[256,1024]{1,0:T(8,128)S(1)} %get-tuple-element.119.residual_grad, f32[8,1024]{1,0:T(8,128)S(1)} %get-tuple-element.95.small, bf16[128,1024]{1,0:T(8,128)(2,1)S(1)} %add_convert_fusion.s0, ...), custom_call_target="tpu_custom_call" | custom-call | flops 5000000 | bytes 4227116 | tf_op jit(solution)/shard_map/pallas_call | solution.py:250
  (143 shorter events, 49.0 us)
Async XLA Ops:
  1.7 9.6 %collective-permute-start.2 = (bf16[528,256]{1,0:T(8,128)(2,1)S(1)}, bf16[528,256]{1,0:T(8,128)(2,1)S(1)}, u32[]{:S(2)}, u32[]{:S(2)}) collective-permute-start(bf16[528,256]{1,0:T(8,128)(2,1)S(1)} %shard_map.170.refs_0_), channel_id=1, source_target_pairs={{0,4},{8,0},{16,8},{24,16},{28,24},{20,28},{12,20},{4,12},{1,5},{9... | collective-permute-start | bytes 811016 | tf_op jit(solution)/shard_map/ppermute | solution.py:634
  15.4 10.3 %collective-permute-start = (bf16[128,1024]{1,0:T(8,128)(2,1)S(1)}, bf16[128,1024]{1,0:T(8,128)(2,1)S(1)}, u32[]{:S(2)}, u32[]{:S(2)}) collective-permute-start(bf16[128,1024]{1,0:T(8,128)(2,1)S(1)} %shard_map.169), channel_id=1, source_target_pairs={{0,4},{1,5},{2,6},{3,7},{8,12},{9,13},{10,14},{11,15},{16,20},{17,... | collective-permute-start | bytes 786440 | tf_op jit(solution)/shard_map/ppermute | solution.py:703
  19.0 10.2 %collective-permute-start.4 = (bf16[528,256]{1,0:T(8,128)(2,1)S(1)}, bf16[528,256]{1,0:T(8,128)(2,1)S(1)}, u32[]{:S(2)}, u32[]{:S(2)}) collective-permute-start(bf16[528,256]{1,0:T(8,128)(2,1)S(1)} %collective-permute-done.3.refs_2_), channel_id=1, source_target_pairs={{0,4},{8,0},{16,8},{24,16},{28,24},{20,28},{12,20},{4,12},{1,5},{9... | collective-permute-start | bytes 811016 | tf_op jit(solution)/shard_map/ppermute | solution.py:634
  20.6 11.8 %collective-permute-start.7 = (bf16[528,256]{1,0:T(8,128)(2,1)S(1)}, bf16[528,256]{1,0:T(8,128)(2,1)S(1)}, u32[]{:S(2)}, u32[]{:S(2)}) collective-permute-start(bf16[528,256]{1,0:T(8,128)(2,1)S(1)} %collective-permute-done.6.refs_7_), channel_id=1, source_target_pairs={{0,8},{8,16},{16,24},{24,28},{28,20},{20,12},{12,4},{4,0},{1,9},{9... | collective-permute-start | bytes 811016 | tf_op jit(solution)/shard_map/ppermute | solution.py:630
  21.1 14.1 %collective-permute-start.17 = (bf16[128,1024]{1,0:T(8,128)(2,1)}, bf16[128,1024]{1,0:T(8,128)(2,1)}, u32[]{:S(2)}, u32[]{:S(2)}) collective-permute-start(bf16[128,1024]{1,0:T(8,128)(2,1)} %refs_0_), channel_id=1, source_target_pairs={{0,8},{8,16},{16,24},{24,28},{28,20},{20,12},{12,4},{4,0},{1,9},{9... | collective-permute-start | bytes 786440 | tf_op jit(solution)/shard_map/ppermute | solution.py:630
  25.7 9.6 %collective-permute-start.1 = (bf16[128,1024]{1,0:T(8,128)(2,1)S(1)}, bf16[128,1024]{1,0:T(8,128)(2,1)S(1)}, u32[]{:S(2)}, u32[]{:S(2)}) collective-permute-start(bf16[128,1024]{1,0:T(8,128)(2,1)S(1)} %collective-permute-done.far_a), channel_id=1, source_target_pairs={{0,1},{1,0},{2,3},{3,2},{4,5},{5,4},{6,7},{7,6},{8,9},{9,8},{10,11... | collective-permute-start | bytes 786440 | tf_op jit(solution)/shard_map/ppermute | solution.py:704
  33.1 13.5 %collective-permute-start.14 = (bf16[128,1024]{1,0:T(8,128)(2,1)}, bf16[128,1024]{1,0:T(8,128)(2,1)}, u32[]{:S(2)}, u32[]{:S(2)}) collective-permute-start(bf16[128,1024]{1,0:T(8,128)(2,1)} %refs_0_), channel_id=1, source_target_pairs={{0,4},{8,0},{16,8},{24,16},{28,24},{20,28},{12,20},{4,12},{1,5},{9... | collective-permute-start | bytes 786440 | tf_op jit(solution)/shard_map/ppermute | solution.py:634
  35.2 11.4 %collective-permute-start.18 = (bf16[128,1024]{1,0:T(8,128)(2,1)}, bf16[128,1024]{1,0:T(8,128)(2,1)S(1)}, u32[]{:S(2)}, u32[]{:S(2)}) collective-permute-start(bf16[128,1024]{1,0:T(8,128)(2,1)} %collective-permute-done.17.refs_8_), channel_id=1, source_target_pairs={{0,8},{8,16},{16,24},{24,28},{28,20},{20,12},{12,4},{4,0},{1,9},{9... | collective-permute-start | bytes 786440 | tf_op jit(solution)/shard_map/ppermute | solution.py:630
  35.3 13.4 %collective-permute-start.25 = (bf16[128,1024]{1,0:T(8,128)(2,1)}, bf16[128,1024]{1,0:T(8,128)(2,1)S(1)}, u32[]{:S(2)}, u32[]{:S(2)}) collective-permute-start(bf16[128,1024]{1,0:T(8,128)(2,1)} %refs_0_.1), channel_id=1, source_target_pairs={{0,8},{8,16},{16,24},{24,28},{28,20},{20,12},{12,4},{4,0},{1,9},{9... | collective-permute-start | bytes 786440 | tf_op jit(solution)/shard_map/ppermute | solution.py:630
  37.0 14.1 %collective-permute-start.22 = (bf16[128,1024]{1,0:T(8,128)(2,1)}, bf16[128,1024]{1,0:T(8,128)(2,1)S(1)}, u32[]{:S(2)}, u32[]{:S(2)}) collective-permute-start(bf16[128,1024]{1,0:T(8,128)(2,1)} %refs_0_.1), channel_id=1, source_target_pairs={{0,4},{8,0},{16,8},{24,16},{28,24},{20,28},{12,20},{4,12},{1,5},{9... | collective-permute-start | bytes 786440 | tf_op jit(solution)/shard_map/ppermute | solution.py:634
  46.5 9.4 %collective-permute-start.15 = (bf16[128,1024]{1,0:T(8,128)(2,1)}, bf16[128,1024]{1,0:T(8,128)(2,1)S(1)}, u32[]{:S(2)}, u32[]{:S(2)}) collective-permute-start(bf16[128,1024]{1,0:T(8,128)(2,1)} %collective-permute-done.14.refs_1_), channel_id=1, source_target_pairs={{0,4},{8,0},{16,8},{24,16},{28,24},{20,28},{12,20},{4,12},{1,5},{9... | collective-permute-start | bytes 786440 | tf_op jit(solution)/shard_map/ppermute | solution.py:634
  46.6 16.8 %collective-permute-start.19 = (bf16[128,1024]{1,0:T(8,128)(2,1)S(1)}, bf16[128,1024]{1,0:T(8,128)(2,1)S(1)}, u32[]{:S(2)}, u32[]{:S(2)}) collective-permute-start(bf16[128,1024]{1,0:T(8,128)(2,1)S(1)} %collective-permute-done.18.refs_7_), channel_id=1, source_target_pairs={{0,8},{8,16},{16,24},{24,28},{28,20},{20,12},{12,4},{4,0},{1,9},{9... | collective-permute-start | bytes 786440 | tf_op jit(solution)/shard_map/ppermute | solution.py:630
  48.7 12.2 %collective-permute-start.26 = (bf16[128,1024]{1,0:T(8,128)(2,1)S(1)}, bf16[128,1024]{1,0:T(8,128)(2,1)S(1)}, u32[]{:S(2)}, u32[]{:S(2)}) collective-permute-start(bf16[128,1024]{1,0:T(8,128)(2,1)S(1)} %collective-permute-done.25.refs_8_), channel_id=1, source_target_pairs={{0,8},{8,16},{16,24},{24,28},{28,20},{20,12},{12,4},{4,0},{1,9},{9... | collective-permute-start | bytes 786440 | tf_op jit(solution)/shard_map/ppermute | solution.py:630
  51.2 11.8 %collective-permute-start.23 = (bf16[128,1024]{1,0:T(8,128)(2,1)S(1)}, bf16[128,1024]{1,0:T(8,128)(2,1)S(1)}, u32[]{:S(2)}, u32[]{:S(2)}) collective-permute-start(bf16[128,1024]{1,0:T(8,128)(2,1)S(1)} %collective-permute-done.22.refs_1_), channel_id=1, source_target_pairs={{0,4},{8,0},{16,8},{24,16},{28,24},{20,28},{12,20},{4,12},{1,5},{9... | collective-permute-start | bytes 786440 | tf_op jit(solution)/shard_map/ppermute | solution.py:634
  51.2 12.2 %collective-permute-start.11 = (bf16[128,1024]{1,0:T(8,128)(2,1)S(1)}, bf16[128,1024]{1,0:T(8,128)(2,1)S(1)}, u32[]{:S(2)}, u32[]{:S(2)}) collective-permute-start(bf16[128,1024]{1,0:T(8,128)(2,1)S(1)} %add_convert_fusion.3.s0), channel_id=1, source_target_pairs={{0,2},{2,0},{1,3},{3,1},{4,6},{6,4},{5,7},{7,5},{8,10},{10,8},{9,1... | collective-permute-start | bytes 786440 | tf_op jit(solution)/shard_map/ppermute | solution.py:663
  56.0 11.2 %collective-permute-start.16 = (bf16[128,1024]{1,0:T(8,128)(2,1)S(1)}, bf16[128,1024]{1,0:T(8,128)(2,1)S(1)}, u32[]{:S(2)}, u32[]{:S(2)}) collective-permute-start(bf16[128,1024]{1,0:T(8,128)(2,1)S(1)} %collective-permute-done.15.refs_2_), channel_id=1, source_target_pairs={{0,4},{8,0},{16,8},{24,16},{28,24},{20,28},{12,20},{4,12},{1,5},{9... | collective-permute-start | bytes 786440 | tf_op jit(solution)/shard_map/ppermute | solution.py:634
  60.9 8.8 %collective-permute-start.27 = (bf16[128,1024]{1,0:T(8,128)(2,1)S(1)}, bf16[128,1024]{1,0:T(8,128)(2,1)S(1)}, u32[]{:S(2)}, u32[]{:S(2)}) collective-permute-start(bf16[128,1024]{1,0:T(8,128)(2,1)S(1)} %collective-permute-done.26.refs_7_), channel_id=1, source_target_pairs={{0,8},{8,16},{16,24},{24,28},{28,20},{20,12},{12,4},{4,0},{1,9},{9... | collective-permute-start | bytes 786440 | tf_op jit(solution)/shard_map/ppermute | solution.py:630
  62.9 10.4 %collective-permute-start.24 = (bf16[128,1024]{1,0:T(8,128)(2,1)S(1)}, bf16[128,1024]{1,0:T(8,128)(2,1)S(1)}, u32[]{:S(2)}, u32[]{:S(2)}) collective-permute-start(bf16[128,1024]{1,0:T(8,128)(2,1)S(1)} %collective-permute-done.23.refs_2_), channel_id=1, source_target_pairs={{0,4},{8,0},{16,8},{24,16},{28,24},{20,28},{12,20},{4,12},{1,5},{9... | collective-permute-start | bytes 786440 | tf_op jit(solution)/shard_map/ppermute | solution.py:634
  63.4 13.2 %collective-permute-start.12 = (bf16[128,1024]{1,0:T(8,128)(2,1)S(1)}, bf16[128,1024]{1,0:T(8,128)(2,1)S(1)}, u32[]{:S(2)}, u32[]{:S(2)}) collective-permute-start(bf16[128,1024]{1,0:T(8,128)(2,1)S(1)} %add_convert_fusion.3.s0), channel_id=1, source_target_pairs={{0,1},{1,0},{2,3},{3,2},{4,5},{5,4},{6,7},{7,6},{8,9},{9,8},{10,11... | collective-permute-start | bytes 786440 | tf_op jit(solution)/shard_map/ppermute | solution.py:663
  63.4 13.2 %collective-permute-start.13 = (bf16[128,1024]{1,0:T(8,128)(2,1)S(1)}, bf16[128,1024]{1,0:T(8,128)(2,1)S(1)}, u32[]{:S(2)}, u32[]{:S(2)}) collective-permute-start(bf16[128,1024]{1,0:T(8,128)(2,1)S(1)} %collective-permute-done.11.s1), channel_id=1, source_target_pairs={{0,1},{1,0},{2,3},{3,2},{4,5},{5,4},{6,7},{7,6},{8,9},{9,8},{10,11... | collective-permute-start | bytes 786440 | tf_op jit(solution)/shard_map/ppermute | solution.py:663
  86.4 8.4 %collective-permute-start.31 = (bf16[128,1024]{1,0:T(8,128)(2,1)S(1)}, bf16[128,1024]{1,0:T(8,128)(2,1)S(1)}, u32[]{:S(2)}, u32[]{:S(2)}) collective-permute-start(bf16[128,1024]{1,0:T(8,128)(2,1)S(1)} %add_convert_fusion.2.s0), channel_id=1, source_target_pairs={{0,2},{2,0},{1,3},{3,1},{4,6},{6,4},{5,7},{7,5},{8,10},{10,8},{9,1... | collective-permute-start | bytes 786440 | tf_op jit(solution)/shard_map/ppermute | solution.py:663
  88.0 16.8 %collective-permute-start.32 = (bf16[128,1024]{1,0:T(8,128)(2,1)S(1)}, bf16[128,1024]{1,0:T(8,128)(2,1)S(1)}, u32[]{:S(2)}, u32[]{:S(2)}) collective-permute-start(bf16[128,1024]{1,0:T(8,128)(2,1)S(1)} %add_convert_fusion.2.s0), channel_id=1, source_target_pairs={{0,1},{1,0},{2,3},{3,2},{4,5},{5,4},{6,7},{7,6},{8,9},{9,8},{10,11... | collective-permute-start | bytes 786440 | tf_op jit(solution)/shard_map/ppermute | solution.py:663
  94.8 10.0 %collective-permute-start.33 = (bf16[128,1024]{1,0:T(8,128)(2,1)S(1)}, bf16[128,1024]{1,0:T(8,128)(2,1)S(1)}, u32[]{:S(2)}, u32[]{:S(2)}) collective-permute-start(bf16[128,1024]{1,0:T(8,128)(2,1)S(1)} %collective-permute-done.31.s1), channel_id=1, source_target_pairs={{0,1},{1,0},{2,3},{3,2},{4,5},{5,4},{6,7},{7,6},{8,9},{9,8},{10,11... | collective-permute-start | bytes 786440 | tf_op jit(solution)/shard_map/ppermute | solution.py:663
  98.6 16.7 %collective-permute-start.53 = (bf16[64,1024]{1,0:T(8,128)(2,1)S(1)}, bf16[64,1024]{1,0:T(8,128)(2,1)S(1)}, u32[]{:S(2)}, u32[]{:S(2)}) collective-permute-start(bf16[64,1024]{1,0:T(8,128)(2,1)S(1)} %get-tuple-element.157), channel_id=1, source_target_pairs={{0,8},{8,16},{16,24},{24,28},{28,20},{20,12},{12,4},{4,0},{1,9},{9... | collective-permute-start | bytes 393224 | tf_op jit(solution)/shard_map/ppermute | solution.py:630
  102.8 20.0 %collective-permute-start.63 = (bf16[128,1024]{1,0:T(8,128)(2,1)S(1)}, bf16[128,1024]{1,0:T(8,128)(2,1)S(1)}, u32[]{:S(2)}, u32[]{:S(2)}) collective-permute-start(bf16[128,1024]{1,0:T(8,128)(2,1)S(1)} %get-tuple-element.175), channel_id=1, source_target_pairs={{0,8},{8,16},{16,24},{24,28},{28,20},{20,12},{12,4},{4,0},{1,9},{9... | collective-permute-start | bytes 786440 | tf_op jit(solution)/shard_map/ppermute | solution.py:630
  104.5 18.6 %collective-permute-start.64 = (bf16[128,1024]{1,0:T(8,128)(2,1)S(1)}, bf16[128,1024]{1,0:T(8,128)(2,1)S(1)}, u32[]{:S(2)}, u32[]{:S(2)}) collective-permute-start(bf16[128,1024]{1,0:T(8,128)(2,1)S(1)} %get-tuple-element.176), channel_id=1, source_target_pairs={{0,4},{8,0},{16,8},{24,16},{28,24},{20,28},{12,20},{4,12},{1,5},{9... | collective-permute-start | bytes 786440 | tf_op jit(solution)/shard_map/ppermute | solution.py:634
  113.3 12.2 %collective-permute-start.43 = (bf16[528,128]{1,0:T(8,128)(2,1)S(1)}, bf16[528,128]{1,0:T(8,128)(2,1)S(1)}, u32[]{:S(2)}, u32[]{:S(2)}) collective-permute-start(bf16[528,128]{1,0:T(8,128)(2,1)S(1)} %get-tuple-element.137), channel_id=1, source_target_pairs={{0,8},{8,16},{16,24},{24,28},{28,20},{20,12},{12,4},{4,0},{1,9},{9... | collective-permute-start | bytes 405512 | tf_op jit(solution)/shard_map/ppermute | solution.py:630
  115.4 10.5 %collective-permute-start.44 = (bf16[528,128]{1,0:T(8,128)(2,1)S(1)}, bf16[528,128]{1,0:T(8,128)(2,1)S(1)}, u32[]{:S(2)}, u32[]{:S(2)}) collective-permute-start(bf16[528,128]{1,0:T(8,128)(2,1)S(1)} %get-tuple-element.138), channel_id=1, source_target_pairs={{0,4},{8,0},{16,8},{24,16},{28,24},{20,28},{12,20},{4,12},{1,5},{9... | collective-permute-start | bytes 405512 | tf_op jit(solution)/shard_map/ppermute | solution.py:634
  121.1 9.2 %collective-permute-start.55 = (bf16[128,1024]{1,0:T(8,128)(2,1)S(1)}, bf16[128,1024]{1,0:T(8,128)(2,1)S(1)}, u32[]{:S(2)}, u32[]{:S(2)}) collective-permute-start(bf16[128,1024]{1,0:T(8,128)(2,1)S(1)} %get-tuple-element.159), channel_id=1, source_target_pairs={{0,8},{8,16},{16,24},{24,28},{28,20},{20,12},{12,4},{4,0},{1,9},{9... | collective-permute-start | bytes 786440 | tf_op jit(solution)/shard_map/ppermute | solution.py:630
  122.8 8.9 %collective-permute-start.56 = (bf16[128,1024]{1,0:T(8,128)(2,1)S(1)}, bf16[128,1024]{1,0:T(8,128)(2,1)S(1)}, u32[]{:S(2)}, u32[]{:S(2)}) collective-permute-start(bf16[128,1024]{1,0:T(8,128)(2,1)S(1)} %get-tuple-element.160), channel_id=1, source_target_pairs={{0,4},{8,0},{16,8},{24,16},{28,24},{20,28},{12,20},{4,12},{1,5},{9... | collective-permute-start | bytes 786440 | tf_op jit(solution)/shard_map/ppermute | solution.py:634
  123.8 12.1 %collective-permute-start.65 = (bf16[128,1024]{1,0:T(8,128)(2,1)S(1)}, bf16[128,1024]{1,0:T(8,128)(2,1)S(1)}, u32[]{:S(2)}, u32[]{:S(2)}) collective-permute-start(bf16[128,1024]{1,0:T(8,128)(2,1)S(1)} %get-tuple-element.177), channel_id=1, source_target_pairs={{0,8},{8,16},{16,24},{24,28},{28,20},{20,12},{12,4},{4,0},{1,9},{9... | collective-permute-start | bytes 786440 | tf_op jit(solution)/shard_map/ppermute | solution.py:630
  125.5 11.8 %collective-permute-start.66 = (bf16[128,1024]{1,0:T(8,128)(2,1)S(1)}, bf16[128,1024]{1,0:T(8,128)(2,1)S(1)}, u32[]{:S(2)}, u32[]{:S(2)}) collective-permute-start(bf16[128,1024]{1,0:T(8,128)(2,1)S(1)} %get-tuple-element.178), channel_id=1, source_target_pairs={{0,4},{8,0},{16,8},{24,16},{28,24},{20,28},{12,20},{4,12},{1,5},{9... | collective-permute-start | bytes 786440 | tf_op jit(solution)/shard_map/ppermute | solution.py:634
  126.6 15.3 %collective-permute-start.45 = (bf16[528,256]{1,0:T(8,128)(2,1)S(1)}, bf16[528,256]{1,0:T(8,128)(2,1)S(1)}, u32[]{:S(2)}, u32[]{:S(2)}) collective-permute-start(bf16[528,256]{1,0:T(8,128)(2,1)S(1)} %get-tuple-element.139), channel_id=1, source_target_pairs={{0,8},{8,16},{16,24},{24,28},{28,20},{20,12},{12,4},{4,0},{1,9},{9... | collective-permute-start | bytes 811016 | tf_op jit(solution)/shard_map/ppermute | solution.py:630
  132.4 20.7 %collective-permute-start.57 = (bf16[128,1024]{1,0:T(8,128)(2,1)S(1)}, bf16[128,1024]{1,0:T(8,128)(2,1)S(1)}, u32[]{:S(2)}, u32[]{:S(2)}) collective-permute-start(bf16[128,1024]{1,0:T(8,128)(2,1)S(1)} %get-tuple-element.161), channel_id=1, source_target_pairs={{0,8},{8,16},{16,24},{24,28},{28,20},{20,12},{12,4},{4,0},{1,9},{9... | collective-permute-start | bytes 786440 | tf_op jit(solution)/shard_map/ppermute | solution.py:630
  133.8 21.4 %collective-permute-start.58 = (bf16[128,1024]{1,0:T(8,128)(2,1)S(1)}, bf16[128,1024]{1,0:T(8,128)(2,1)S(1)}, u32[]{:S(2)}, u32[]{:S(2)}) collective-permute-start(bf16[128,1024]{1,0:T(8,128)(2,1)S(1)} %get-tuple-element.162), channel_id=1, source_target_pairs={{0,4},{8,0},{16,8},{24,16},{28,24},{20,28},{12,20},{4,12},{1,5},{9... | collective-permute-start | bytes 786440 | tf_op jit(solution)/shard_map/ppermute | solution.py:634
  135.9 16.1 %collective-permute-start.38 = (bf16[256,512]{1,0:T(8,128)(2,1)S(1)}, bf16[256,512]{1,0:T(8,128)(2,1)S(1)}, u32[]{:S(2)}, u32[]{:S(2)}) collective-permute-start(bf16[256,512]{1,0:T(8,128)(2,1)S(1)} %get-tuple-element.123.kv_grad_far), channel_id=1, source_target_pairs={{4,0},{5,1},{6,2},{7,3},{12,8},{13,9},{14,10},{15,11},{20,16},{21,... | collective-permute-start | bytes 786440 | tf_op jit(solution)/shard_map/ppermute | solution.py:762
  141.9 14.0 %collective-permute-start.34 = (bf16[128,1024]{1,0:T(8,128)(2,1)S(1)}, bf16[128,1024]{1,0:T(8,128)(2,1)S(1)}, u32[]{:S(2)}, u32[]{:S(2)}) collective-permute-start(bf16[128,1024]{1,0:T(8,128)(2,1)S(1)} %get-tuple-element.118), channel_id=1, source_target_pairs={{0,1},{1,0},{2,3},{3,2},{4,5},{5,4},{6,7},{7,6},{8,9},{9,8},{10,11... | collective-permute-start | bytes 786440 | tf_op jit(solution)/shard_map/ppermute | solution.py:663
  145.7 12.1 %collective-permute-start.47 = (bf16[528,256]{1,0:T(8,128)(2,1)S(1)}, bf16[528,256]{1,0:T(8,128)(2,1)S(1)}, u32[]{:S(2)}, u32[]{:S(2)}) collective-permute-start(bf16[528,256]{1,0:T(8,128)(2,1)S(1)} %get-tuple-element.141), channel_id=1, source_target_pairs={{0,8},{8,16},{16,24},{24,28},{28,20},{20,12},{12,4},{4,0},{1,9},{9... | collective-permute-start | bytes 811016 | tf_op jit(solution)/shard_map/ppermute | solution.py:630
  153.1 9.1 %collective-permute-start.67 = (bf16[128,1024]{1,0:T(8,128)(2,1)S(1)}, bf16[128,1024]{1,0:T(8,128)(2,1)S(1)}, u32[]{:S(2)}, u32[]{:S(2)}) collective-permute-start(bf16[128,1024]{1,0:T(8,128)(2,1)S(1)} %get-tuple-element.179), channel_id=1, source_target_pairs={{0,8},{8,16},{16,24},{24,28},{28,20},{20,12},{12,4},{4,0},{1,9},{9... | collective-permute-start | bytes 786440 | tf_op jit(solution)/shard_map/ppermute | solution.py:630
  155.9 9.1 %collective-permute-start.68 = (bf16[128,1024]{1,0:T(8,128)(2,1)S(1)}, bf16[128,1024]{1,0:T(8,128)(2,1)S(1)}, u32[]{:S(2)}, u32[]{:S(2)}) collective-permute-start(bf16[128,1024]{1,0:T(8,128)(2,1)S(1)} %get-tuple-element.180), channel_id=1, source_target_pairs={{0,4},{8,0},{16,8},{24,16},{28,24},{20,28},{12,20},{4,12},{1,5},{9... | collective-permute-start | bytes 786440 | tf_op jit(solution)/shard_map/ppermute | solution.py:634
  157.8 16.2 %collective-permute-start.59 = (bf16[128,1024]{1,0:T(8,128)(2,1)S(1)}, bf16[128,1024]{1,0:T(8,128)(2,1)S(1)}, u32[]{:S(2)}, u32[]{:S(2)}) collective-permute-start(bf16[128,1024]{1,0:T(8,128)(2,1)S(1)} %get-tuple-element.163), channel_id=1, source_target_pairs={{0,8},{8,16},{16,24},{24,28},{28,20},{20,12},{12,4},{4,0},{1,9},{9... | collective-permute-start | bytes 786440 | tf_op jit(solution)/shard_map/ppermute | solution.py:630
  162.1 9.9 %collective-permute-start.49 = (bf16[528,256]{1,0:T(8,128)(2,1)S(1)}, bf16[528,256]{1,0:T(8,128)(2,1)S(1)}, u32[]{:S(2)}, u32[]{:S(2)}) collective-permute-start(bf16[528,256]{1,0:T(8,128)(2,1)S(1)} %get-tuple-element.143), channel_id=1, source_target_pairs={{0,8},{8,16},{16,24},{24,28},{28,20},{20,12},{12,4},{4,0},{1,9},{9... | collective-permute-start | bytes 811016 | tf_op jit(solution)/shard_map/ppermute | solution.py:630
  163.4 8.8 %collective-permute-start.50 = (bf16[528,256]{1,0:T(8,128)(2,1)S(1)}, bf16[528,256]{1,0:T(8,128)(2,1)S(1)}, u32[]{:S(2)}, u32[]{:S(2)}) collective-permute-start(bf16[528,256]{1,0:T(8,128)(2,1)S(1)} %get-tuple-element.144), channel_id=1, source_target_pairs={{0,4},{8,0},{16,8},{24,16},{28,24},{20,28},{12,20},{4,12},{1,5},{9... | collective-permute-start | bytes 811016 | tf_op jit(solution)/shard_map/ppermute | solution.py:634
  165.0 9.1 %collective-permute-start.40 = (bf16[128,1024]{1,0:T(8,128)(2,1)S(1)}, bf16[128,1024]{1,0:T(8,128)(2,1)S(1)}, u32[]{:S(2)}, u32[]{:S(2)}) collective-permute-start(bf16[128,1024]{1,0:T(8,128)(2,1)S(1)} %add_convert_fusion.s0), channel_id=1, source_target_pairs={{0,2},{2,0},{1,3},{3,1},{4,6},{6,4},{5,7},{7,5},{8,10},{10,8},{9,1... | collective-permute-start | bytes 786440 | tf_op jit(solution)/shard_map/ppermute | solution.py:663
  166.6 9.5 %collective-permute-start.60 = (bf16[128,1024]{1,0:T(8,128)(2,1)S(1)}, bf16[128,1024]{1,0:T(8,128)(2,1)S(1)}, u32[]{:S(2)}, u32[]{:S(2)}) collective-permute-start(bf16[128,1024]{1,0:T(8,128)(2,1)S(1)} %get-tuple-element.164), channel_id=1, source_target_pairs={{0,4},{8,0},{16,8},{24,16},{28,24},{20,28},{12,20},{4,12},{1,5},{9... | collective-permute-start | bytes 786440 | tf_op jit(solution)/shard_map/ppermute | solution.py:634
  172.1 8.5 %collective-permute-start.36 = (bf16[128,1024]{1,0:T(8,128)(2,1)S(1)}, bf16[128,1024]{1,0:T(8,128)(2,1)S(1)}, u32[]{:S(2)}, u32[]{:S(2)}) collective-permute-start(bf16[128,1024]{1,0:T(8,128)(2,1)S(1)} %add_convert_fusion.1.s0), channel_id=1, source_target_pairs={{0,1},{1,0},{2,3},{3,2},{4,5},{5,4},{6,7},{7,6},{8,9},{9,8},{10,11... | collective-permute-start | bytes 786440 | tf_op jit(solution)/shard_map/ppermute | solution.py:663
  172.2 8.4 %collective-permute-start.37 = (bf16[128,1024]{1,0:T(8,128)(2,1)S(1)}, bf16[128,1024]{1,0:T(8,128)(2,1)S(1)}, u32[]{:S(2)}, u32[]{:S(2)}) collective-permute-start(bf16[128,1024]{1,0:T(8,128)(2,1)S(1)} %collective-permute-done.35.s1), channel_id=1, source_target_pairs={{0,1},{1,0},{2,3},{3,2},{4,5},{5,4},{6,7},{7,6},{8,9},{9,8},{10,11... | collective-permute-start | bytes 786440 | tf_op jit(solution)/shard_map/ppermute | solution.py:663
  174.1 8.8 %collective-permute-start.41 = (bf16[128,1024]{1,0:T(8,128)(2,1)S(1)}, bf16[128,1024]{1,0:T(8,128)(2,1)S(1)}, u32[]{:S(2)}, u32[]{:S(2)}) collective-permute-start(bf16[128,1024]{1,0:T(8,128)(2,1)S(1)} %add_convert_fusion.s0), channel_id=1, source_target_pairs={{0,1},{1,0},{2,3},{3,2},{4,5},{5,4},{6,7},{7,6},{8,9},{9,8},{10,11... | collective-permute-start | bytes 786440 | tf_op jit(solution)/shard_map/ppermute | solution.py:663
  (27 other events, 269.5 us)
